TPU v7x, 32 devices: a whole 2x2x4 slice. The times are simulated.
32 devices in a mesh: ctx: 8 (over y, x, core), mp: 4 (over z).
Axes of the slice: x: 2, y: 2, z: 4, core: 2. Of those that a mesh axis runs over, the one named last changes fastest.
Arguments:
- queries: bfloat16 [128, 6144], P('ctx', 'mp'), may hold values from -9 to 9
- cache_keys: bfloat16 [8, 4096, 128], P('mp', 'ctx'), may hold values from -9 to 9, as said below
- cache_values: bfloat16 [8, 4096, 128], P('mp', 'ctx'), may hold values from -6 to 6, as said below
- new_keys: bfloat16 [8, 128, 128], P('mp', 'ctx'), may hold values from -6 to 6, as said below
- new_values: bfloat16 [8, 128, 128], P('mp', 'ctx'), may hold values from -6 to 6, as said below
- out_proj: bfloat16 [6144, 6144], P('mp', 'ctx'), may hold values from -3 to 3
- residual: bfloat16 [128, 6144], P('mp', 'ctx'), may hold values from -24 to 24
- norm_gain: bfloat16 [6144], replicated, may hold values from 0.5 to 1.5
- gate_proj: bfloat16 [8, 6144, 8192], P('ctx', None, 'mp'), may hold values from -0.078125 to 0.078125
- up_proj: bfloat16 [8, 6144, 8192], P('ctx', None, 'mp'), may hold values from -0.078125 to 0.078125
- down_proj: bfloat16 [8, 8192, 6144], P('ctx', 'mp'), may hold values from -0.09375 to 0.09375
- expert_ids: int32 [128, 2], replicated, may hold values from 0 to 7, all different within a row; in each aligned block of 128 rows (0 to 127, 128 to 255, ...) at most 64 rows name the same one
- route_logits: float32 [128, 2], replicated, may hold values from -6 to 6
Outputs:
- layer_out: bfloat16 [128, 6144], P('mp', 'ctx')
Inputs may be any that keep to these rules, and one draw needn't show every extreme that they name: `expert_ids`: each row names 2 different experts; at most 64 rows name one expert, a bound that some block reaches. `cache_keys`: slot s holds key head s * 1; slots of one key head are equal. `cache_values`: slot s holds value head s * 1; slots of one head are equal. `new_keys`: slot s holds key head s * 1; slots of one key head are equal. `new_values`: slot s holds value head s * 1; slots of one head are equal.
All inputs are finite; a program needn't handle non-finite values.
Results may differ from a plain program's by a relative error of at most 0.024.
Values may be sent and summed in bfloat16 or wider, within the bound.
No kernel may reach another device: no remote copies, remote signals or barrier semaphores. Data moves between devices by JAX's collectives and lax.ppermute only.
A program may use at most 128 MiB of HBM per device.

v0:
```python
import math

import jax
import jax.numpy as jnp
from jax import lax
from jax.sharding import PartitionSpec as P

D = 6144
EXPERTS = 8
TOP = 2


neg_big = -1e30
norm_eps = 1e-05


def route_slots(expert_ids):
    flat = expert_ids.reshape(-1)
    onehot = (flat[:, None] == jnp.arange(EXPERTS, dtype=jnp.int32)[None, :]).astype(jnp.int32)
    before = jnp.cumsum(onehot, axis=0, dtype=jnp.int32) - onehot
    return jnp.sum(before * onehot, axis=1, dtype=jnp.int32).reshape(expert_ids.shape)


def softmax_pieces(query_block, keys_local, values_local, allowed, scale):
    scores = (
        jnp.einsum("srd,skd->srk", query_block, keys_local, preferred_element_type=jnp.float32)
        * scale
    )
    scores = jnp.where(allowed[None, :, :], scores, neg_big)
    highest = jnp.max(scores, axis=2)
    expo = jnp.exp(scores - highest[:, :, None])
    denom = jnp.sum(expo, axis=2)
    summed = jnp.einsum(
        "srk,skd->srd", expo.astype(jnp.bfloat16), values_local, preferred_element_type=jnp.float32
    )
    return (highest, denom, summed)


def join_softmax(former, latter):
    highest = jnp.maximum(former[0], latter[0])
    right = jnp.exp(latter[0] - highest)
    denom = latter[1] * right
    summed = latter[2] * right[:, :, None]
    return (highest, denom, summed)


def on_device(
    queries,
    cache_keys,
    cache_values,
    new_keys,
    new_values,
    out_proj,
    residual,
    norm_gain,
    gate_proj,
    up_proj,
    down_proj,
    expert_ids,
    route_logits,
):
    ctx_count = lax.axis_size("ctx")
    mp_count = lax.axis_size("mp")
    ctx_index = lax.axis_index("ctx")
    mp_index = lax.axis_index("mp")
    tok_local = queries.shape[0]
    tokens = tok_local * ctx_count
    slot_local = cache_keys.shape[0]
    cache_local = cache_keys.shape[1]
    head_dim = cache_keys.shape[2]
    heads_local = queries.shape[1] // head_dim
    group_size = heads_local // slot_local
    width = cache_local + tok_local
    scale = 1.0 / math.sqrt(head_dim)
    d_local = out_proj.shape[1]
    key_value = jnp.stack(
        [
            jnp.concatenate([cache_keys, new_keys], axis=1),
            jnp.concatenate([cache_values, new_values], axis=1),
        ]
    )
    shaped = queries.reshape(tok_local, slot_local, group_size, head_dim)
    query_block = jnp.transpose(shaped, (1, 2, 0, 3)).reshape(
        slot_local, group_size * tok_local, head_dim
    )
    query_tok = ctx_index * tok_local + jnp.tile(jnp.arange(tok_local, dtype=jnp.int32), group_size)
    query_count = group_size * tok_local
    start_state = (
        jnp.full((slot_local, query_count), neg_big, jnp.float32),
        jnp.zeros((slot_local, query_count), jnp.float32),
        jnp.zeros((slot_local, query_count, head_dim), jnp.float32),
    )
    piece = lax.all_gather(key_value, "ctx", axis=2, tiled=True)
    position = jnp.arange(piece.shape[2], dtype=jnp.int32)
    shard = position // width
    within = position % width
    new_tok = shard * tok_local + within - cache_local
    allowed = (within[None, :] < cache_local) | (new_tok[None, :] <= query_tok[:, None])
    highest, denom, summed = join_softmax(
        start_state, softmax_pieces(query_block, piece[0], piece[1], allowed, scale)
    )
    shaped = (
        (summed / denom[:, :, None])
        .astype(jnp.bfloat16)
        .reshape(slot_local, group_size, tok_local, head_dim)
    )
    attn = jnp.transpose(shaped, (2, 0, 1, 3)).reshape(tok_local, heads_local * head_dim)
    projected = jnp.dot(
        lax.all_gather(attn, "ctx", axis=0, tiled=True),
        out_proj,
        preferred_element_type=jnp.float32,
    )
    res_rows = residual.shape[0]
    res_start = mp_index * res_rows
    current = lax.dynamic_slice_in_dim(projected, res_start, res_rows, 0)
    projected = lax.dynamic_update_slice_in_dim(
        projected, current + residual.astype(jnp.float32), res_start, 0
    )
    hidden = lax.psum(projected.astype(jnp.bfloat16), "mp")
    capacity = tokens * TOP // 4
    slots = route_slots(expert_ids)
    per_row = max(1, EXPERTS // mp_count)
    first_expert = mp_index * EXPERTS // mp_count
    own_expert = (mp_index * ctx_count + ctx_index) * EXPERTS // (ctx_count * mp_count)
    local = own_expert - first_expert
    row_experts = first_expert + jnp.arange(per_row, dtype=jnp.int32)
    match = expert_ids[None, :, :] == row_experts[:, None, None]
    place = jnp.where(match, slots[None, :, :], capacity)
    table = place[:, :, :, None] == jnp.arange(capacity, dtype=jnp.int32)[None, None, None, :]
    pick = jnp.any(table, axis=2)
    packed = jnp.einsum(
        "rtc,td->rcd", pick.astype(jnp.bfloat16), hidden, preferred_element_type=jnp.float32
    ).astype(jnp.bfloat16)
    gate_local = gate_proj[0]
    up_local = up_proj[0]
    down_local = down_proj[0]
    chosen = lax.dynamic_index_in_dim(
        lax.all_gather(packed, "ctx", axis=2, tiled=True), local, 0, keepdims=False
    )
    wide = chosen.astype(jnp.float32)
    gains = norm_gain.astype(jnp.float32)
    scaled = (wide * gains[None, :]).astype(jnp.bfloat16)
    gate_sum = jnp.dot(scaled, gate_local, preferred_element_type=jnp.float32)
    up_sum = jnp.dot(scaled, up_local, preferred_element_type=jnp.float32)
    gate_sum, up_sum, squares = (gate_sum, up_sum, jnp.sum(wide * wide, axis=1))
    rms = lax.rsqrt(squares / D + norm_eps)
    act = (jax.nn.silu(rms[:, None] * gate_sum) * (rms[:, None] * up_sum)).astype(jnp.bfloat16)
    part = lax.dot_general(
        down_local, act, (((0,), (1,)), ((), ())), preferred_element_type=jnp.float32
    )
    returned = lax.psum_scatter(
        jnp.concatenate(
            [jnp.where(local == which, part, 0.0) for which in range(per_row)], axis=1
        ).astype(jnp.bfloat16),
        "ctx",
        scatter_dimension=0,
        tiled=True,
    ).astype(jnp.float32)
    weights = jax.nn.softmax(route_logits, axis=1)
    combine = jnp.sum(jnp.where(table, weights[None, :, :, None], 0.0), axis=2)
    moe = jnp.einsum(
        "drc,rtc->td",
        returned.reshape(d_local, per_row, capacity),
        combine,
        precision=lax.Precision.HIGHEST,
        preferred_element_type=jnp.float32,
    )
    share = lax.psum_scatter(
        moe.astype(jnp.bfloat16), "mp", scatter_dimension=0, tiled=True
    ).astype(jnp.float32)
    own_hidden = lax.dynamic_slice_in_dim(hidden, res_start, res_rows, 0).astype(jnp.float32)
    return (own_hidden + share).astype(jnp.bfloat16)


def solution(mesh):
    placed = (
        P("ctx", "mp"),
        P("mp", "ctx", None),
        P("mp", "ctx", None),
        P("mp", "ctx", None),
        P("mp", "ctx", None),
        P("mp", "ctx"),
        P("mp", "ctx"),
        P(),
        P("ctx", None, "mp"),
        P("ctx", None, "mp"),
        P("ctx", "mp", None),
        P(),
        P(),
    )
    return jax.shard_map(
        on_device, mesh=mesh, in_specs=placed, out_specs=P("mp", "ctx"), check_vma=False
    )
```

profile of v0, /device:TPU:0, one launch (start us, length us, event | category | flops | bytes accessed | tf_op | source)
XLA Modules:
  0.0 234.1 jit_solution(1601538211125830650)
XLA Ops:
  6.5 1.3 maximum_bitcast_fusion
  7.8 0.9 pad_maximum_fusion.1
  8.8 0.8 copy.30
  9.8 0.6 reduce-window.6
  11.3 0.3 compare_or_fusion
  11.6 37.6 %all-gather.3.cloned.1.call-done = bf16[2,2,4224,128]{3,2,1,0:T(8,128)(2,1)} async-done(((bf16[2,2,528,128]{3,2,1,0:T(8,128)(2,1)}), bf16[2,2,4224,128]{3,2,1,0:T(8,128)(2,1)}) %all-gather.3.cloned.1.call-update) | async-done | bytes 4325392 | tf_op jit(solution)/shard_map/all_gather | solution.py:93
  49.3 2.8 %fusion.74 = (f32[2,96]{1,0:T(2,128)S(1)}, f32[2,96,4224]{2,1,0:T(8,128)S(1)}) fusion(bf16[2,96,128]{2,1,0:T(8,128)(2,1)S(1)} %bitcast.87, bf16[2,2,4224,128]{3,2,1,0:T(8,128)(2,1)} %all-gather.3.cloned.1.call-done, pred[96,4224]{1,0:T(8,128)(4,1)S(1)} %compare_or_fusion), kind=kOutput, calls=%fused_computation.88 | convolution fusion | flops 210050880 | bytes 5862144 | tf_op jit(solution)/shard_map/srd,skd->srk/dot_general | solution.py:26
  52.1 0.6 fusion.8
  52.7 0.8 fusion.36
  53.7 9.6 %all_gather.10 = bf16[128,1536]{1,0:T(8,128)(2,1)S(1)} all-gather(bf16[16,1536]{1,0:T(8,128)(2,1)S(1)} %reshape.152), channel_id=1, replica_groups=mesh['ctx'=8,'mp'=4] {'ctx'}, dimensions={0}, use_global_device_ids=true | all-gather | bytes 442368 | tf_op jit(solution)/shard_map/all_gather | solution.py:109
  63.2 0.5 fusion.81
  63.7 0.7 convert_element_type.59
  64.6 34.8 %all-reduce.2.cloned.1.call-done = bf16[128,768]{1,0:T(8,128)(2,1)} async-done(((bf16[128,768]{1,0:T(8,128)(2,1)}), bf16[128,768]{1,0:T(8,128)(2,1)}) %all-reduce.2.cloned.1.call-update) | async-done | bytes 196624 | tf_op jit(solution)/shard_map/psum | solution.py:119
  99.5 1.8 convolution_convert_fusion
  101.3 0.2 reduce-scatter.3.cloned.1.call-start
  101.6 25.4 %all-gather.5.cloned.1.call-done = bf16[2,64,6144]{2,1,0:T(8,128)(2,1)} async-done(((bf16[2,64,768]{2,1,0:T(8,128)(2,1)}), bf16[2,64,6144]{2,1,0:T(8,128)(2,1)}) %all-gather.5.cloned.1.call-update) | async-done | bytes 1572880 | tf_op jit(solution)/shard_map/all_gather | solution.py:138
  127.0 1.4 fusion.27
  128.4 13.7 %fusion.10 = f32[64,2048]{1,0:T(8,128)} fusion(bf16[1,6144,2048]{2,1,0:T(8,128)(2,1)} %param.21, f32[6144]{0:T(1024)S(1)} %convert_element_type.65, bf16[2,64,6144]{2,1,0:T(8,128)(2,1)} %all-gather.5.cloned.1.call-done, s32[]{:T(128)S(6)} %select_n.86, f32[64]{0:T(128)S(1)} %add_rsqrt_fusion), kind=kOutput, calls=%fused_computation.12 | convolution fusion | flops 1611923456 | bytes 26501380 | tf_op jit(solution)/shard_map/dot_general | solution.py:143
  142.1 21.4 %fusion.39 = (bf16[6144,64]{0,1:T(8,128)(2,1)S(1)}, bf16[6144,64]{0,1:T(8,128)(2,1)}) fusion(pred[]{:T(512)S(6)} %eq.77, pred[]{:T(512)S(6)} %eq.78, bf16[1,2048,6144]{2,1,0:T(8,128)(2,1)} %param.23, bf16[1,6144,2048]{2,1,0:T(8,128)(2,1)} %param.22, f32[6144]{0:T(1024)S(1)} %convert_element_type.65, bf16[2,64,6144]{2,1,0:T(8,128)(2,1)} %all-gather.5.cloned.1.call-done, ...), kind=kOutput, calls=%fused_computation.34 | convolution fusion | flops 3224109056 | bytes 53240072 | tf_op jit(solution)/shard_map/dot_general | solution.py:148
  163.5 2.4 %pad_maximum_fusion = bf16[6144,128]{0,1:T(8,128)(2,1)} fusion(bf16[6144,64]{0,1:T(8,128)(2,1)} %get-tuple-element.6, bf16[6144,64]{0,1:T(8,128)(2,1)S(1)} %get-tuple-element.5), kind=kLoop, calls=%fused_computation.25 | loop fusion | flops 3145728 | bytes 3145728 | tf_op jit(solution)/shard_map/concatenate | solution.py:152
  166.1 38.5 %reduce-scatter.3.cloned.1.call-done = bf16[768,128]{0,1:T(8,128)(2,1)} async-done(((bf16[6144,128]{0,1:T(8,128)(2,1)}), bf16[768,128]{0,1:T(8,128)(2,1)}) %reduce-scatter.3.cloned.1.call-update) | async-done | bytes 196624 | tf_op jit(solution)/shard_map/reduce_scatter | solution.py:151
  204.6 2.0 fusion.29
  206.6 19.6 %reduce-scatter.5.cloned.1.call-done = bf16[32,768]{1,0:T(8,128)(2,1)} async-done(((bf16[128,768]{1,0:T(8,128)(2,1)}), bf16[32,768]{1,0:T(8,128)(2,1)}) %reduce-scatter.5.cloned.1.call-update) | async-done | bytes 49168 | tf_op jit(solution)/shard_map/reduce_scatter | solution.py:168
  226.1 1.5 add_convert_fusion
  (56 shorter events, 1.6 us)
Async XLA Ops:
  6.5 56.7 %copy-start = (bf16[1536,768]{1,0:T(8,128)(2,1)S(1)}, bf16[1536,768]{1,0:T(8,128)(2,1)}, u32[]{:S(2)}) copy-start(bf16[1536,768]{1,0:T(8,128)(2,1)} %param.18) | copy-start | bytes 7077892
  6.5 4.6 %copy-start.2 = (bf16[16,1536]{1,0:T(8,128)(2,1)S(1)}, bf16[16,1536]{1,0:T(8,128)(2,1)}, u32[]{:S(2)}) copy-start(bf16[16,1536]{1,0:T(8,128)(2,1)} %param.13) | copy-start | bytes 147460
  6.5 42.7 %all-gather.3.cloned.1.call-start = ((), (), s32[]{:S(2)}) async-start(), calls=%async_computation.2 | async-start | bytes 4866048 | tf_op jit(solution)/shard_map/all_gather | solution.py:93
  8.7 90.8 %all-reduce.2.cloned.1.call-start = ((), (), s32[]{:S(2)}) async-start(), calls=%async_computation.3 | async-start | bytes 393216 | tf_op jit(solution)/shard_map/psum | solution.py:119
  49.3 3.4 %slice-start = ((s8[4325376]{0:T(1024)(128)(4,1)}), s8[4194304]{0:T(1024)(128)(4,1)S(1)}, s32[]{:S(2)}) async-start(s8[4325376]{0:T(1024)(128)(4,1)} %bitcast.89), calls=%async_computation.7 | async-start | bytes 8388608
  49.3 3.4 %slice-start.1 = ((s8[4325376]{0:T(1024)(128)(4,1)}), s8[131072]{0:T(1024)(128)(4,1)S(1)}, s32[]{:S(2)}) async-start(s8[4325376]{0:T(1024)(128)(4,1)} %bitcast.89), calls=%async_computation.8 | async-start | bytes 262144
  53.5 10.2 %copy-start.3 = (bf16[32,768]{1,0:T(8,128)(2,1)S(1)}, bf16[32,768]{1,0:T(8,128)(2,1)}, u32[]{:S(2)}) copy-start(bf16[32,768]{1,0:T(8,128)(2,1)} %param.19) | copy-start | bytes 147460
  53.5 11.0 %copy-start.6 = (s32[128,2]{0,1:T(2,128)S(1)}, s32[128,2]{0,1:T(2,128)}, u32[]{:S(2)}) copy-start(s32[128,2]{0,1:T(2,128)} %param.24) | copy-start | bytes 3076
  53.5 48.0 %copy-start.4 = (bf16[6144]{0:T(1024)(128)(2,1)S(1)}, bf16[6144]{0:T(1024)(128)(2,1)}, u32[]{:S(2)}) copy-start(bf16[6144]{0:T(1024)(128)(2,1)} %param.20) | copy-start | bytes 36868
  64.4 62.5 %all-gather.5.cloned.1.call-start = ((), (), s32[]{:S(2)}) async-start(), calls=%async_computation.4 | async-start | bytes 1769472 | tf_op jit(solution)/shard_map/all_gather | solution.py:138
  101.3 103.3 %reduce-scatter.3.cloned.1.call-start = ((), (), s32[]{:S(2)}) async-start(), calls=%async_computation.5 | async-start | bytes 1769472 | tf_op jit(solution)/shard_map/reduce_scatter | solution.py:151
  142.1 85.5 %copy-start.1 = (bf16[1536,768]{1,0:T(8,128)(2,1)S(1)}, bf16[1536,768]{1,0:T(8,128)(2,1)}, u32[]{:S(2)}) copy-start(bf16[1536,768]{1,0:T(8,128)(2,1)} %param.18) | copy-start | bytes 7077892
  163.5 2.5 %copy-start.5 = (f32[128,2]{0,1:T(2,128)S(1)}, f32[128,2]{0,1:T(2,128)}, u32[]{:S(2)}) copy-start(f32[128,2]{0,1:T(2,128)} %param.25) | copy-start | bytes 3076
  166.0 60.2 %reduce-scatter.5.cloned.1.call-start = ((), (), s32[]{:S(2)}) async-start(), calls=%async_computation.6 | async-start | bytes 245760 | tf_op jit(solution)/shard_map/reduce_scatter | solution.py:168
Sparse Core Ops, SparseCore 0:
  9.3 39.9 all-gather.2
  64.6 34.8 all-reduce.1
  101.5 25.3 all-gather.4
  166.1 38.4 reduce-scatter.2
  206.8 19.3 reduce-scatter.4
where the time goes:
time: 235 us; the launch traced here: 234 us
  waiting for transfers between devices  156 us (66%)
  matrix products  42.9 us (18%)
  between operations  13.4 us (6%)
  other arithmetic  10 us (4%)
  blocking collectives  9.55 us (4%)
    reduce_scatter x1, waiting for transfers between devices, on_device(): lax.psum_scatter(jnp.concatenate([jnp.where(local == which, part, 0.0) fo...  38.5 us
    all_gather x1, waiting for transfers between devices, on_device(): piece = lax.all_gather(key_value, 'ctx', axis=2, tiled=True)  37.6 us
    psum x1, waiting for transfers between devices, on_device(): hidden = lax.psum(projected.astype(jnp.bfloat16), 'mp')  34.8 us
    all_gather x1, waiting for transfers between devices, on_device(): lax.all_gather(packed, 'ctx', axis=2, tiled=True)  25.4 us
    dot_general x1, matrix products, on_device(): lax.dot_general(down_local, act, (((0,), (1,)), ((), ())), preferred_elem...  21.4 us
    reduce_scatter x1, waiting for transfers between devices, on_device(): lax.psum_scatter(moe.astype(jnp.bfloat16), 'mp', scatter_dimension=0, til...  19.6 us
    dot_general x1, matrix products, on_device(): gate_sum = jnp.dot(scaled, gate_local, preferred_element_type=jnp.float32)  13.7 us
    all_gather x1, blocking collectives, on_device(): lax.all_gather(attn, 'ctx', axis=0, tiled=True)  9.55 us
  transfers between devices with their start and end apart: 5, of which 5 were waited for; matrix products, arithmetic and copies ran while one was open for 1% of the time, Pallas kernels for 0%

commit v1 on v0

--- a/solution.py
+++ b/solution.py
@@ -3,6 +3,8 @@
 import jax
 import jax.numpy as jnp
 from jax import lax
+from jax.experimental import pallas as pl
+from jax.experimental.pallas import tpu as pltpu
 from jax.sharding import PartitionSpec as P
 
 D = 6144
@@ -44,7 +46,7 @@
     return (highest, denom, summed)
 
 
-def on_device(
+def gathered_path(
     queries,
     cache_keys,
     cache_values,
@@ -172,6 +174,279 @@
     return (own_hidden + share).astype(jnp.bfloat16)
 
 
+BF16 = jnp.bfloat16
+F32 = jnp.float32
+
+
+def swap(array, axis_name, mask):
+    count = lax.axis_size(axis_name)
+    return lax.ppermute(array, axis_name, [(i, i ^ mask) for i in range(count)])
+
+
+def experts_kernel(
+    place_ref, even_ref, odd_ref, gain_ref, gate_hbm, up_hbm, down_hbm, out_even_ref, out_odd_ref,
+    scaled_ref, act_ref, gate_acc, up_acc, out_acc, gate_buf, up_buf, down_buf, gate_sem, up_sem, down_sem,
+):
+    own = place_ref[0]
+    half = even_ref.shape[0]
+    blocks = 2 * half
+    deep = even_ref.shape[2]
+    ring = gate_buf.shape[0]
+    down_blocks, down_rows = down_buf.shape[0], down_buf.shape[1]
+
+    def gate_copy(step):
+        rows = pl.ds(pl.multiple_of((own ^ step) * deep, deep), deep)
+        slot = lax.rem(step, ring)
+        return (
+            pltpu.make_async_copy(gate_hbm.at[0, rows, :], gate_buf.at[slot], gate_sem.at[slot]),
+            pltpu.make_async_copy(up_hbm.at[0, rows, :], up_buf.at[slot], up_sem.at[slot]),
+        )
+
+    def down_copy(step):
+        rows = pl.ds(pl.multiple_of(step * down_rows, down_rows), down_rows)
+        return pltpu.make_async_copy(down_hbm.at[0, rows, :], down_buf.at[step], down_sem.at[step])
+
+    for step in range(ring):
+        for copy in gate_copy(jnp.int32(step)):
+            copy.start()
+    squares = jnp.zeros((even_ref.shape[1], 1), F32)
+    for step in range(blocks):
+        wide = (even_ref if step % 2 == 0 else odd_ref)[step // 2].astype(F32)
+        squares = squares + jnp.sum(wide * wide, axis=1, keepdims=True)
+        scaled_ref[step] = (wide * gain_ref[own ^ step]).astype(BF16)
+    rms = lax.rsqrt(squares / D + norm_eps)
+    gate_acc[...] = jnp.zeros_like(gate_acc)
+    up_acc[...] = jnp.zeros_like(up_acc)
+
+    def gate_step(step, carry):
+        slot = lax.rem(step, ring)
+        for copy in gate_copy(step):
+            copy.wait()
+        rows = scaled_ref[step]
+        gate_acc[...] += jnp.dot(rows, gate_buf[slot], preferred_element_type=F32)
+        up_acc[...] += jnp.dot(rows, up_buf[slot], preferred_element_type=F32)
+
+        @pl.when(step + ring < blocks)
+        def _():
+            for copy in gate_copy(step + ring):
+                copy.start()
+
+        @pl.when(step + ring == blocks)
+        def _():
+            for index in range(down_blocks):
+                down_copy(jnp.int32(index)).start()
+
+        return carry
+
+    lax.fori_loop(0, blocks, gate_step, 0)
+    gate = rms * gate_acc[...]
+    act = (gate / (1.0 + jnp.exp(-gate)) * (rms * up_acc[...])).astype(BF16)
+    for index in range(down_blocks):
+        act_ref[index] = act[:, index * down_rows : (index + 1) * down_rows]
+    out_acc[...] = jnp.zeros_like(out_acc)
+
+    def down_step(step, carry):
+        down_copy(step).wait()
+        out_acc[...] += jnp.dot(act_ref[step], down_buf[step], preferred_element_type=F32)
+        return carry
+
+    lax.fori_loop(0, down_blocks, down_step, 0)
+    for step in range(blocks):
+        columns = pl.ds(pl.multiple_of((own ^ step) * deep, deep), deep)
+        (out_even_ref if step % 2 == 0 else out_odd_ref)[step // 2] = out_acc[:, columns].astype(BF16)
+
+
+def run_experts(place, even, odd, gain, gate_proj, up_proj, down_proj):
+    half, rows, deep = even.shape
+    units = gate_proj.shape[2]
+    wide = down_proj.shape[2]
+    ring, down_blocks = 3, 8
+    vmem = pl.BlockSpec(memory_space=pltpu.VMEM)
+    hbm = pl.BlockSpec(memory_space=pl.ANY)
+    weights = 2 * (2 * gate_proj.size + down_proj.size)
+    return pl.pallas_call(
+        experts_kernel,
+        out_shape=(jax.ShapeDtypeStruct(even.shape, BF16),) * 2,
+        in_specs=[pl.BlockSpec(memory_space=pltpu.SMEM), vmem, vmem, vmem, hbm, hbm, hbm],
+        out_specs=(vmem, vmem),
+        scratch_shapes=[
+            pltpu.VMEM((2 * half, rows, deep), BF16),
+            pltpu.VMEM((down_blocks, rows, units // down_blocks), BF16),
+            pltpu.VMEM((rows, units), F32),
+            pltpu.VMEM((rows, units), F32),
+            pltpu.VMEM((rows, wide), F32),
+            pltpu.VMEM((ring, deep, units), BF16),
+            pltpu.VMEM((ring, deep, units), BF16),
+            pltpu.VMEM((down_blocks, units // down_blocks, wide), BF16),
+            pltpu.SemaphoreType.DMA((ring,)),
+            pltpu.SemaphoreType.DMA((ring,)),
+            pltpu.SemaphoreType.DMA((down_blocks,)),
+        ],
+        compiler_params=pltpu.CompilerParams(vmem_limit_bytes=58 << 20),
+        cost_estimate=pl.CostEstimate(flops=rows * weights, bytes_accessed=weights, transcendentals=rows * units),
+        name="experts",
+    )(place, even, odd, gain, gate_proj, up_proj, down_proj)
+
+
+def exchange_path(
+    queries,
+    cache_keys,
+    cache_values,
+    new_keys,
+    new_values,
+    out_proj,
+    residual,
+    norm_gain,
+    gate_proj,
+    up_proj,
+    down_proj,
+    expert_ids,
+    route_logits,
+):
+    ctx_count = lax.axis_size("ctx")
+    mp_count = lax.axis_size("mp")
+    ctx_index = lax.axis_index("ctx")
+    mp_index = lax.axis_index("mp")
+    tok_local = queries.shape[0]
+    tokens = tok_local * ctx_count
+    slot_local, cache_local, head_dim = cache_keys.shape
+    heads_local = queries.shape[1] // head_dim
+    group_size = heads_local // slot_local
+    d_local = out_proj.shape[1]
+    res_rows = residual.shape[0]
+    half = ctx_count // 2
+    scale = 1.0 / math.sqrt(head_dim)
+    capacity = tokens * TOP // 4
+    per_row = max(1, EXPERTS // mp_count)
+    first_expert = mp_index * EXPERTS // mp_count
+
+    def local_expert(ctx_at):
+        return (mp_index * ctx_count + ctx_at) * EXPERTS // (ctx_count * mp_count) - first_expert
+
+    blocks = [queries] + [swap(queries, "ctx", 2 * k) for k in range(1, half)]
+    pair_keys = [swap(cache_keys, "ctx", 1), swap(new_keys, "ctx", 1)]
+    pair_values = [swap(cache_values, "ctx", 1), swap(new_values, "ctx", 1)]
+    keys = jnp.concatenate([cache_keys, pair_keys[0], new_keys, pair_keys[1]], axis=1)
+    values = jnp.concatenate([cache_values, pair_values[0], new_values, pair_values[1]], axis=1)
+    rows = half * tok_local
+    shaped = jnp.stack(blocks).reshape(rows, slot_local, group_size, head_dim)
+    query_block = jnp.transpose(shaped, (1, 2, 0, 3)).reshape(slot_local, group_size * rows, head_dim)
+    row = jnp.arange(group_size * rows, dtype=jnp.int32) % rows
+    row_tok = (ctx_index ^ (2 * (row // tok_local))) * tok_local + row % tok_local
+    column = jnp.arange(2 * (cache_local + tok_local), dtype=jnp.int32)
+    late = column - 2 * cache_local
+    key_tok = (ctx_index ^ (late // tok_local)) * tok_local + late % tok_local
+    allowed = (late < 0)[None, :] | (key_tok[None, :] <= row_tok[:, None])
+    scores = jnp.einsum("srd,skd->srk", query_block, keys, preferred_element_type=F32) * scale
+    scores = jnp.where(allowed[None, :, :], scores, neg_big)
+    shift = lax.reduce_precision(jnp.max(scores, axis=2), 8, 7)
+    expo = jnp.exp(scores - shift[:, :, None])
+    denom = jnp.sum(expo, axis=2)
+    summed = jnp.einsum("srk,skd->srd", expo.astype(BF16), values, preferred_element_type=F32)
+    denom_high = lax.reduce_precision(denom, 8, 7)
+    stats = jnp.stack([shift, denom_high, denom - denom_high]).reshape(3 * heads_local, rows)
+    stats = jnp.pad(stats.astype(BF16).T, ((0, 0), (0, head_dim - 3 * heads_local)))
+    mine = jnp.concatenate(
+        [summed.astype(BF16).reshape(heads_local, rows, head_dim), stats[None]], axis=0
+    )
+
+    def ordered(array, k):
+        parts = array.reshape(heads_local + 1, half, tok_local, head_dim)
+        parts = jnp.concatenate([parts[:, k ^ b : (k ^ b) + 1] for b in range(half)], axis=1)
+        return parts.reshape(heads_local + 1, rows, head_dim)
+
+    partials = [mine] + [ordered(swap(mine, "ctx", 2 * k), k) for k in range(1, half)]
+    pieces = []
+    for part in partials:
+        held = part[heads_local, :, : 3 * heads_local].astype(F32).T.reshape(3, heads_local, rows)
+        pieces.append((held[0], held[1] + held[2], part[:heads_local].astype(F32)))
+    highest = pieces[0][0]
+    for piece in pieces[1:]:
+        highest = jnp.maximum(highest, piece[0])
+    lifts = [jnp.exp(piece[0] - highest) for piece in pieces]
+    total = sum(lift * piece[1] for lift, piece in zip(lifts, pieces))
+    mixed = sum((lift / total)[:, :, None] * piece[2] for lift, piece in zip(lifts, pieces))
+    attn = jnp.transpose(mixed.astype(BF16), (1, 0, 2)).reshape(half, tok_local, heads_local * head_dim)
+    attn_pair = swap(attn, "ctx", 1)
+    is_odd = (ctx_index & 1) == 1
+    attn = jnp.stack([jnp.where(is_odd, attn_pair, attn), jnp.where(is_odd, attn, attn_pair)], axis=1)
+
+    projected = jnp.dot(
+        attn.reshape(tokens, heads_local * head_dim), out_proj, preferred_element_type=F32
+    ).reshape(mp_count, res_rows, d_local)
+    pair_at = (ctx_index // 2) ^ mp_index
+    parts = [lax.dynamic_index_in_dim(projected, pair_at ^ k, 0, keepdims=False) for k in range(mp_count)]
+    hidden = parts[0] + residual.astype(F32)
+    for k in range(1, mp_count):
+        hidden = hidden + swap(parts[k].astype(BF16), "mp", k).astype(F32)
+    hidden = hidden.astype(BF16)
+
+    order = mp_index ^ jnp.arange(mp_count, dtype=jnp.int32)
+
+    def by_block(table):
+        return jnp.take(table.reshape(mp_count, res_rows, TOP), order, axis=0).reshape(tokens, TOP)
+
+    ids = by_block(expert_ids)
+    slots = by_block(route_slots(expert_ids))
+    weights = by_block(jax.nn.softmax(route_logits, axis=1))
+    row_experts = first_expert + jnp.arange(per_row, dtype=jnp.int32)
+    match = ids[None, :, :] == row_experts[:, None, None]
+    place = jnp.where(match, slots[None, :, :], capacity)
+    table = place[:, :, :, None] == jnp.arange(capacity, dtype=jnp.int32)[None, None, None, :]
+    pick = jnp.any(table, axis=2).astype(BF16)
+    combine = jnp.sum(jnp.where(table, weights[None, :, :, None], 0.0), axis=2)
+
+    everyone = jnp.concatenate([hidden] + [swap(hidden, "mp", k) for k in range(1, mp_count)], axis=0)
+    packed = jnp.einsum("rtc,td->rcd", pick, everyone, preferred_element_type=F32).astype(BF16)
+    even = [lax.dynamic_index_in_dim(packed, local_expert(ctx_index), 0, keepdims=False)]
+    for k in range(1, half):
+        sent = lax.dynamic_index_in_dim(packed, local_expert(ctx_index ^ (2 * k)), 0, keepdims=False)
+        even.append(swap(sent, "ctx", 2 * k))
+    even = jnp.stack(even)
+    odd = swap(even, "ctx", 1)
+    out_even, out_odd = run_experts(
+        ctx_index.reshape(1),
+        even,
+        odd,
+        norm_gain.astype(F32).reshape(ctx_count, 1, d_local),
+        gate_proj,
+        up_proj,
+        down_proj,
+    )
+    summed = (out_even.astype(F32) + swap(out_odd, "ctx", 1).astype(F32)).astype(BF16)
+    returned = [summed[0]] + [swap(summed[k], "ctx", 2 * k) for k in range(1, half)]
+    spread = [
+        lax.dynamic_index_in_dim(combine, local_expert(ctx_index ^ (2 * k)), 0, keepdims=False)
+        for k in range(half)
+    ]
+    spread = jnp.concatenate(spread, axis=1)
+    spread_high = lax.reduce_precision(spread, 8, 7)
+    spread = jnp.concatenate([spread_high, spread - spread_high], axis=1).astype(BF16)
+    moe = jnp.dot(
+        spread, jnp.concatenate(returned + returned, axis=0), preferred_element_type=F32
+    ).reshape(mp_count, res_rows, d_local)
+    total = hidden.astype(F32) + moe[0]
+    for k in range(1, mp_count):
+        total = total + swap(moe[k].astype(BF16), "mp", k).astype(F32)
+    return total.astype(BF16)
+
+
+def on_device(*args):
+    queries, cache_keys, out_proj, gate_proj, down_proj = (args[i] for i in (0, 1, 5, 8, 10))
+    ctx_count, mp_count = lax.axis_size("ctx"), lax.axis_size("mp")
+    per_row = max(1, EXPERTS // mp_count)
+    fits = (
+        ctx_count == 2 * mp_count
+        and ctx_count & (ctx_count - 1) == 0
+        and (ctx_count // per_row) % 2 == 0
+        and out_proj.shape[1] % 256 == 0
+        and gate_proj.shape[2] % 2048 == 0
+        and queries.shape[0] % 16 == 0
+        and 3 * (queries.shape[1] // cache_keys.shape[2]) <= cache_keys.shape[2]
+    )
+    return exchange_path(*args) if fits else gathered_path(*args)
+
+
 def solution(mesh):
     placed = (
         P("ctx", "mp"),

time: 235 us -> 112 us (0.48)
  waiting for transfers between devices: 156 us -> 34.6 us
  matrix products: 42.9 us -> 5.55 us
  starting transfers between devices: 0.35 us -> 30.3 us
  Pallas kernels: 0 us -> 25.9 us
  between operations: 13.4 us -> 0.78 us
  blocking collectives: 9.55 us -> 0 us
  local copies, waits for them, and re-layouts: 1.81 us -> 8.19 us
  other arithmetic: 10 us -> 6.81 us
    all_gather x2 -> x0, waiting for transfers between devices: 63 us -> none  [the longest x1 37.6 us: on_device(): piece = lax.all_gather(key_value, 'ctx', axis=2, tiled=True)]
    reduce_scatter x2 -> x0, waiting for transfers between devices: 58 us -> none  [the longest x1 38.5 us: on_device(): lax.psum_scatter(jnp.concatenate([jnp.where(local == which, part, 0.0) fo...]
    dot_general x7 -> x5, matrix products: 42.9 us -> 5.55 us  [the longest x1 2.77 us: exchange_path(): jnp.einsum('srk,skd->srd', expo.astype(BF16), values, preferred_element_t...]
    psum x1 -> x0, waiting for transfers between devices: 34.8 us -> none  [on_device(): hidden = lax.psum(projected.astype(jnp.bfloat16), 'mp')]
    ppermute x0 -> x28, waiting for transfers between devices: none -> 34.6 us  [swap(): return lax.ppermute(array, axis_name, [(i, i ^ mask) for i in range(count)])]
    ppermute x0 -> x28, starting transfers between devices: none -> 30.3 us  [swap(): return lax.ppermute(array, axis_name, [(i, i ^ mask) for i in range(count)])]
    pallas_call x0 -> x1, Pallas kernels: none -> 25.9 us  [run_experts(): pl.pallas_call(experts_kernel, out_shape=(jax.ShapeDtypeStruct(even.shape...]
    all_gather x1 -> x0, blocking collectives: 9.55 us -> none  [on_device(): lax.all_gather(attn, 'ctx', axis=0, tiled=True)]
  transfers between devices with their start and end apart: 5 -> 28, of which waited for: 5 -> 17; matrix products, arithmetic and copies ran while one was open for 1% -> 10% of each run, Pallas kernels for 0% -> 0%
where the time goes in v1:
time: 112 us
  waiting for transfers between devices  34.6 us (31%)
  starting transfers between devices  30.3 us (27%)
  Pallas kernels  25.9 us (23%)
  local copies, waits for them, and re-layouts  8.19 us (7%)
  other arithmetic  6.81 us (6%)
  matrix products  5.55 us (5%)
    ppermute x28, waiting for transfers between devices, swap(): return lax.ppermute(array, axis_name, [(i, i ^ mask) for i in range(count)])  34.6 us
    ppermute x28, starting transfers between devices, swap(): return lax.ppermute(array, axis_name, [(i, i ^ mask) for i in range(count)])  30.3 us
    pallas_call x1, Pallas kernels, run_experts(): pl.pallas_call(experts_kernel, out_shape=(jax.ShapeDtypeStruct(even.shape...  25.9 us
    unnamed x37, local copies, waits for them, and re-layouts  3.46 us
    dot_general x1, matrix products, exchange_path(): jnp.einsum('srk,skd->srd', expo.astype(BF16), values, preferred_element_t...  2.77 us
  transfers between devices with their start and end apart: 28, of which 17 were waited for; matrix products, arithmetic and copies ran while one was open for 10% of the time, Pallas kernels for 0%

profile of v1, /device:TPU:0, one launch (start us, length us, event | category | flops | bytes accessed | tf_op | source)
XLA Modules:
  0.0 112.1 jit_solution(4426800233288112984)
XLA Ops:
  0.0 2.9 %collective-permute-start = (bf16[16,1536]{1,0:T(8,128)(2,1)}, bf16[16,1536]{1,0:T(8,128)(2,1)S(1)}, u32[]{:S(2)}, u32[]{:S(2)}) collective-permute-start(bf16[16,1536]{1,0:T(8,128)(2,1)} %param.15), channel_id=1, source_target_pairs={{0,8},{4,12},{8,0},{12,4},{16,24},{20,28},{24,16},{28,20},{1,9},{5... | collective-permute-start | bytes 147464 | tf_op jit(solution)/shard_map/ppermute | solution.py:183
  2.9 1.5 %collective-permute-start.1 = (bf16[16,1536]{1,0:T(8,128)(2,1)}, bf16[16,1536]{1,0:T(8,128)(2,1)S(1)}, u32[]{:S(2)}, u32[]{:S(2)}) collective-permute-start(bf16[16,1536]{1,0:T(8,128)(2,1)} %param.15), channel_id=1, source_target_pairs={{0,16},{4,20},{8,24},{12,28},{16,0},{20,4},{24,8},{28,12},{1,17},{... | collective-permute-start | bytes 147464 | tf_op jit(solution)/shard_map/ppermute | solution.py:183
  11.8 1.8 %fusion.100 = (f32[2,384]{1,0:T(2,128)S(1)}, f32[2,384,1056]{1,2,0:T(8,128)S(1)}) fusion(bf16[2,384,128]{2,1,0:T(8,128)(2,1)S(1)} %bitcast.158, bf16[2,16,128]{2,1,0:T(8,128)(2,1)S(1)} %collective-permute-done.4, bf16[2,16,128]{2,1,0:T(8,128)(2,1)S(1)} %copy-done.9, bf16[2,512,128]{2,1,0:T(8,128)(2,1)} %collective-permute-done.3, ...), kind=kOutput, calls=%fused_computation.204 | convolution fusion | flops 212212992 | bytes 4389888 | tf_op jit(solution)/shard_map/srd,skd->srk/dot_general | solution.py:340
  13.7 1.6 %copy-done.2 = f32[2,384,1056]{1,2,0:T(8,128)} copy-done((f32[2,384,1056]{1,2,0:T(8,128)}, f32[2,384,1056]{1,2,0:T(8,128)S(1)}, u32[]{:S(2)}) %copy-start.2) | copy-done | bytes 3244056
  16.0 2.8 %fusion.8 = bf16[2,384,128]{2,1,0:T(8,128)(2,1)S(1)} fusion(f32[2,384,1056]{1,2,0:T(8,128)} %copy-done.2, f32[2,384]{1,0:T(2,128)S(1)} %get-tuple-element.48, bf16[2,16,128]{2,1,0:T(8,128)(2,1)S(1)} %collective-permute-done.6, bf16[2,16,128]{2,1,0:T(8,128)(2,1)S(1)} %copy-done.10, bf16[2,512,128]{2,1,0:T(8,128)(2,1)} %collective-permute-done.5, ...), kind=kOutput, calls=%fused_computation.13 | convolution fusion | flops 211501056 | bytes 3984384 | tf_op jit(solution)/shard_map/srk,skd->srd/dot_general | solution.py:345
  18.9 3.0 %collective-permute-start.9 = (bf16[13,64,128]{2,1,0:T(8,128)(2,1)S(1)}, bf16[13,64,128]{2,1,0:T(8,128)(2,1)S(1)}, u32[]{:S(2)}, u32[]{:S(2)}) collective-permute-start(bf16[13,64,128]{2,1,0:T(8,128)(2,1)S(1)} %pad_maximum_fusion.2), channel_id=1, source_target_pairs={{0,24},{4,28},{8,16},{12,20},{16,8},{20,12},{24,0},{28,4},{1,25},{... | collective-permute-start | bytes 638984 | tf_op jit(solution)/shard_map/ppermute | solution.py:183
  22.5 5.5 %collective-permute-done.9 = bf16[13,64,128]{2,1,0:T(8,128)(2,1)S(1)} collective-permute-done((bf16[13,64,128]{2,1,0:T(8,128)(2,1)S(1)}, bf16[13,64,128]{2,1,0:T(8,128)(2,1)S(1)}, u32[]{:S(2)}, u32[]{:S(2)}) %collective-permute-start.9) | collective-permute-done | bytes 213024 | tf_op jit(solution)/shard_map/ppermute | solution.py:183
  28.1 3.8 %collective-permute-done.8 = bf16[13,64,128]{2,1,0:T(8,128)(2,1)S(1)} collective-permute-done((bf16[13,64,128]{2,1,0:T(8,128)(2,1)S(1)}, bf16[13,64,128]{2,1,0:T(8,128)(2,1)S(1)}, u32[]{:S(2)}, u32[]{:S(2)}) %collective-permute-start.8) | collective-permute-done | bytes 213024 | tf_op jit(solution)/shard_map/ppermute | solution.py:183
  35.6 1.8 %collective-permute-start.11 = (bf16[32,768]{1,0:T(8,128)(2,1)S(1)}, bf16[32,768]{1,0:T(8,128)(2,1)S(1)}, u32[]{:S(2)}, u32[]{:S(2)}) collective-permute-start(bf16[32,768]{1,0:T(8,128)(2,1)S(1)} %get-tuple-element.16), channel_id=1, source_target_pairs={{0,1},{1,0},{2,3},{3,2},{4,5},{5,4},{6,7},{7,6},{8,9},{9,8},{10,11... | collective-permute-start | bytes 147464 | tf_op jit(solution)/shard_map/ppermute | solution.py:183
  37.4 2.6 %collective-permute-start.12 = (bf16[32,768]{1,0:T(8,128)(2,1)S(1)}, bf16[32,768]{1,0:T(8,128)(2,1)S(1)}, u32[]{:S(2)}, u32[]{:S(2)}) collective-permute-start(bf16[32,768]{1,0:T(8,128)(2,1)S(1)} %get-tuple-element.18), channel_id=1, source_target_pairs={{0,2},{1,3},{2,0},{3,1},{4,6},{5,7},{6,4},{7,5},{8,10},{9,11},{10,... | collective-permute-start | bytes 147464 | tf_op jit(solution)/shard_map/ppermute | solution.py:183
  40.1 3.1 %collective-permute-done.12 = bf16[32,768]{1,0:T(8,128)(2,1)S(1)} collective-permute-done((bf16[32,768]{1,0:T(8,128)(2,1)S(1)}, bf16[32,768]{1,0:T(8,128)(2,1)S(1)}, u32[]{:S(2)}, u32[]{:S(2)}) %collective-permute-start.12) | collective-permute-done | bytes 49184 | tf_op jit(solution)/shard_map/ppermute | solution.py:183
  43.3 2.6 %collective-permute-done.13 = bf16[32,768]{1,0:T(8,128)(2,1)S(1)} collective-permute-done((bf16[32,768]{1,0:T(8,128)(2,1)S(1)}, bf16[32,768]{1,0:T(8,128)(2,1)S(1)}, u32[]{:S(2)}, u32[]{:S(2)}) %collective-permute-start.13) | collective-permute-done | bytes 49184 | tf_op jit(solution)/shard_map/ppermute | solution.py:183
  46.0 1.6 %collective-permute-start.15 = (bf16[32,768]{1,0:T(8,128)(2,1)S(1)}, bf16[32,768]{1,0:T(8,128)(2,1)S(1)}, u32[]{:S(2)}, u32[]{:S(2)}) collective-permute-start(bf16[32,768]{1,0:T(8,128)(2,1)S(1)} %fusion.49), channel_id=1, source_target_pairs={{0,2},{1,3},{2,0},{3,1},{4,6},{5,7},{6,4},{7,5},{8,10},{9,11},{10,... | collective-permute-start | bytes 147464 | tf_op jit(solution)/shard_map/ppermute | solution.py:183
  47.6 2.8 %collective-permute-start.16 = (bf16[32,768]{1,0:T(8,128)(2,1)S(1)}, bf16[32,768]{1,0:T(8,128)(2,1)S(1)}, u32[]{:S(2)}, u32[]{:S(2)}) collective-permute-start(bf16[32,768]{1,0:T(8,128)(2,1)S(1)} %fusion.49), channel_id=1, source_target_pairs={{0,3},{1,2},{2,1},{3,0},{4,7},{5,6},{6,5},{7,4},{8,11},{9,10},{10,... | collective-permute-start | bytes 147464 | tf_op jit(solution)/shard_map/ppermute | solution.py:183
  51.2 2.3 %collective-permute-done.16 = bf16[32,768]{1,0:T(8,128)(2,1)S(1)} collective-permute-done((bf16[32,768]{1,0:T(8,128)(2,1)S(1)}, bf16[32,768]{1,0:T(8,128)(2,1)S(1)}, u32[]{:S(2)}, u32[]{:S(2)}) %collective-permute-start.16) | collective-permute-done | bytes 49184 | tf_op jit(solution)/shard_map/ppermute | solution.py:183
  53.7 1.6 %collective-permute-start.17 = (bf16[64,768]{1,0:T(8,128)(2,1)S(1)}, bf16[64,768]{1,0:T(8,128)(2,1)S(1)}, u32[]{:S(2)}, u32[]{:S(2)}) collective-permute-start(bf16[64,768]{1,0:T(8,128)(2,1)S(1)} %get-tuple-element.37), channel_id=1, source_target_pairs={{0,8},{4,12},{8,0},{12,4},{16,24},{20,28},{24,16},{28,20},{1,9},{5... | collective-permute-start | bytes 294920 | tf_op jit(solution)/shard_map/ppermute | solution.py:183
  58.4 1.5 %collective-permute-done.18 = bf16[64,768]{1,0:T(8,128)(2,1)S(1)} collective-permute-done((bf16[64,768]{1,0:T(8,128)(2,1)S(1)}, bf16[64,768]{1,0:T(8,128)(2,1)S(1)}, u32[]{:S(2)}, u32[]{:S(2)}) %collective-permute-start.18) | collective-permute-done | bytes 98336 | tf_op jit(solution)/shard_map/ppermute | solution.py:183
  59.9 1.7 %collective-permute-done.19 = bf16[64,768]{1,0:T(8,128)(2,1)S(1)} collective-permute-done((bf16[64,768]{1,0:T(8,128)(2,1)S(1)}, bf16[64,768]{1,0:T(8,128)(2,1)S(1)}, u32[]{:S(2)}, u32[]{:S(2)}) %collective-permute-start.19) | collective-permute-done | bytes 98336 | tf_op jit(solution)/shard_map/ppermute | solution.py:183
  64.2 25.9 %experts.1 = (bf16[4,64,768]{2,1,0:T(8,128)(2,1)}, bf16[4,64,768]{2,1,0:T(8,128)(2,1)}) custom-call(s32[1]{0:T(128)} %bitcast.49.place_ref, bf16[4,64,768]{2,1,0:T(8,128)(2,1)} %copy-done.3, bf16[4,64,768]{2,1,0:T(8,128)(2,1)} %copy-done.4, f32[8,1,768]{2,1,0:T(1,128)} %bitcast.159, bf16[1,6144,2048]{2,1,0:T(8,128)(2,1)} %gate_hbm.1, ...), custom_call_target="tpu_custom_call" | custom-call | flops 4831838208 | bytes 75497472 | tf_op jit(solution)/shard_map/experts/pallas_call | solution.py:267
  95.3 1.7 %collective-permute-start.24 = (bf16[64,768]{1,0:T(8,128)(2,1)S(1)}, bf16[64,768]{1,0:T(8,128)(2,1)S(1)}, u32[]{:S(2)}, u32[]{:S(2)}) collective-permute-start(bf16[64,768]{1,0:T(8,128)(2,1)S(1)} %get-tuple-element.13), channel_id=1, source_target_pairs={{0,24},{4,28},{8,16},{12,20},{16,8},{20,12},{24,0},{28,4},{1,25},{... | collective-permute-start | bytes 294920 | tf_op jit(solution)/shard_map/ppermute | solution.py:183
  97.0 1.5 %collective-permute-done.22 = bf16[64,768]{1,0:T(8,128)(2,1)S(1)} collective-permute-done((bf16[64,768]{1,0:T(8,128)(2,1)S(1)}, bf16[64,768]{1,0:T(8,128)(2,1)S(1)}, u32[]{:S(2)}, u32[]{:S(2)}) %collective-permute-start.22) | collective-permute-done | bytes 98336 | tf_op jit(solution)/shard_map/ppermute | solution.py:183
  98.5 3.1 %collective-permute-done.23 = bf16[64,768]{1,0:T(8,128)(2,1)S(1)} collective-permute-done((bf16[64,768]{1,0:T(8,128)(2,1)S(1)}, bf16[64,768]{1,0:T(8,128)(2,1)S(1)}, u32[]{:S(2)}, u32[]{:S(2)}) %collective-permute-start.23) | collective-permute-done | bytes 98336 | tf_op jit(solution)/shard_map/ppermute | solution.py:183
  102.2 3.3 %collective-permute-start.26 = (bf16[32,768]{1,0:T(8,128)(2,1)S(1)}, bf16[32,768]{1,0:T(8,128)(2,1)S(1)}, u32[]{:S(2)}, u32[]{:S(2)}) collective-permute-start(bf16[32,768]{1,0:T(8,128)(2,1)S(1)} %get-tuple-element.33), channel_id=1, source_target_pairs={{0,2},{1,3},{2,0},{3,1},{4,6},{5,7},{6,4},{7,5},{8,10},{9,11},{10,... | collective-permute-start | bytes 147464 | tf_op jit(solution)/shard_map/ppermute | solution.py:183
  107.6 3.8 %collective-permute-done.27 = bf16[32,768]{1,0:T(8,128)(2,1)S(1)} collective-permute-done((bf16[32,768]{1,0:T(8,128)(2,1)S(1)}, bf16[32,768]{1,0:T(8,128)(2,1)S(1)}, u32[]{:S(2)}, u32[]{:S(2)}) %collective-permute-start.27) | collective-permute-done | bytes 49184 | tf_op jit(solution)/shard_map/ppermute | solution.py:183
  (158 shorter events, 27.5 us)
Async XLA Ops:
  0.0 10.1 %collective-permute-start = (bf16[16,1536]{1,0:T(8,128)(2,1)}, bf16[16,1536]{1,0:T(8,128)(2,1)S(1)}, u32[]{:S(2)}, u32[]{:S(2)}) collective-permute-start(bf16[16,1536]{1,0:T(8,128)(2,1)} %param.15), channel_id=1, source_target_pairs={{0,8},{4,12},{8,0},{12,4},{16,24},{20,28},{24,16},{28,20},{1,9},{5... | collective-permute-start | bytes 147464 | tf_op jit(solution)/shard_map/ppermute | solution.py:183
  2.9 7.2 %collective-permute-start.1 = (bf16[16,1536]{1,0:T(8,128)(2,1)}, bf16[16,1536]{1,0:T(8,128)(2,1)S(1)}, u32[]{:S(2)}, u32[]{:S(2)}) collective-permute-start(bf16[16,1536]{1,0:T(8,128)(2,1)} %param.15), channel_id=1, source_target_pairs={{0,16},{4,20},{8,24},{12,28},{16,0},{20,4},{24,8},{28,12},{1,17},{... | collective-permute-start | bytes 147464 | tf_op jit(solution)/shard_map/ppermute | solution.py:183
  4.5 6.2 %collective-permute-start.2 = (bf16[16,1536]{1,0:T(8,128)(2,1)}, bf16[16,1536]{1,0:T(8,128)(2,1)S(1)}, u32[]{:S(2)}, u32[]{:S(2)}) collective-permute-start(bf16[16,1536]{1,0:T(8,128)(2,1)} %param.15), channel_id=1, source_target_pairs={{0,24},{4,28},{8,16},{12,20},{16,8},{20,12},{24,0},{28,4},{1,25},{... | collective-permute-start | bytes 147464 | tf_op jit(solution)/shard_map/ppermute | solution.py:183
  4.5 7.3 %collective-permute-start.3 = (bf16[2,512,128]{2,1,0:T(8,128)(2,1)}, bf16[2,512,128]{2,1,0:T(8,128)(2,1)}, u32[]{:S(2)}, u32[]{:S(2)}) collective-permute-start(bf16[2,512,128]{2,1,0:T(8,128)(2,1)} %param.16), channel_id=1, source_target_pairs={{0,4},{4,0},{8,12},{12,8},{16,20},{20,16},{24,28},{28,24},{1,5},{5... | collective-permute-start | bytes 786440 | tf_op jit(solution)/shard_map/ppermute | solution.py:183
  4.5 7.3 %collective-permute-start.4 = (bf16[2,16,128]{2,1,0:T(8,128)(2,1)}, bf16[2,16,128]{2,1,0:T(8,128)(2,1)S(1)}, u32[]{:S(2)}, u32[]{:S(2)}) collective-permute-start(bf16[2,16,128]{2,1,0:T(8,128)(2,1)} %param.18), channel_id=1, source_target_pairs={{0,4},{4,0},{8,12},{12,8},{16,20},{20,16},{24,28},{28,24},{1,5},{5... | collective-permute-start | bytes 24584 | tf_op jit(solution)/shard_map/ppermute | solution.py:183
  10.1 5.9 %collective-permute-start.5 = (bf16[2,512,128]{2,1,0:T(8,128)(2,1)}, bf16[2,512,128]{2,1,0:T(8,128)(2,1)}, u32[]{:S(2)}, u32[]{:S(2)}) collective-permute-start(bf16[2,512,128]{2,1,0:T(8,128)(2,1)} %param.17), channel_id=1, source_target_pairs={{0,4},{4,0},{8,12},{12,8},{16,20},{20,16},{24,28},{28,24},{1,5},{5... | collective-permute-start | bytes 786440 | tf_op jit(solution)/shard_map/ppermute | solution.py:183
  10.2 5.8 %collective-permute-start.6 = (bf16[2,16,128]{2,1,0:T(8,128)(2,1)}, bf16[2,16,128]{2,1,0:T(8,128)(2,1)S(1)}, u32[]{:S(2)}, u32[]{:S(2)}) collective-permute-start(bf16[2,16,128]{2,1,0:T(8,128)(2,1)} %param.19), channel_id=1, source_target_pairs={{0,4},{4,0},{8,12},{12,8},{16,20},{20,16},{24,28},{28,24},{1,5},{5... | collective-permute-start | bytes 24584 | tf_op jit(solution)/shard_map/ppermute | solution.py:183
  18.9 9.1 %collective-permute-start.9 = (bf16[13,64,128]{2,1,0:T(8,128)(2,1)S(1)}, bf16[13,64,128]{2,1,0:T(8,128)(2,1)S(1)}, u32[]{:S(2)}, u32[]{:S(2)}) collective-permute-start(bf16[13,64,128]{2,1,0:T(8,128)(2,1)S(1)} %pad_maximum_fusion.2), channel_id=1, source_target_pairs={{0,24},{4,28},{8,16},{12,20},{16,8},{20,12},{24,0},{28,4},{1,25},{... | collective-permute-start | bytes 638984 | tf_op jit(solution)/shard_map/ppermute | solution.py:183
  21.8 10.1 %collective-permute-start.8 = (bf16[13,64,128]{2,1,0:T(8,128)(2,1)S(1)}, bf16[13,64,128]{2,1,0:T(8,128)(2,1)S(1)}, u32[]{:S(2)}, u32[]{:S(2)}) collective-permute-start(bf16[13,64,128]{2,1,0:T(8,128)(2,1)S(1)} %pad_maximum_fusion.2), channel_id=1, source_target_pairs={{0,16},{4,20},{8,24},{12,28},{16,0},{20,4},{24,8},{28,12},{1,17},{... | collective-permute-start | bytes 638984 | tf_op jit(solution)/shard_map/ppermute | solution.py:183
  22.3 9.9 %collective-permute-start.7 = (bf16[13,64,128]{2,1,0:T(8,128)(2,1)S(1)}, bf16[13,64,128]{2,1,0:T(8,128)(2,1)S(1)}, u32[]{:S(2)}, u32[]{:S(2)}) collective-permute-start(bf16[13,64,128]{2,1,0:T(8,128)(2,1)S(1)} %pad_maximum_fusion.2), channel_id=1, source_target_pairs={{0,8},{4,12},{8,0},{12,4},{16,24},{20,28},{24,16},{28,20},{1,9},{5... | collective-permute-start | bytes 638984 | tf_op jit(solution)/shard_map/ppermute | solution.py:183
  35.6 4.5 %collective-permute-start.11 = (bf16[32,768]{1,0:T(8,128)(2,1)S(1)}, bf16[32,768]{1,0:T(8,128)(2,1)S(1)}, u32[]{:S(2)}, u32[]{:S(2)}) collective-permute-start(bf16[32,768]{1,0:T(8,128)(2,1)S(1)} %get-tuple-element.16), channel_id=1, source_target_pairs={{0,1},{1,0},{2,3},{3,2},{4,5},{5,4},{6,7},{7,6},{8,9},{9,8},{10,11... | collective-permute-start | bytes 147464 | tf_op jit(solution)/shard_map/ppermute | solution.py:183
  37.4 5.9 %collective-permute-start.12 = (bf16[32,768]{1,0:T(8,128)(2,1)S(1)}, bf16[32,768]{1,0:T(8,128)(2,1)S(1)}, u32[]{:S(2)}, u32[]{:S(2)}) collective-permute-start(bf16[32,768]{1,0:T(8,128)(2,1)S(1)} %get-tuple-element.18), channel_id=1, source_target_pairs={{0,2},{1,3},{2,0},{3,1},{4,6},{5,7},{6,4},{7,5},{8,10},{9,11},{10,... | collective-permute-start | bytes 147464 | tf_op jit(solution)/shard_map/ppermute | solution.py:183
  40.0 5.9 %collective-permute-start.13 = (bf16[32,768]{1,0:T(8,128)(2,1)S(1)}, bf16[32,768]{1,0:T(8,128)(2,1)S(1)}, u32[]{:S(2)}, u32[]{:S(2)}) collective-permute-start(bf16[32,768]{1,0:T(8,128)(2,1)S(1)} %get-tuple-element.17), channel_id=1, source_target_pairs={{0,3},{1,2},{2,1},{3,0},{4,7},{5,6},{6,5},{7,4},{8,11},{9,10},{10,... | collective-permute-start | bytes 147464 | tf_op jit(solution)/shard_map/ppermute | solution.py:183
  45.9 4.6 %collective-permute-start.14 = (bf16[32,768]{1,0:T(8,128)(2,1)S(1)}, bf16[32,768]{1,0:T(8,128)(2,1)S(1)}, u32[]{:S(2)}, u32[]{:S(2)}) collective-permute-start(bf16[32,768]{1,0:T(8,128)(2,1)S(1)} %fusion.49), channel_id=1, source_target_pairs={{0,1},{1,0},{2,3},{3,2},{4,5},{5,4},{6,7},{7,6},{8,9},{9,8},{10,11... | collective-permute-start | bytes 147464 | tf_op jit(solution)/shard_map/ppermute | solution.py:183
  46.0 5.2 %collective-permute-start.15 = (bf16[32,768]{1,0:T(8,128)(2,1)S(1)}, bf16[32,768]{1,0:T(8,128)(2,1)S(1)}, u32[]{:S(2)}, u32[]{:S(2)}) collective-permute-start(bf16[32,768]{1,0:T(8,128)(2,1)S(1)} %fusion.49), channel_id=1, source_target_pairs={{0,2},{1,3},{2,0},{3,1},{4,6},{5,7},{6,4},{7,5},{8,10},{9,11},{10,... | collective-permute-start | bytes 147464 | tf_op jit(solution)/shard_map/ppermute | solution.py:183
  47.6 5.9 %collective-permute-start.16 = (bf16[32,768]{1,0:T(8,128)(2,1)S(1)}, bf16[32,768]{1,0:T(8,128)(2,1)S(1)}, u32[]{:S(2)}, u32[]{:S(2)}) collective-permute-start(bf16[32,768]{1,0:T(8,128)(2,1)S(1)} %fusion.49), channel_id=1, source_target_pairs={{0,3},{1,2},{2,1},{3,0},{4,7},{5,6},{6,5},{7,4},{8,11},{9,10},{10,... | collective-permute-start | bytes 147464 | tf_op jit(solution)/shard_map/ppermute | solution.py:183
  53.7 4.7 %collective-permute-start.17 = (bf16[64,768]{1,0:T(8,128)(2,1)S(1)}, bf16[64,768]{1,0:T(8,128)(2,1)S(1)}, u32[]{:S(2)}, u32[]{:S(2)}) collective-permute-start(bf16[64,768]{1,0:T(8,128)(2,1)S(1)} %get-tuple-element.37), channel_id=1, source_target_pairs={{0,8},{4,12},{8,0},{12,4},{16,24},{20,28},{24,16},{28,20},{1,9},{5... | collective-permute-start | bytes 294920 | tf_op jit(solution)/shard_map/ppermute | solution.py:183
  55.3 4.6 %collective-permute-start.18 = (bf16[64,768]{1,0:T(8,128)(2,1)S(1)}, bf16[64,768]{1,0:T(8,128)(2,1)S(1)}, u32[]{:S(2)}, u32[]{:S(2)}) collective-permute-start(bf16[64,768]{1,0:T(8,128)(2,1)S(1)} %get-tuple-element.36), channel_id=1, source_target_pairs={{0,16},{4,20},{8,24},{12,28},{16,0},{20,4},{24,8},{28,12},{1,17},{... | collective-permute-start | bytes 294920 | tf_op jit(solution)/shard_map/ppermute | solution.py:183
  56.1 5.5 %collective-permute-start.19 = (bf16[64,768]{1,0:T(8,128)(2,1)S(1)}, bf16[64,768]{1,0:T(8,128)(2,1)S(1)}, u32[]{:S(2)}, u32[]{:S(2)}) collective-permute-start(bf16[64,768]{1,0:T(8,128)(2,1)S(1)} %get-tuple-element.35), channel_id=1, source_target_pairs={{0,24},{4,28},{8,16},{12,20},{16,8},{20,12},{24,0},{28,4},{1,25},{... | collective-permute-start | bytes 294920 | tf_op jit(solution)/shard_map/ppermute | solution.py:183
  93.4 5.1 %collective-permute-start.22 = (bf16[64,768]{1,0:T(8,128)(2,1)S(1)}, bf16[64,768]{1,0:T(8,128)(2,1)S(1)}, u32[]{:S(2)}, u32[]{:S(2)}) collective-permute-start(bf16[64,768]{1,0:T(8,128)(2,1)S(1)} %get-tuple-element.15), channel_id=1, source_target_pairs={{0,8},{4,12},{8,0},{12,4},{16,24},{20,28},{24,16},{28,20},{1,9},{5... | collective-permute-start | bytes 294920 | tf_op jit(solution)/shard_map/ppermute | solution.py:183
  94.7 6.9 %collective-permute-start.23 = (bf16[64,768]{1,0:T(8,128)(2,1)S(1)}, bf16[64,768]{1,0:T(8,128)(2,1)S(1)}, u32[]{:S(2)}, u32[]{:S(2)}) collective-permute-start(bf16[64,768]{1,0:T(8,128)(2,1)S(1)} %get-tuple-element.14), channel_id=1, source_target_pairs={{0,16},{4,20},{8,24},{12,28},{16,0},{20,4},{24,8},{28,12},{1,17},{... | collective-permute-start | bytes 294920 | tf_op jit(solution)/shard_map/ppermute | solution.py:183
  95.3 6.4 %collective-permute-start.24 = (bf16[64,768]{1,0:T(8,128)(2,1)S(1)}, bf16[64,768]{1,0:T(8,128)(2,1)S(1)}, u32[]{:S(2)}, u32[]{:S(2)}) collective-permute-start(bf16[64,768]{1,0:T(8,128)(2,1)S(1)} %get-tuple-element.13), channel_id=1, source_target_pairs={{0,24},{4,28},{8,16},{12,20},{16,8},{20,12},{24,0},{28,4},{1,25},{... | collective-permute-start | bytes 294920 | tf_op jit(solution)/shard_map/ppermute | solution.py:183
  102.2 5.4 %collective-permute-start.26 = (bf16[32,768]{1,0:T(8,128)(2,1)S(1)}, bf16[32,768]{1,0:T(8,128)(2,1)S(1)}, u32[]{:S(2)}, u32[]{:S(2)}) collective-permute-start(bf16[32,768]{1,0:T(8,128)(2,1)S(1)} %get-tuple-element.33), channel_id=1, source_target_pairs={{0,2},{1,3},{2,0},{3,1},{4,6},{5,7},{6,4},{7,5},{8,10},{9,11},{10,... | collective-permute-start | bytes 147464 | tf_op jit(solution)/shard_map/ppermute | solution.py:183
  105.5 5.9 %collective-permute-start.27 = (bf16[32,768]{1,0:T(8,128)(2,1)S(1)}, bf16[32,768]{1,0:T(8,128)(2,1)S(1)}, u32[]{:S(2)}, u32[]{:S(2)}) collective-permute-start(bf16[32,768]{1,0:T(8,128)(2,1)S(1)} %get-tuple-element.32), channel_id=1, source_target_pairs={{0,3},{1,2},{2,1},{3,0},{4,7},{5,6},{6,5},{7,4},{8,11},{9,10},{10,... | collective-permute-start | bytes 147464 | tf_op jit(solution)/shard_map/ppermute | solution.py:183
  (15 other events, 149.5 us)

commit v2 on v0

--- a/solution.py
+++ b/solution.py
@@ -1,8 +1,11 @@
+import functools
 import math
 
 import jax
 import jax.numpy as jnp
 from jax import lax
+from jax.experimental import pallas as pl
+from jax.experimental.pallas import tpu as pltpu
 from jax.sharding import PartitionSpec as P
 
 D = 6144
@@ -44,7 +47,7 @@
     return (highest, denom, summed)
 
 
-def on_device(
+def gathered_path(
     queries,
     cache_keys,
     cache_values,
@@ -172,6 +175,543 @@
     return (own_hidden + share).astype(jnp.bfloat16)
 
 
+BF16 = jnp.bfloat16
+F32 = jnp.float32
+VMEM_SPEC = pl.BlockSpec(memory_space=pltpu.VMEM)
+HBM_SPEC = pl.BlockSpec(memory_space=pl.ANY)
+SMALL_MIB = 12
+STAGED = (3, 1)
+RING = 2
+DOWN_RING = 3
+EXPERTS_MIB = 27
+
+
+def swap(array, axis_name, mask):
+    count = lax.axis_size(axis_name)
+    return lax.ppermute(array, axis_name, [(i, i ^ mask) for i in range(count)])
+
+
+def device_call(kernel, name, outs, arrays, scratch=(), flops=0, limit=SMALL_MIB, specs=None):
+    moved = sum(a.size * a.dtype.itemsize for a in arrays if specs is None)
+    return pl.pallas_call(
+        kernel,
+        out_shape=outs,
+        in_specs=specs or [VMEM_SPEC] * len(arrays),
+        out_specs=jax.tree.map(lambda _: VMEM_SPEC, outs),
+        scratch_shapes=list(scratch),
+        compiler_params=pltpu.CompilerParams(vmem_limit_bytes=limit << 20),
+        cost_estimate=pl.CostEstimate(flops=flops, bytes_accessed=moved, transcendentals=0),
+        name=name,
+    )(*arrays)
+
+
+def in_hbm(array):
+    return pltpu.with_memory_space_constraint(array, pltpu.HBM)
+
+
+def in_vmem(array):
+    return pltpu.with_memory_space_constraint(array, pltpu.VMEM)
+
+
+def like(shape, dtype=BF16):
+    return jax.ShapeDtypeStruct(shape, dtype)
+
+
+def expert_at(shape, ctx_at):
+    ctx_count, mp_count = shape
+    mp_index = lax.axis_index("mp")
+    own = lax.div((mp_index * ctx_count + ctx_at) * EXPERTS, ctx_count * mp_count)
+    return own - lax.div(mp_index * EXPERTS, mp_count)
+
+
+def tables_kernel(shape, ids_ref, logits_ref, pick_ref, high_ref, low_ref):
+    mp_index = lax.axis_index("mp")
+    mp_count = shape[1]
+    per_row, capacity, tokens = pick_ref.shape
+    rows = tokens // mp_count
+    first = lax.div(mp_index * EXPERTS, mp_count)
+    lane = lax.broadcasted_iota(jnp.int32, (1, tokens), 1)
+
+    def by_block(values):
+        for bit in range(mp_count.bit_length() - 1):
+            size = rows << bit
+            forward = pltpu.roll(values, size, 1)
+            back = pltpu.roll(values, tokens - size, 1)
+            moved = jnp.where((lane & size) != 0, forward, back)
+            values = jnp.where(((mp_index >> bit) & 1) == 1, moved, values)
+        return values
+
+    logits = logits_ref[...]
+    weights = jnp.exp(logits - jnp.max(logits, axis=0, keepdims=True))
+    weights = weights / jnp.sum(weights, axis=0, keepdims=True)
+    ids = ids_ref[...]
+    earlier = lax.broadcasted_iota(jnp.int32, (tokens, tokens), 0) < lax.broadcasted_iota(
+        jnp.int32, (tokens, tokens), 1
+    )
+    earlier = earlier.astype(F32).astype(BF16)
+    for which in range(per_row):
+        named = (ids == first + which).astype(F32)
+        member = jnp.max(named, axis=0, keepdims=True)
+        weight = jnp.sum(named * weights, axis=0, keepdims=True)
+        slot = jnp.dot(
+            jnp.broadcast_to(member, (8, tokens)).astype(BF16), earlier, preferred_element_type=F32
+        )[0:1]
+        slot = by_block(jnp.where(member > 0, slot, float(capacity)))
+        weight = by_block(weight)
+        taken = lax.broadcasted_iota(jnp.int32, (capacity, tokens), 0) == slot.astype(jnp.int32)
+        pick_ref[which] = jnp.where(taken, 1.0, 0.0).astype(BF16)
+        weight = jnp.where(taken, weight, 0.0)
+        high = weight.astype(BF16)
+        high_ref[which] = high
+        low_ref[which] = (weight - high.astype(F32)).astype(BF16)
+
+
+def attention_kernel(*refs):
+    half = len(refs) - 8 - 1 - 3 - 4 - 1
+    query_refs = refs[:half]
+    sources = refs[half : half + 4]
+    pair_k, pair_v, pair_nk, pair_nv = refs[half + 4 : half + 8]
+    mine_ref, query_buf, key_buf, value_buf = refs[half + 8 : half + 12]
+    held, copy_sem = refs[half + 12 : -1], refs[-1]
+    copies = [
+        pltpu.make_async_copy(source, buf, copy_sem.at[at]) for at, (source, buf) in enumerate(zip(sources, held))
+    ]
+    for at in (2, 0, 3, 1):
+        copies[at].start()
+    own_k, own_v, new_k, new_v = held
+    own = lax.axis_index("ctx")
+    slots, _, head_dim = own_k.shape
+    tok_local = new_k.shape[1]
+    rows = half * tok_local
+    group = query_refs[0].shape[1] // head_dim // slots
+    heads = slots * group
+    factor = math.log2(math.e) / math.sqrt(head_dim)
+    for at, query_ref in enumerate(query_refs):
+        for head in range(heads):
+            start = (head % group) * rows + at * tok_local
+            query_buf[head // group, start : start + tok_local, :] = query_ref[
+                :, head * head_dim : (head + 1) * head_dim
+            ]
+    for copy in copies:
+        copy.wait()
+    for part, (key_ref, value_ref) in enumerate(((new_k, new_v), (pair_nk, pair_nv))):
+        for slot in range(slots):
+            key_buf[slot, part * tok_local : (part + 1) * tok_local, :] = key_ref[slot]
+            value_buf[slot, part * tok_local : (part + 1) * tok_local, :] = value_ref[slot]
+    row = lax.rem(lax.broadcasted_iota(jnp.int32, (group * rows, 1), 0), rows)
+    block = lax.div(row, tok_local)
+    row_tok = (own ^ (2 * block)) * tok_local + row - block * tok_local
+    column = lax.broadcasted_iota(jnp.int32, (1, 2 * tok_local), 1)
+    block = lax.div(column, tok_local)
+    key_tok = (own ^ block) * tok_local + column - block * tok_local
+    seen = key_tok <= row_tok
+    lane = lax.broadcasted_iota(jnp.int32, (rows, head_dim), 1)
+    stats = jnp.zeros((rows, head_dim), F32)
+
+    def product(left, right):
+        return lax.dot_general(left, right, (((1,), (1,)), ((), ())), preferred_element_type=F32)
+
+    for slot in range(slots):
+        query = query_buf[slot]
+        first = product(query, own_k[slot]) * factor
+        second = product(query, pair_k[slot]) * factor
+        third = jnp.where(seen, product(query, key_buf[slot]) * factor, neg_big)
+        top = jnp.maximum(
+            jnp.max(jnp.maximum(first, second), axis=1, keepdims=True),
+            jnp.max(third, axis=1, keepdims=True),
+        )
+        shift = top.astype(BF16).astype(F32)
+        first = jnp.exp2(first - shift)
+        second = jnp.exp2(second - shift)
+        third = jnp.exp2(third - shift)
+        denom = jnp.sum(first + second, axis=1, keepdims=True) + jnp.sum(third, axis=1, keepdims=True)
+        summed = jnp.dot(first.astype(BF16), own_v[slot], preferred_element_type=F32)
+        summed += jnp.dot(second.astype(BF16), pair_v[slot], preferred_element_type=F32)
+        summed += jnp.dot(third.astype(BF16), value_buf[slot], preferred_element_type=F32)
+        summed = summed.astype(BF16)
+        high = denom.astype(BF16).astype(F32)
+        low = denom - high
+        for index in range(group):
+            head = slot * group + index
+            span = slice(index * rows, (index + 1) * rows)
+            mine_ref[head] = summed[span]
+            stats = jnp.where(lane == head, shift[span], stats)
+            stats = jnp.where(lane == heads + head, high[span], stats)
+            stats = jnp.where(lane == 2 * heads + head, low[span], stats)
+    mine_ref[heads] = stats.astype(BF16)
+
+
+def join_kernel(*refs):
+    part_refs, attn_ref = refs[:-1], refs[-1]
+    half = len(part_refs)
+    heads, head_dim = part_refs[0].shape[0] - 1, part_refs[0].shape[2]
+    tok = part_refs[0].shape[1] // half
+    for block in range(half):
+        spans = [slice((k ^ block) * tok, ((k ^ block) + 1) * tok) for k in range(half)]
+        stats = [ref[heads, span, :].astype(F32) for ref, span in zip(part_refs, spans)]
+        highest = functools.reduce(jnp.maximum, stats)
+        lifts = [jnp.exp2(stat - highest) for stat in stats]
+        denoms = [
+            pltpu.roll(stat, head_dim - heads, 1) + pltpu.roll(stat, head_dim - 2 * heads, 1)
+            for stat in stats
+        ]
+        total = sum(lift * denom for lift, denom in zip(lifts, denoms))
+        shares = [lift / total for lift in lifts]
+        for head in range(heads):
+            mixed = sum(
+                share[:, head : head + 1] * ref[head, span, :].astype(F32)
+                for share, ref, span in zip(shares, part_refs, spans)
+            )
+            attn_ref[block * tok : (block + 1) * tok, head * head_dim : (head + 1) * head_dim] = mixed.astype(BF16)
+
+
+def project_kernel(own_ref, pair_ref, weight_ref, kept_ref, *refs):
+    sent_refs, left = refs[:-1], refs[-1]
+    ctx_index, mp_index = lax.axis_index("ctx"), lax.axis_index("mp")
+    mp_count = len(sent_refs) + 1
+    tok = own_ref.shape[0] // mp_count
+    odd = ctx_index & 1
+    pair_at = (ctx_index >> 1) ^ mp_index
+    for k in range(mp_count):
+        source = pl.ds(pl.multiple_of((pair_at ^ k) * tok, tok), tok)
+        left[pl.ds(pl.multiple_of((2 * k + odd) * tok, tok), tok), :] = own_ref[source, :]
+        left[pl.ds(pl.multiple_of((2 * k + 1 - odd) * tok, tok), tok), :] = pair_ref[source, :]
+    projected = jnp.dot(left[...], weight_ref[...], preferred_element_type=F32)
+    kept_ref[...] = projected[: 2 * tok]
+    for k, ref in enumerate(sent_refs, 1):
+        ref[...] = projected[2 * k * tok : 2 * (k + 1) * tok].astype(BF16)
+
+
+def total_kernel(*refs):
+    total = refs[0][...].astype(F32)
+    for ref in refs[1:-1]:
+        total = total + ref[...].astype(F32)
+    refs[-1][...] = total.astype(BF16)
+
+
+def pack_kernel(shape, pick_ref, *refs):
+    mp_count, half = shape[1], shape[0] // 2
+    hidden_refs, out_refs, packed = refs[:mp_count], refs[mp_count:-1], refs[-1]
+    hidden = jnp.concatenate([ref[...] for ref in hidden_refs], axis=0)
+    for which in range(pick_ref.shape[0]):
+        packed[which] = jnp.dot(pick_ref[which], hidden, preferred_element_type=F32).astype(BF16)
+    for k in range(half):
+        out_refs[k][...] = packed[expert_at(shape, lax.axis_index("ctx") ^ (2 * k))]
+
+
+def stage_kernel(first, *refs):
+    gate_hbm, up_hbm = refs[:2]
+    extra = (len(refs) - 5) // 2
+    plain, gate_out, up_out = refs[2 : 2 + extra], refs[2 + extra], refs[3 + extra]
+    plain_out, sem = refs[4 + extra : -1], refs[-1]
+    own = lax.axis_index("ctx")
+    count, deep = gate_out.shape[0], gate_out.shape[1]
+    pairs = list(zip(plain, plain_out))
+    for step in range(count):
+        rows = pl.ds(pl.multiple_of((own ^ (first + step)) * deep, deep), deep)
+        pairs.append((gate_hbm.at[0, rows, :], gate_out.at[step]))
+        pairs.append((up_hbm.at[0, rows, :], up_out.at[step]))
+    copies = [pltpu.make_async_copy(source, target, sem.at[at]) for at, (source, target) in enumerate(pairs)]
+    for copy in copies:
+        copy.start()
+    for copy in copies:
+        copy.wait()
+
+
+def stage(gate_proj, up_proj, deep, first, count, limit, *plain):
+    units = gate_proj.shape[2]
+    return pl.pallas_call(
+        functools.partial(stage_kernel, first),
+        out_shape=(pltpu.VMEM((count, deep, units), BF16),) * 2 + tuple(pltpu.VMEM(a.shape, a.dtype) for a in plain),
+        in_specs=[HBM_SPEC] * (2 + len(plain)),
+        out_specs=(VMEM_SPEC,) * (2 + len(plain)),
+        scratch_shapes=[pltpu.SemaphoreType.DMA((2 * count + len(plain),))],
+        compiler_params=pltpu.CompilerParams(vmem_limit_bytes=limit << 20),
+        cost_estimate=pl.CostEstimate(flops=0, bytes_accessed=4 * count * deep * units, transcendentals=0),
+        name="stage",
+    )(gate_proj, up_proj, *plain)
+
+
+def experts_kernel(early, *refs):
+    early_refs, refs = refs[: 2 * len(early)], refs[2 * len(early) :]
+    count = len(refs) - 4 - 2 - 10
+    row_refs = refs[:count]
+    staged = sum(early)
+    gain_ref, gate_hbm, up_hbm, down_hbm, out_even_ref, out_odd_ref = refs[count : count + 6]
+    (scaled_ref, act_ref, gate_acc, up_acc, out_acc, gate_buf, up_buf, down_buf, gate_sem, down_sem) = refs[count + 6 :]
+    own = lax.axis_index("ctx")
+    half = count // 2
+    deep = row_refs[0].shape[1]
+    ring = gate_buf.shape[0]
+    down_blocks, down_ring, down_rows = act_ref.shape[0], down_buf.shape[0], down_buf.shape[1]
+
+    def gate_copy(step):
+        rows = pl.ds(pl.multiple_of((own ^ step) * deep, deep), deep)
+        slot = lax.rem(step, ring)
+        return (
+            pltpu.make_async_copy(gate_hbm.at[0, rows, :], gate_buf.at[slot], gate_sem.at[0, slot]),
+            pltpu.make_async_copy(up_hbm.at[0, rows, :], up_buf.at[slot], gate_sem.at[1, slot]),
+        )
+
+    def down_copy(step):
+        rows = pl.ds(pl.multiple_of(step * down_rows, down_rows), down_rows)
+        slot = lax.rem(step, down_ring)
+        return pltpu.make_async_copy(down_hbm.at[0, rows, :], down_buf.at[slot], down_sem.at[slot])
+
+    for step in range(staged, min(count, staged + ring)):
+        for copy in gate_copy(jnp.int32(step)):
+            copy.start()
+    squares = jnp.zeros((row_refs[0].shape[0], 1), F32)
+    for step in range(count):
+        wide = row_refs[step][...].astype(F32)
+        squares = squares + jnp.sum(wide * wide, axis=1, keepdims=True)
+        scaled_ref[step] = (wide * gain_ref[own ^ step]).astype(BF16)
+    rms = lax.rsqrt(squares / D + norm_eps)
+    gate_acc[...] = jnp.zeros_like(gate_acc)
+    up_acc[...] = jnp.zeros_like(up_acc)
+
+    begin = 0
+    for at, number in enumerate(early):
+
+        def early_step(step, carry, at=at, begin=begin):
+            rows = scaled_ref[begin + step]
+            gate_acc[...] += jnp.dot(rows, early_refs[2 * at][step], preferred_element_type=F32)
+            up_acc[...] += jnp.dot(rows, early_refs[2 * at + 1][step], preferred_element_type=F32)
+            return carry
+
+        lax.fori_loop(0, number, early_step, 0)
+        begin += number
+
+    def gate_step(step, carry):
+        slot = lax.rem(step, ring)
+        for copy in gate_copy(step):
+            copy.wait()
+        rows = scaled_ref[step]
+        gate_acc[...] += jnp.dot(rows, gate_buf[slot], preferred_element_type=F32)
+        up_acc[...] += jnp.dot(rows, up_buf[slot], preferred_element_type=F32)
+
+        @pl.when(step + ring < count)
+        def _():
+            for copy in gate_copy(step + ring):
+                copy.start()
+
+        @pl.when(step + ring == count)
+        def _():
+            for index in range(down_ring):
+                down_copy(jnp.int32(index)).start()
+
+        return carry
+
+    lax.fori_loop(staged, count, gate_step, 0)
+    gate = rms * gate_acc[...]
+    act = (gate / (1.0 + jnp.exp(-gate)) * (rms * up_acc[...])).astype(BF16)
+    for index in range(down_blocks):
+        act_ref[index] = act[:, index * down_rows : (index + 1) * down_rows]
+    out_acc[...] = jnp.zeros_like(out_acc)
+
+    def down_step(step, carry):
+        down_copy(step).wait()
+        slot = lax.rem(step, down_ring)
+        out_acc[...] += jnp.dot(act_ref[step], down_buf[slot], preferred_element_type=F32)
+
+        @pl.when(step + down_ring < down_blocks)
+        def _():
+            down_copy(step + down_ring).start()
+
+        return carry
+
+    lax.fori_loop(0, down_blocks, down_step, 0)
+    for step in range(count):
+        columns = pl.ds(pl.multiple_of((own ^ step) * deep, deep), deep)
+        (out_even_ref if step % 2 == 0 else out_odd_ref)[step // 2] = out_acc[:, columns].astype(BF16)
+
+
+def run_experts(early, row_blocks, gain, gate_proj, up_proj, down_proj):
+    rows, deep = row_blocks[0].shape
+    count = len(row_blocks)
+    units = gate_proj.shape[2]
+    wide = down_proj.shape[2]
+    ring, down_blocks, down_ring = RING, 8, DOWN_RING
+    weights = 2 * (2 * gate_proj.size + down_proj.size)
+    return pl.pallas_call(
+        functools.partial(experts_kernel, tuple(gate.shape[0] for gate, _ in early)),
+        out_shape=(like((count // 2, rows, deep)),) * 2,
+        in_specs=[VMEM_SPEC] * (2 * len(early) + count + 1) + [HBM_SPEC] * 3,
+        out_specs=(VMEM_SPEC, VMEM_SPEC),
+        scratch_shapes=[
+            pltpu.VMEM((count, rows, deep), BF16),
+            pltpu.VMEM((down_blocks, rows, units // down_blocks), BF16),
+            pltpu.VMEM((rows, units), F32),
+            pltpu.VMEM((rows, units), F32),
+            pltpu.VMEM((rows, wide), F32),
+            pltpu.VMEM((ring, deep, units), BF16),
+            pltpu.VMEM((ring, deep, units), BF16),
+            pltpu.VMEM((down_ring, units // down_blocks, wide), BF16),
+            pltpu.SemaphoreType.DMA((2, ring)),
+            pltpu.SemaphoreType.DMA((down_ring,)),
+        ],
+        compiler_params=pltpu.CompilerParams(vmem_limit_bytes=EXPERTS_MIB << 20),
+        cost_estimate=pl.CostEstimate(flops=rows * weights, bytes_accessed=weights, transcendentals=rows * units),
+        name="experts",
+    )(*[in_vmem(array) for both in early for array in both], *row_blocks, gain, gate_proj, up_proj, down_proj)
+
+
+def pair_total_kernel(even_ref, other_ref, *out_refs):
+    for k, ref in enumerate(out_refs):
+        ref[...] = (even_ref[k].astype(F32) + other_ref[k].astype(F32)).astype(BF16)
+
+
+def combine_kernel(shape, high_ref, low_ref, *refs):
+    half, mp_count = shape[0] // 2, shape[1]
+    piece_refs, kept_ref, sent_refs = refs[:half], refs[half], refs[half + 1 :]
+    pieces = jnp.concatenate([ref[...] for ref in piece_refs], axis=0)
+    experts = [expert_at(shape, lax.axis_index("ctx") ^ (2 * k)) for k in range(half)]
+    total = None
+    for table in (high_ref, low_ref):
+        spread = jnp.concatenate([table[expert] for expert in experts], axis=0)
+        term = lax.dot_general(spread, pieces, (((0,), (0,)), ((), ())), preferred_element_type=F32)
+        total = term if total is None else total + term
+    rows = kept_ref.shape[0]
+    kept_ref[...] = total[:rows]
+    for k, ref in enumerate(sent_refs, 1):
+        ref[...] = total[k * rows : (k + 1) * rows].astype(BF16)
+
+
+def exchange_path(
+    queries,
+    cache_keys,
+    cache_values,
+    new_keys,
+    new_values,
+    out_proj,
+    residual,
+    norm_gain,
+    gate_proj,
+    up_proj,
+    down_proj,
+    expert_ids,
+    route_logits,
+):
+    ctx_count = lax.axis_size("ctx")
+    mp_count = lax.axis_size("mp")
+    shape = (ctx_count, mp_count)
+    gate_hbm, up_hbm, down_hbm = in_hbm(gate_proj), in_hbm(up_proj), in_hbm(down_proj)
+    tok_local = queries.shape[0]
+    tokens = tok_local * ctx_count
+    slot_local, cache_local, head_dim = cache_keys.shape
+    heads = queries.shape[1] // head_dim
+    d_local = out_proj.shape[1]
+    res_rows = residual.shape[0]
+    half = ctx_count // 2
+    rows = half * tok_local
+    capacity = tokens * TOP // 4
+    per_row = max(1, EXPERTS // mp_count)
+
+    blocks = [queries] + [swap(queries, "ctx", 2 * k) for k in range(1, half)]
+    own = [cache_keys, cache_values, new_keys, new_values]
+    pair = [swap(array, "ctx", 1) for array in own]
+    mine = device_call(
+        attention_kernel,
+        "attention",
+        like((heads + 1, rows, head_dim)),
+        [in_vmem(array) for array in blocks] + [in_hbm(array) for array in own] + [in_vmem(array) for array in pair],
+        [
+            pltpu.VMEM((slot_local, heads // slot_local * rows, head_dim), BF16),
+            pltpu.VMEM((slot_local, 2 * tok_local, head_dim), BF16),
+            pltpu.VMEM((slot_local, 2 * tok_local, head_dim), BF16),
+            *[pltpu.VMEM(array.shape, BF16) for array in own],
+            pltpu.SemaphoreType.DMA((4,)),
+        ],
+        flops=8 * heads * rows * (cache_local + tok_local) * head_dim,
+        limit=24,
+        specs=[VMEM_SPEC] * half + [HBM_SPEC] * 4 + [VMEM_SPEC] * 4,
+    )
+    others = [swap(mine, "ctx", 2 * k) for k in range(1, half)]
+    ids, logits, _ = lax.optimization_barrier((expert_ids.T, route_logits.T, mine))
+    pick, high, low = device_call(
+        functools.partial(tables_kernel, shape),
+        "tables",
+        (like((per_row, capacity, tokens)),) * 3,
+        [ids, logits],
+    )
+    gain = norm_gain.astype(F32).reshape(ctx_count, 1, d_local)
+    gate_later, _ = lax.optimization_barrier((gate_proj, mine))
+    gate_a, up_a, out_proj, residual = stage(in_hbm(gate_later), up_hbm, d_local, 0, STAGED[0], 2, in_hbm(out_proj), in_hbm(residual)
+    )
+    pick, high, low, gain, gate_a, up_a, out_proj, residual, *others = lax.optimization_barrier(
+        (pick, high, low, gain, gate_a, up_a, out_proj, residual, *others)
+    )
+    attn = device_call(join_kernel, "join", like((rows, heads * head_dim)), [mine] + others)
+    block = like((res_rows, d_local))
+
+    kept, *sent = device_call(
+        project_kernel,
+        "project",
+        (like((res_rows, d_local), F32),) + (block,) * (mp_count - 1),
+        [attn, swap(attn, "ctx", 1), out_proj],
+        [pltpu.VMEM((tokens, heads * head_dim), BF16)],
+        flops=2 * tokens * heads * head_dim * d_local,
+    )
+    arrived = [swap(array, "mp", k) for k, array in enumerate(sent, 1)]
+    early = [(gate_a, up_a)]
+    if STAGED[1]:
+        gate_later, _ = lax.optimization_barrier((gate_proj, kept))
+        gate_b, up_b = stage(in_hbm(gate_later), up_hbm, d_local, STAGED[0], STAGED[1], 2)
+        gate_b, up_b, *arrived = lax.optimization_barrier((gate_b, up_b, *arrived))
+        early.append((gate_b, up_b))
+    hidden = device_call(total_kernel, "hidden", block, [kept, residual] + arrived)
+
+    everyone = [hidden] + [swap(hidden, "mp", k) for k in range(1, mp_count)]
+    even = device_call(
+        functools.partial(pack_kernel, shape),
+        "pack",
+        (like((capacity, d_local)),) * half,
+        [pick] + everyone,
+        [pltpu.VMEM((per_row, capacity, d_local), BF16)],
+    )
+    even = [even[0]] + [swap(even[k], "ctx", 2 * k) for k in range(1, half)]
+    odd = [swap(array, "ctx", 1) for array in even]
+    out_even, out_odd = run_experts(
+        early,
+        [array for both in zip(even, odd) for array in both],
+        gain,
+        gate_hbm,
+        up_hbm,
+        down_hbm,
+    )
+    pieces = device_call(
+        pair_total_kernel,
+        "pair_total",
+        (like((capacity, d_local)),) * half,
+        [out_even, swap(out_odd, "ctx", 1)],
+    )
+    pieces = [pieces[0]] + [swap(pieces[k], "ctx", 2 * k) for k in range(1, half)]
+    kept, *sent = device_call(
+        functools.partial(combine_kernel, shape),
+        "combine",
+        (like((res_rows, d_local), F32),) + (block,) * (mp_count - 1),
+        [high, low] + pieces,
+    )
+    arrived = [swap(array, "mp", k) for k, array in enumerate(sent, 1)]
+    return device_call(total_kernel, "layer_out", block, [kept, hidden] + arrived)
+
+
+def on_device(*args):
+    queries, cache_keys, out_proj, gate_proj, down_proj = (args[i] for i in (0, 1, 5, 8, 10))
+    ctx_count, mp_count = lax.axis_size("ctx"), lax.axis_size("mp")
+    per_row = max(1, EXPERTS // mp_count)
+    fits = (
+        ctx_count == 2 * mp_count
+        and ctx_count & (ctx_count - 1) == 0
+        and (ctx_count // per_row) % 2 == 0
+        and out_proj.shape[1] % 256 == 0
+        and gate_proj.shape[2] % 2048 == 0
+        and queries.shape[0] % 16 == 0
+        and 3 * (queries.shape[1] // cache_keys.shape[2]) <= cache_keys.shape[2]
+    )
+    return exchange_path(*args) if fits else gathered_path(*args)
+
+
 def solution(mesh):
     placed = (
         P("ctx", "mp"),

time: 235 us -> 96.2 us (0.41)
  waiting for transfers between devices: 156 us -> 26.1 us
  matrix products: 42.9 us -> 0 us
  Pallas kernels: 0 us -> 35.9 us
  starting transfers between devices: 0.35 us -> 30.9 us
  between operations: 13.4 us -> 0.16 us
  blocking collectives: 9.55 us -> 0 us
  other arithmetic: 10 us -> 0.71 us
    all_gather x2 -> x0, waiting for transfers between devices: 63 us -> none  [the longest x1 37.6 us: on_device(): piece = lax.all_gather(key_value, 'ctx', axis=2, tiled=True)]
    reduce_scatter x2 -> x0, waiting for transfers between devices: 58 us -> none  [the longest x1 38.5 us: on_device(): lax.psum_scatter(jnp.concatenate([jnp.where(local == which, part, 0.0) fo...]
    dot_general x7 -> x0, matrix products: 42.9 us -> none  [the longest x1 21.4 us: on_device(): lax.dot_general(down_local, act, (((0,), (1,)), ((), ())), preferred_elem...]
    pallas_call x0 -> x12, Pallas kernels: none -> 35.9 us  [the longest x1 19.5 us: run_experts(): pl.pallas_call(functools.partial(experts_kernel, tuple((gate.shape[0] for...]
    psum x1 -> x0, waiting for transfers between devices: 34.8 us -> none  [on_device(): hidden = lax.psum(projected.astype(jnp.bfloat16), 'mp')]
    ppermute x0 -> x31, starting transfers between devices: none -> 30.9 us  [swap(): return lax.ppermute(array, axis_name, [(i, i ^ mask) for i in range(count)])]
    ppermute x0 -> x31, waiting for transfers between devices: none -> 26.1 us  [swap(): return lax.ppermute(array, axis_name, [(i, i ^ mask) for i in range(count)])]
    all_gather x1 -> x0, blocking collectives: 9.55 us -> none  [on_device(): lax.all_gather(attn, 'ctx', axis=0, tiled=True)]
  transfers between devices with their start and end apart: 5 -> 31, of which waited for: 5 -> 17; matrix products, arithmetic and copies ran while one was open for 1% -> 1% of each run, Pallas kernels for 0% -> 11%
where the time goes in v2:
time: 96.2 us; the launch traced here: 95.9 us
  Pallas kernels  35.9 us (37%)
  starting transfers between devices  30.9 us (32%)
  waiting for transfers between devices  26.1 us (27%)
  local copies, waits for them, and re-layouts  2.15 us (2%)
    ppermute x31, starting transfers between devices, swap(): return lax.ppermute(array, axis_name, [(i, i ^ mask) for i in range(count)])  30.9 us
    ppermute x31, waiting for transfers between devices, swap(): return lax.ppermute(array, axis_name, [(i, i ^ mask) for i in range(count)])  26.1 us
    pallas_call x1, Pallas kernels, run_experts(): pl.pallas_call(functools.partial(experts_kernel, tuple((gate.shape[0] for...  19.5 us
    pallas_call x2, Pallas kernels, stage(): pl.pallas_call(functools.partial(stage_kernel, first), out_shape=(pltpu.V...  10.1 us
    pallas_call x9, Pallas kernels, device_call(): pl.pallas_call(kernel, out_shape=outs, in_specs=specs or [VMEM_SPEC] * le...  6.35 us
    unnamed x6, local copies, waits for them, and re-layouts  2.15 us
  transfers between devices with their start and end apart: 31, of which 17 were waited for; matrix products, arithmetic and copies ran while one was open for 1% of the time, Pallas kernels for 11%

profile of v2, /device:TPU:0, one launch (start us, length us, event | category | flops | bytes accessed | tf_op | source)
XLA Modules:
  0.0 95.9 jit_solution(16215735795894635874)
XLA Ops:
  1.0 3.0 %collective-permute-start.1 = (bf16[16,1536]{1,0:T(8,128)(2,1)}, bf16[16,1536]{1,0:T(8,128)(2,1)S(1)}, u32[]{:S(2)}, u32[]{:S(2)}) collective-permute-start(bf16[16,1536]{1,0:T(8,128)(2,1)} %refs_0_.1), channel_id=1, source_target_pairs={{0,16},{4,20},{8,24},{12,28},{16,0},{20,4},{24,8},{28,12},{1,17},{... | collective-permute-start | bytes 147464 | tf_op jit(solution)/shard_map/ppermute | solution.py:191
  4.0 1.5 %collective-permute-start = (bf16[16,1536]{1,0:T(8,128)(2,1)}, bf16[16,1536]{1,0:T(8,128)(2,1)S(1)}, u32[]{:S(2)}, u32[]{:S(2)}) collective-permute-start(bf16[16,1536]{1,0:T(8,128)(2,1)} %refs_0_.1), channel_id=1, source_target_pairs={{0,8},{4,12},{8,0},{12,4},{16,24},{20,28},{24,16},{28,20},{1,9},{5... | collective-permute-start | bytes 147464 | tf_op jit(solution)/shard_map/ppermute | solution.py:191
  6.6 1.7 %collective-permute-done.refs_1_ = bf16[16,1536]{1,0:T(8,128)(2,1)S(1)} collective-permute-done((bf16[16,1536]{1,0:T(8,128)(2,1)}, bf16[16,1536]{1,0:T(8,128)(2,1)S(1)}, u32[]{:S(2)}, u32[]{:S(2)}) %collective-permute-start) | collective-permute-done | bytes 49184 | tf_op jit(solution)/shard_map/ppermute | solution.py:191
  8.3 2.4 %collective-permute-done.2.refs_3_ = bf16[16,1536]{1,0:T(8,128)(2,1)S(1)} collective-permute-done((bf16[16,1536]{1,0:T(8,128)(2,1)}, bf16[16,1536]{1,0:T(8,128)(2,1)S(1)}, u32[]{:S(2)}, u32[]{:S(2)}) %collective-permute-start.2) | collective-permute-done | bytes 49184 | tf_op jit(solution)/shard_map/ppermute | solution.py:191
  11.5 3.2 %attention.1.refs_0_ = bf16[13,64,128]{2,1,0:T(8,128)(2,1)S(1)} custom-call(bf16[16,1536]{1,0:T(8,128)(2,1)S(1)} %copy-done.2, bf16[16,1536]{1,0:T(8,128)(2,1)S(1)} %collective-permute-done.refs_1_, bf16[16,1536]{1,0:T(8,128)(2,1)S(1)} %collective-permute-done.1.refs_2_, bf16[16,1536]{1,0:T(8,128)(2,1)S(1)} %collective-permute-done.2.refs_3_, ...), custom_call_target="tpu_custom_call" | custom-call | flops 415236096 | tf_op jit(solution)/shard_map/attention/pallas_call | solution.py:196
  16.7 1.5 %collective-permute-start.7 = (bf16[13,64,128]{2,1,0:T(8,128)(2,1)S(1)}, bf16[13,64,128]{2,1,0:T(8,128)(2,1)S(1)}, u32[]{:S(2)}, u32[]{:S(2)}) collective-permute-start(bf16[13,64,128]{2,1,0:T(8,128)(2,1)S(1)} %attention.1.refs_0_), channel_id=1, source_target_pairs={{0,8},{4,12},{8,0},{12,4},{16,24},{20,28},{24,16},{28,20},{1,9},{5... | collective-permute-start | bytes 638984 | tf_op jit(solution)/shard_map/ppermute | solution.py:191
  20.6 7.2 %stage.2 = (bf16[3,768,2048]{2,1,0:T(8,128)(2,1)S(1)}, bf16[3,768,2048]{2,1,0:T(8,128)(2,1)S(1)}, bf16[1536,768]{1,0:T(8,128)(2,1)S(1)}, bf16[32,768]{1,0:T(8,128)(2,1)S(1)}) custom-call(bf16[1,6144,2048]{2,1,0:T(8,128)(2,1)} %refs_13_.1, bf16[1,6144,2048]{2,1,0:T(8,128)(2,1)} %refs_14_.1, bf16[1536,768]{1,0:T(8,128)(2,1)} %refs_2_.1, bf16[32,768]{1,0:T(8,128)(2,1)} %refs_3_.1), custom_call_target="tpu_custom_call" | custom-call | bytes 18874368 | tf_op jit(solution)/shard_map/stage/pallas_call | solution.py:423
  29.0 1.4 %collective-permute-done.10.pair_ref = bf16[64,1536]{1,0:T(8,128)(2,1)S(1)} collective-permute-done((bf16[64,1536]{1,0:T(8,128)(2,1)S(1)}, bf16[64,1536]{1,0:T(8,128)(2,1)S(1)}, u32[]{:S(2)}, u32[]{:S(2)}) %collective-permute-start.10) | collective-permute-done | bytes 196640 | tf_op jit(solution)/shard_map/ppermute | solution.py:191
  30.9 1.6 %collective-permute-start.11 = (bf16[32,768]{1,0:T(8,128)(2,1)S(1)}, bf16[32,768]{1,0:T(8,128)(2,1)S(1)}, u32[]{:S(2)}, u32[]{:S(2)}) collective-permute-start(bf16[32,768]{1,0:T(8,128)(2,1)S(1)} %get-tuple-element.74), channel_id=1, source_target_pairs={{0,1},{1,0},{2,3},{3,2},{4,5},{5,4},{6,7},{7,6},{8,9},{9,8},{10,11... | collective-permute-start | bytes 147464 | tf_op jit(solution)/shard_map/ppermute | solution.py:191
  32.6 2.6 %collective-permute-start.12 = (bf16[32,768]{1,0:T(8,128)(2,1)S(1)}, bf16[32,768]{1,0:T(8,128)(2,1)S(1)}, u32[]{:S(2)}, u32[]{:S(2)}) collective-permute-start(bf16[32,768]{1,0:T(8,128)(2,1)S(1)} %get-tuple-element.75), channel_id=1, source_target_pairs={{0,2},{1,3},{2,0},{3,1},{4,6},{5,7},{6,4},{7,5},{8,10},{9,11},{10,... | collective-permute-start | bytes 147464 | tf_op jit(solution)/shard_map/ppermute | solution.py:191
  35.4 2.9 %stage.3 = (bf16[1,768,2048]{2,1,0:T(8,128)(2,1)S(1)}, bf16[1,768,2048]{2,1,0:T(8,128)(2,1)S(1)}) custom-call(bf16[1,6144,2048]{2,1,0:T(8,128)(2,1)} %refs_13_.1, bf16[1,6144,2048]{2,1,0:T(8,128)(2,1)} %refs_14_.1), custom_call_target="tpu_custom_call" | custom-call | bytes 6291456 | tf_op jit(solution)/shard_map/stage/pallas_call | solution.py:423
  38.5 2.6 %collective-permute-done.13.refs_4_ = bf16[32,768]{1,0:T(8,128)(2,1)S(1)} collective-permute-done((bf16[32,768]{1,0:T(8,128)(2,1)S(1)}, bf16[32,768]{1,0:T(8,128)(2,1)S(1)}, u32[]{:S(2)}, u32[]{:S(2)}) %collective-permute-start.13) | collective-permute-done | bytes 49184 | tf_op jit(solution)/shard_map/ppermute | solution.py:191
  42.2 3.3 %collective-permute-start.14 = (bf16[32,768]{1,0:T(8,128)(2,1)S(1)}, bf16[32,768]{1,0:T(8,128)(2,1)S(1)}, u32[]{:S(2)}, u32[]{:S(2)}) collective-permute-start(bf16[32,768]{1,0:T(8,128)(2,1)S(1)} %hidden.1.refs_0_.refs_1_), channel_id=1, source_target_pairs={{0,1},{1,0},{2,3},{3,2},{4,5},{5,4},{6,7},{7,6},{8,9},{9,8},{10,11... | collective-permute-start | bytes 147464 | tf_op jit(solution)/shard_map/ppermute | solution.py:191
  45.5 1.5 %collective-permute-done.16.refs_3_ = bf16[32,768]{1,0:T(8,128)(2,1)S(1)} collective-permute-done((bf16[32,768]{1,0:T(8,128)(2,1)S(1)}, bf16[32,768]{1,0:T(8,128)(2,1)S(1)}, u32[]{:S(2)}, u32[]{:S(2)}) %collective-permute-start.16) | collective-permute-done | bytes 49184 | tf_op jit(solution)/shard_map/ppermute | solution.py:191
  50.0 1.8 %collective-permute-start.22 = (bf16[64,768]{1,0:T(8,128)(2,1)S(1)}, bf16[64,768]{1,0:T(8,128)(2,1)S(1)}, u32[]{:S(2)}, u32[]{:S(2)}) collective-permute-start(bf16[64,768]{1,0:T(8,128)(2,1)S(1)} %get-tuple-element.87), channel_id=1, source_target_pairs={{0,24},{4,28},{8,16},{12,20},{16,8},{20,12},{24,0},{28,4},{1,25},{... | collective-permute-start | bytes 294920 | tf_op jit(solution)/shard_map/ppermute | solution.py:191
  53.6 2.0 %collective-permute-done.22.refs_10_ = bf16[64,768]{1,0:T(8,128)(2,1)S(1)} collective-permute-done((bf16[64,768]{1,0:T(8,128)(2,1)S(1)}, bf16[64,768]{1,0:T(8,128)(2,1)S(1)}, u32[]{:S(2)}, u32[]{:S(2)}) %collective-permute-start.22) | collective-permute-done | bytes 98336 | tf_op jit(solution)/shard_map/ppermute | solution.py:191
  56.9 19.5 %experts.1 = (bf16[4,64,768]{2,1,0:T(8,128)(2,1)S(1)}, bf16[4,64,768]{2,1,0:T(8,128)(2,1)S(1)}) custom-call(bf16[3,768,2048]{2,1,0:T(8,128)(2,1)S(1)} %get-tuple-element.64.refs_0_, bf16[3,768,2048]{2,1,0:T(8,128)(2,1)S(1)} %get-tuple-element.65.refs_1_, bf16[1,768,2048]{2,1,0:T(8,128)(2,1)S(1)} %get-tuple-element.77.refs_2_, ...), custom_call_target="tpu_custom_call" | custom-call | flops 4831838208 | bytes 75497472 | tf_op jit(solution)/shard_map/experts/pallas_call | solution.py:536
  76.6 1.6 %collective-permute-done.24.other_ref = bf16[4,64,768]{2,1,0:T(8,128)(2,1)S(1)} collective-permute-done((bf16[4,64,768]{2,1,0:T(8,128)(2,1)S(1)}, bf16[4,64,768]{2,1,0:T(8,128)(2,1)S(1)}, u32[]{:S(2)}, u32[]{:S(2)}) %collective-permute-start.24) | collective-permute-done | bytes 393248 | tf_op jit(solution)/shard_map/ppermute | solution.py:191
  78.3 1.6 %collective-permute-start.25 = (bf16[64,768]{1,0:T(8,128)(2,1)S(1)}, bf16[64,768]{1,0:T(8,128)(2,1)S(1)}, u32[]{:S(2)}, u32[]{:S(2)}) collective-permute-start(bf16[64,768]{1,0:T(8,128)(2,1)S(1)} %get-tuple-element.92), channel_id=1, source_target_pairs={{0,8},{4,12},{8,0},{12,4},{16,24},{20,28},{24,16},{28,20},{1,9},{5... | collective-permute-start | bytes 294920 | tf_op jit(solution)/shard_map/ppermute | solution.py:191
  81.8 1.4 %collective-permute-done.25.refs_1_ = bf16[64,768]{1,0:T(8,128)(2,1)S(1)} collective-permute-done((bf16[64,768]{1,0:T(8,128)(2,1)S(1)}, bf16[64,768]{1,0:T(8,128)(2,1)S(1)}, u32[]{:S(2)}, u32[]{:S(2)}) %collective-permute-start.25) | collective-permute-done | bytes 98336 | tf_op jit(solution)/shard_map/ppermute | solution.py:191
  83.2 3.4 %collective-permute-done.26.refs_2_ = bf16[64,768]{1,0:T(8,128)(2,1)S(1)} collective-permute-done((bf16[64,768]{1,0:T(8,128)(2,1)S(1)}, bf16[64,768]{1,0:T(8,128)(2,1)S(1)}, u32[]{:S(2)}, u32[]{:S(2)}) %collective-permute-start.26) | collective-permute-done | bytes 98336 | tf_op jit(solution)/shard_map/ppermute | solution.py:191
  86.9 1.6 %collective-permute-start.28 = (bf16[32,768]{1,0:T(8,128)(2,1)S(1)}, bf16[32,768]{1,0:T(8,128)(2,1)S(1)}, u32[]{:S(2)}, u32[]{:S(2)}) collective-permute-start(bf16[32,768]{1,0:T(8,128)(2,1)S(1)} %get-tuple-element.96), channel_id=1, source_target_pairs={{0,1},{1,0},{2,3},{3,2},{4,5},{5,4},{6,7},{7,6},{8,9},{9,8},{10,11... | collective-permute-start | bytes 147464 | tf_op jit(solution)/shard_map/ppermute | solution.py:191
  89.4 2.0 %collective-permute-start.30 = (bf16[32,768]{1,0:T(8,128)(2,1)S(1)}, bf16[32,768]{1,0:T(8,128)(2,1)S(1)}, u32[]{:S(2)}, u32[]{:S(2)}) collective-permute-start(bf16[32,768]{1,0:T(8,128)(2,1)S(1)} %get-tuple-element.98), channel_id=1, source_target_pairs={{0,3},{1,2},{2,1},{3,0},{4,7},{5,6},{6,5},{7,4},{8,11},{9,10},{10,... | collective-permute-start | bytes 147464 | tf_op jit(solution)/shard_map/ppermute | solution.py:191
  91.5 2.5 %collective-permute-done.29.refs_3_ = bf16[32,768]{1,0:T(8,128)(2,1)S(1)} collective-permute-done((bf16[32,768]{1,0:T(8,128)(2,1)S(1)}, bf16[32,768]{1,0:T(8,128)(2,1)S(1)}, u32[]{:S(2)}, u32[]{:S(2)}) %collective-permute-start.29) | collective-permute-done | bytes 49184 | tf_op jit(solution)/shard_map/ppermute | solution.py:191
  (57 shorter events, 22.1 us)
Async XLA Ops:
  0.0 10.7 %collective-permute-start.3 = (bf16[2,512,128]{2,1,0:T(8,128)(2,1)}, bf16[2,512,128]{2,1,0:T(8,128)(2,1)S(1)}, u32[]{:S(2)}, u32[]{:S(2)}) collective-permute-start(bf16[2,512,128]{2,1,0:T(8,128)(2,1)} %refs_4_.1), channel_id=1, source_target_pairs={{0,4},{4,0},{8,12},{12,8},{16,20},{20,16},{24,28},{28,24},{1,5},{5... | collective-permute-start | bytes 786440 | tf_op jit(solution)/shard_map/ppermute | solution.py:191
  0.5 10.2 %collective-permute-start.4 = (bf16[2,512,128]{2,1,0:T(8,128)(2,1)}, bf16[2,512,128]{2,1,0:T(8,128)(2,1)S(1)}, u32[]{:S(2)}, u32[]{:S(2)}) collective-permute-start(bf16[2,512,128]{2,1,0:T(8,128)(2,1)} %refs_5_.1), channel_id=1, source_target_pairs={{0,4},{4,0},{8,12},{12,8},{16,20},{20,16},{24,28},{28,24},{1,5},{5... | collective-permute-start | bytes 786440 | tf_op jit(solution)/shard_map/ppermute | solution.py:191
  1.0 4.5 %collective-permute-start.6 = (bf16[2,16,128]{2,1,0:T(8,128)(2,1)}, bf16[2,16,128]{2,1,0:T(8,128)(2,1)S(1)}, u32[]{:S(2)}, u32[]{:S(2)}) collective-permute-start(bf16[2,16,128]{2,1,0:T(8,128)(2,1)} %refs_7_.1), channel_id=1, source_target_pairs={{0,4},{4,0},{8,12},{12,8},{16,20},{20,16},{24,28},{28,24},{1,5},{5... | collective-permute-start | bytes 24584 | tf_op jit(solution)/shard_map/ppermute | solution.py:191
  1.0 5.5 %collective-permute-start.1 = (bf16[16,1536]{1,0:T(8,128)(2,1)}, bf16[16,1536]{1,0:T(8,128)(2,1)S(1)}, u32[]{:S(2)}, u32[]{:S(2)}) collective-permute-start(bf16[16,1536]{1,0:T(8,128)(2,1)} %refs_0_.1), channel_id=1, source_target_pairs={{0,16},{4,20},{8,24},{12,28},{16,0},{20,4},{24,8},{28,12},{1,17},{... | collective-permute-start | bytes 147464 | tf_op jit(solution)/shard_map/ppermute | solution.py:191
  4.0 4.3 %collective-permute-start = (bf16[16,1536]{1,0:T(8,128)(2,1)}, bf16[16,1536]{1,0:T(8,128)(2,1)S(1)}, u32[]{:S(2)}, u32[]{:S(2)}) collective-permute-start(bf16[16,1536]{1,0:T(8,128)(2,1)} %refs_0_.1), channel_id=1, source_target_pairs={{0,8},{4,12},{8,0},{12,4},{16,24},{20,28},{24,16},{28,20},{1,9},{5... | collective-permute-start | bytes 147464 | tf_op jit(solution)/shard_map/ppermute | solution.py:191
  5.5 5.2 %collective-permute-start.2 = (bf16[16,1536]{1,0:T(8,128)(2,1)}, bf16[16,1536]{1,0:T(8,128)(2,1)S(1)}, u32[]{:S(2)}, u32[]{:S(2)}) collective-permute-start(bf16[16,1536]{1,0:T(8,128)(2,1)} %refs_0_.1), channel_id=1, source_target_pairs={{0,24},{4,28},{8,16},{12,20},{16,8},{20,12},{24,0},{28,4},{1,25},{... | collective-permute-start | bytes 147464 | tf_op jit(solution)/shard_map/ppermute | solution.py:191
  14.7 13.1 %collective-permute-start.9 = (bf16[13,64,128]{2,1,0:T(8,128)(2,1)S(1)}, bf16[13,64,128]{2,1,0:T(8,128)(2,1)S(1)}, u32[]{:S(2)}, u32[]{:S(2)}) collective-permute-start(bf16[13,64,128]{2,1,0:T(8,128)(2,1)S(1)} %attention.1.refs_0_), channel_id=1, source_target_pairs={{0,24},{4,28},{8,16},{12,20},{16,8},{20,12},{24,0},{28,4},{1,25},{... | collective-permute-start | bytes 638984 | tf_op jit(solution)/shard_map/ppermute | solution.py:191
  15.8 12.0 %collective-permute-start.8 = (bf16[13,64,128]{2,1,0:T(8,128)(2,1)S(1)}, bf16[13,64,128]{2,1,0:T(8,128)(2,1)S(1)}, u32[]{:S(2)}, u32[]{:S(2)}) collective-permute-start(bf16[13,64,128]{2,1,0:T(8,128)(2,1)S(1)} %attention.1.refs_0_), channel_id=1, source_target_pairs={{0,16},{4,20},{8,24},{12,28},{16,0},{20,4},{24,8},{28,12},{1,17},{... | collective-permute-start | bytes 638984 | tf_op jit(solution)/shard_map/ppermute | solution.py:191
  16.7 11.1 %collective-permute-start.7 = (bf16[13,64,128]{2,1,0:T(8,128)(2,1)S(1)}, bf16[13,64,128]{2,1,0:T(8,128)(2,1)S(1)}, u32[]{:S(2)}, u32[]{:S(2)}) collective-permute-start(bf16[13,64,128]{2,1,0:T(8,128)(2,1)S(1)} %attention.1.refs_0_), channel_id=1, source_target_pairs={{0,8},{4,12},{8,0},{12,4},{16,24},{20,28},{24,16},{28,20},{1,9},{5... | collective-permute-start | bytes 638984 | tf_op jit(solution)/shard_map/ppermute | solution.py:191
  30.9 7.3 %collective-permute-start.11 = (bf16[32,768]{1,0:T(8,128)(2,1)S(1)}, bf16[32,768]{1,0:T(8,128)(2,1)S(1)}, u32[]{:S(2)}, u32[]{:S(2)}) collective-permute-start(bf16[32,768]{1,0:T(8,128)(2,1)S(1)} %get-tuple-element.74), channel_id=1, source_target_pairs={{0,1},{1,0},{2,3},{3,2},{4,5},{5,4},{6,7},{7,6},{8,9},{9,8},{10,11... | collective-permute-start | bytes 147464 | tf_op jit(solution)/shard_map/ppermute | solution.py:191
  32.6 5.9 %collective-permute-start.12 = (bf16[32,768]{1,0:T(8,128)(2,1)S(1)}, bf16[32,768]{1,0:T(8,128)(2,1)S(1)}, u32[]{:S(2)}, u32[]{:S(2)}) collective-permute-start(bf16[32,768]{1,0:T(8,128)(2,1)S(1)} %get-tuple-element.75), channel_id=1, source_target_pairs={{0,2},{1,3},{2,0},{3,1},{4,6},{5,7},{6,4},{7,5},{8,10},{9,11},{10,... | collective-permute-start | bytes 147464 | tf_op jit(solution)/shard_map/ppermute | solution.py:191
  35.2 5.9 %collective-permute-start.13 = (bf16[32,768]{1,0:T(8,128)(2,1)S(1)}, bf16[32,768]{1,0:T(8,128)(2,1)S(1)}, u32[]{:S(2)}, u32[]{:S(2)}) collective-permute-start(bf16[32,768]{1,0:T(8,128)(2,1)S(1)} %get-tuple-element.76), channel_id=1, source_target_pairs={{0,3},{1,2},{2,1},{3,0},{4,7},{5,6},{6,5},{7,4},{8,11},{9,10},{10,... | collective-permute-start | bytes 147464 | tf_op jit(solution)/shard_map/ppermute | solution.py:191
  41.1 6.0 %collective-permute-start.16 = (bf16[32,768]{1,0:T(8,128)(2,1)S(1)}, bf16[32,768]{1,0:T(8,128)(2,1)S(1)}, u32[]{:S(2)}, u32[]{:S(2)}) collective-permute-start(bf16[32,768]{1,0:T(8,128)(2,1)S(1)} %hidden.1.refs_0_.refs_1_), channel_id=1, source_target_pairs={{0,3},{1,2},{2,1},{3,0},{4,7},{5,6},{6,5},{7,4},{8,11},{9,10},{10,... | collective-permute-start | bytes 147464 | tf_op jit(solution)/shard_map/ppermute | solution.py:191
  42.2 5.9 %collective-permute-start.15 = (bf16[32,768]{1,0:T(8,128)(2,1)S(1)}, bf16[32,768]{1,0:T(8,128)(2,1)S(1)}, u32[]{:S(2)}, u32[]{:S(2)}) collective-permute-start(bf16[32,768]{1,0:T(8,128)(2,1)S(1)} %hidden.1.refs_0_.refs_1_), channel_id=1, source_target_pairs={{0,2},{1,3},{2,0},{3,1},{4,6},{5,7},{6,4},{7,5},{8,10},{9,11},{10,... | collective-permute-start | bytes 147464 | tf_op jit(solution)/shard_map/ppermute | solution.py:191
  42.2 5.9 %collective-permute-start.14 = (bf16[32,768]{1,0:T(8,128)(2,1)S(1)}, bf16[32,768]{1,0:T(8,128)(2,1)S(1)}, u32[]{:S(2)}, u32[]{:S(2)}) collective-permute-start(bf16[32,768]{1,0:T(8,128)(2,1)S(1)} %hidden.1.refs_0_.refs_1_), channel_id=1, source_target_pairs={{0,1},{1,0},{2,3},{3,2},{4,5},{5,4},{6,7},{7,6},{8,9},{9,8},{10,11... | collective-permute-start | bytes 147464 | tf_op jit(solution)/shard_map/ppermute | solution.py:191
  48.3 4.7 %collective-permute-start.18 = (bf16[64,768]{1,0:T(8,128)(2,1)S(1)}, bf16[64,768]{1,0:T(8,128)(2,1)S(1)}, u32[]{:S(2)}, u32[]{:S(2)}) collective-permute-start(bf16[64,768]{1,0:T(8,128)(2,1)S(1)} %get-tuple-element.85), channel_id=1, source_target_pairs={{0,8},{4,12},{8,0},{12,4},{16,24},{20,28},{24,16},{28,20},{1,9},{5... | collective-permute-start | bytes 294920 | tf_op jit(solution)/shard_map/ppermute | solution.py:191
  48.9 4.6 %collective-permute-start.20 = (bf16[64,768]{1,0:T(8,128)(2,1)S(1)}, bf16[64,768]{1,0:T(8,128)(2,1)S(1)}, u32[]{:S(2)}, u32[]{:S(2)}) collective-permute-start(bf16[64,768]{1,0:T(8,128)(2,1)S(1)} %get-tuple-element.86), channel_id=1, source_target_pairs={{0,16},{4,20},{8,24},{12,28},{16,0},{20,4},{24,8},{28,12},{1,17},{... | collective-permute-start | bytes 294920 | tf_op jit(solution)/shard_map/ppermute | solution.py:191
  50.0 5.5 %collective-permute-start.22 = (bf16[64,768]{1,0:T(8,128)(2,1)S(1)}, bf16[64,768]{1,0:T(8,128)(2,1)S(1)}, u32[]{:S(2)}, u32[]{:S(2)}) collective-permute-start(bf16[64,768]{1,0:T(8,128)(2,1)S(1)} %get-tuple-element.87), channel_id=1, source_target_pairs={{0,24},{4,28},{8,16},{12,20},{16,8},{20,12},{24,0},{28,4},{1,25},{... | collective-permute-start | bytes 294920 | tf_op jit(solution)/shard_map/ppermute | solution.py:191
  78.3 4.9 %collective-permute-start.25 = (bf16[64,768]{1,0:T(8,128)(2,1)S(1)}, bf16[64,768]{1,0:T(8,128)(2,1)S(1)}, u32[]{:S(2)}, u32[]{:S(2)}) collective-permute-start(bf16[64,768]{1,0:T(8,128)(2,1)S(1)} %get-tuple-element.92), channel_id=1, source_target_pairs={{0,8},{4,12},{8,0},{12,4},{16,24},{20,28},{24,16},{28,20},{1,9},{5... | collective-permute-start | bytes 294920 | tf_op jit(solution)/shard_map/ppermute | solution.py:191
  79.8 6.7 %collective-permute-start.26 = (bf16[64,768]{1,0:T(8,128)(2,1)S(1)}, bf16[64,768]{1,0:T(8,128)(2,1)S(1)}, u32[]{:S(2)}, u32[]{:S(2)}) collective-permute-start(bf16[64,768]{1,0:T(8,128)(2,1)S(1)} %get-tuple-element.93), channel_id=1, source_target_pairs={{0,16},{4,20},{8,24},{12,28},{16,0},{20,4},{24,8},{28,12},{1,17},{... | collective-permute-start | bytes 294920 | tf_op jit(solution)/shard_map/ppermute | solution.py:191
  80.8 5.8 %collective-permute-start.27 = (bf16[64,768]{1,0:T(8,128)(2,1)S(1)}, bf16[64,768]{1,0:T(8,128)(2,1)S(1)}, u32[]{:S(2)}, u32[]{:S(2)}) collective-permute-start(bf16[64,768]{1,0:T(8,128)(2,1)S(1)} %get-tuple-element.94), channel_id=1, source_target_pairs={{0,24},{4,28},{8,16},{12,20},{16,8},{20,12},{24,0},{28,4},{1,25},{... | collective-permute-start | bytes 294920 | tf_op jit(solution)/shard_map/ppermute | solution.py:191
  86.9 4.6 %collective-permute-start.28 = (bf16[32,768]{1,0:T(8,128)(2,1)S(1)}, bf16[32,768]{1,0:T(8,128)(2,1)S(1)}, u32[]{:S(2)}, u32[]{:S(2)}) collective-permute-start(bf16[32,768]{1,0:T(8,128)(2,1)S(1)} %get-tuple-element.96), channel_id=1, source_target_pairs={{0,1},{1,0},{2,3},{3,2},{4,5},{5,4},{6,7},{7,6},{8,9},{9,8},{10,11... | collective-permute-start | bytes 147464 | tf_op jit(solution)/shard_map/ppermute | solution.py:191
  88.5 5.5 %collective-permute-start.29 = (bf16[32,768]{1,0:T(8,128)(2,1)S(1)}, bf16[32,768]{1,0:T(8,128)(2,1)S(1)}, u32[]{:S(2)}, u32[]{:S(2)}) collective-permute-start(bf16[32,768]{1,0:T(8,128)(2,1)S(1)} %get-tuple-element.97), channel_id=1, source_target_pairs={{0,2},{1,3},{2,0},{3,1},{4,6},{5,7},{6,4},{7,5},{8,10},{9,11},{10,... | collective-permute-start | bytes 147464 | tf_op jit(solution)/shard_map/ppermute | solution.py:191
  89.4 5.9 %collective-permute-start.30 = (bf16[32,768]{1,0:T(8,128)(2,1)S(1)}, bf16[32,768]{1,0:T(8,128)(2,1)S(1)}, u32[]{:S(2)}, u32[]{:S(2)}) collective-permute-start(bf16[32,768]{1,0:T(8,128)(2,1)S(1)} %get-tuple-element.98), channel_id=1, source_target_pairs={{0,3},{1,2},{2,1},{3,0},{4,7},{5,6},{6,5},{7,4},{8,11},{9,10},{10,... | collective-permute-start | bytes 147464 | tf_op jit(solution)/shard_map/ppermute | solution.py:191
  (10 other events, 18.5 us)

commit v3 on v2

--- a/solution.py
+++ b/solution.py
@@ -180,9 +180,9 @@
 VMEM_SPEC = pl.BlockSpec(memory_space=pltpu.VMEM)
 HBM_SPEC = pl.BlockSpec(memory_space=pl.ANY)
 SMALL_MIB = 12
-STAGED = (3, 1)
-RING = 2
-DOWN_RING = 3
+STAGE_AT = ((0, 1, 2), (3, 4), (5,), ())
+GATE_RING = 2
+DOWN_RING = 4
 EXPERTS_MIB = 27
 
 
@@ -191,8 +191,14 @@
     return lax.ppermute(array, axis_name, [(i, i ^ mask) for i in range(count)])
 
 
-def device_call(kernel, name, outs, arrays, scratch=(), flops=0, limit=SMALL_MIB, specs=None):
-    moved = sum(a.size * a.dtype.itemsize for a in arrays if specs is None)
+def spread(arrays, axis_name, unit=1):
+    masks = range(unit, unit * (len(arrays) + 1), unit)
+    moved = [swap(array, axis_name, mask) for mask, array in reversed(list(zip(masks, arrays)))]
+    return moved[::-1]
+
+
+def device_call(kernel, name, outs, arrays, scratch=(), flops=0, limit=SMALL_MIB, specs=None, moved=0):
+    moved = moved or sum(a.size * a.dtype.itemsize for a in arrays)
     return pl.pallas_call(
         kernel,
         out_shape=outs,
@@ -267,18 +273,10 @@
 
 
 def attention_kernel(*refs):
-    half = len(refs) - 8 - 1 - 3 - 4 - 1
+    half = len(refs) - 8 - 1 - 3
     query_refs = refs[:half]
-    sources = refs[half : half + 4]
-    pair_k, pair_v, pair_nk, pair_nv = refs[half + 4 : half + 8]
-    mine_ref, query_buf, key_buf, value_buf = refs[half + 8 : half + 12]
-    held, copy_sem = refs[half + 12 : -1], refs[-1]
-    copies = [
-        pltpu.make_async_copy(source, buf, copy_sem.at[at]) for at, (source, buf) in enumerate(zip(sources, held))
-    ]
-    for at in (2, 0, 3, 1):
-        copies[at].start()
-    own_k, own_v, new_k, new_v = held
+    own_k, own_v, new_k, new_v, pair_k, pair_v, pair_nk, pair_nv = refs[half : half + 8]
+    mine_ref, query_buf, key_buf, value_buf = refs[half + 8 :]
     own = lax.axis_index("ctx")
     slots, _, head_dim = own_k.shape
     tok_local = new_k.shape[1]
@@ -292,8 +290,6 @@
             query_buf[head // group, start : start + tok_local, :] = query_ref[
                 :, head * head_dim : (head + 1) * head_dim
             ]
-    for copy in copies:
-        copy.wait()
     for part, (key_ref, value_ref) in enumerate(((new_k, new_v), (pair_nk, pair_nv))):
         for slot in range(slots):
             key_buf[slot, part * tok_local : (part + 1) * tok_local, :] = key_ref[slot]
@@ -399,161 +395,226 @@
         out_refs[k][...] = packed[expert_at(shape, lax.axis_index("ctx") ^ (2 * k))]
 
 
-def stage_kernel(first, *refs):
+def block_rows(step, deep):
+    return pl.ds(pl.multiple_of((lax.axis_index("ctx") ^ step) * deep, deep), deep)
+
+
+def stage_copies(steps, gate_hbm, up_hbm, outs, sem):
+    copies = []
+    for at, step in enumerate(steps):
+        rows = block_rows(step, outs[0].shape[0])
+        copies.append(pltpu.make_async_copy(gate_hbm.at[0, rows, :], outs[2 * at], sem.at[2 * at]))
+        copies.append(pltpu.make_async_copy(up_hbm.at[0, rows, :], outs[2 * at + 1], sem.at[2 * at + 1]))
+    return copies
+
+
+def stage_kernel(steps, *refs):
     gate_hbm, up_hbm = refs[:2]
-    extra = (len(refs) - 5) // 2
-    plain, gate_out, up_out = refs[2 : 2 + extra], refs[2 + extra], refs[3 + extra]
-    plain_out, sem = refs[4 + extra : -1], refs[-1]
-    own = lax.axis_index("ctx")
-    count, deep = gate_out.shape[0], gate_out.shape[1]
-    pairs = list(zip(plain, plain_out))
-    for step in range(count):
-        rows = pl.ds(pl.multiple_of((own ^ (first + step)) * deep, deep), deep)
-        pairs.append((gate_hbm.at[0, rows, :], gate_out.at[step]))
-        pairs.append((up_hbm.at[0, rows, :], up_out.at[step]))
-    copies = [pltpu.make_async_copy(source, target, sem.at[at]) for at, (source, target) in enumerate(pairs)]
+    extra = (len(refs) - 4 - 2 * len(steps)) // 2
+    plain, outs = refs[2 : 2 + extra], refs[2 + extra : -2 - extra]
+    plain_out, sem, plain_sem = refs[-2 - extra : -2], refs[-2], refs[-1]
+    copies = [
+        pltpu.make_async_copy(source, target, plain_sem.at[at])
+        for at, (source, target) in enumerate(zip(plain, plain_out))
+    ]
+    copies += stage_copies(steps, gate_hbm, up_hbm, outs, sem)
     for copy in copies:
         copy.start()
     for copy in copies:
         copy.wait()
 
 
-def stage(gate_proj, up_proj, deep, first, count, limit, *plain):
+def staged_like(steps, deep, units):
+    return (pltpu.VMEM((deep, units), BF16),) * (2 * len(steps))
+
+
+def stage(gate_proj, up_proj, deep, steps, *plain):
     units = gate_proj.shape[2]
     return pl.pallas_call(
-        functools.partial(stage_kernel, first),
-        out_shape=(pltpu.VMEM((count, deep, units), BF16),) * 2 + tuple(pltpu.VMEM(a.shape, a.dtype) for a in plain),
+        functools.partial(stage_kernel, steps),
+        out_shape=staged_like(steps, deep, units) + tuple(pltpu.VMEM(a.shape, a.dtype) for a in plain),
         in_specs=[HBM_SPEC] * (2 + len(plain)),
-        out_specs=(VMEM_SPEC,) * (2 + len(plain)),
-        scratch_shapes=[pltpu.SemaphoreType.DMA((2 * count + len(plain),))],
-        compiler_params=pltpu.CompilerParams(vmem_limit_bytes=limit << 20),
-        cost_estimate=pl.CostEstimate(flops=0, bytes_accessed=4 * count * deep * units, transcendentals=0),
+        out_specs=(VMEM_SPEC,) * (2 * len(steps) + len(plain)),
+        scratch_shapes=[
+            pltpu.SemaphoreType.DMA((max(1, 2 * len(steps)),)),
+            pltpu.SemaphoreType.DMA((max(1, len(plain)),)),
+        ],
+        compiler_params=pltpu.CompilerParams(vmem_limit_bytes=2 << 20),
+        cost_estimate=pl.CostEstimate(flops=0, bytes_accessed=4 * len(steps) * deep * units, transcendentals=0),
         name="stage",
     )(gate_proj, up_proj, *plain)
 
 
-def experts_kernel(early, *refs):
-    early_refs, refs = refs[: 2 * len(early)], refs[2 * len(early) :]
-    count = len(refs) - 4 - 2 - 10
-    row_refs = refs[:count]
-    staged = sum(early)
-    gain_ref, gate_hbm, up_hbm, down_hbm, out_even_ref, out_odd_ref = refs[count : count + 6]
-    (scaled_ref, act_ref, gate_acc, up_acc, out_acc, gate_buf, up_buf, down_buf, gate_sem, down_sem) = refs[count + 6 :]
+def scaled_rows(row_ref, gain_ref, step):
+    wide = row_ref[...].astype(F32)
+    squares = jnp.sum(wide * wide, axis=1, keepdims=True)
+    return squares, (wide * gain_ref[lax.axis_index("ctx") ^ step]).astype(BF16)
+
+
+def early_kernel(count, steps, *refs):
+    row_refs, gain_ref, weight_refs, refs = refs[:count], refs[count], refs[count + 1 : 3 * count + 1], refs[3 * count + 1 :]
+    gate_hbm, up_hbm, gate_acc, up_acc, squares_ref = refs[:5]
+    copies = stage_copies(steps, gate_hbm, up_hbm, refs[5:-1], refs[-1]) if steps else []
+    for copy in copies:
+        copy.start()
+    squares = 0.0
+    for step in range(count):
+        more, rows = scaled_rows(row_refs[step], gain_ref, step)
+        squares = squares + more
+        for acc, weights in ((gate_acc, weight_refs[2 * step]), (up_acc, weight_refs[2 * step + 1])):
+            term = jnp.dot(rows, weights[...], preferred_element_type=F32)
+            acc[...] = term if step == 0 else acc[...] + term
+    squares_ref[...] = jnp.broadcast_to(squares, squares_ref.shape)
+    for copy in copies:
+        copy.wait()
+
+
+def experts_kernel(first, held, count, *refs):
+    own_rows = count - first
+    row_refs, gain_ref = refs[:own_rows], refs[own_rows]
+    weight_refs, refs = refs[own_rows + 1 : own_rows + 1 + 2 * held], refs[own_rows + 1 + 2 * held :]
+    gate_in, up_in, squares_ref, gate_hbm, up_hbm, down_hbm, even_ref, odd_ref, act_ref = refs[:9]
+    gate_acc, up_acc, pair_acc, gate_buf, up_buf, down_buf, gate_sem, down_sem = refs[9:]
     own = lax.axis_index("ctx")
     half = count // 2
     deep = row_refs[0].shape[1]
-    ring = gate_buf.shape[0]
-    down_blocks, down_ring, down_rows = act_ref.shape[0], down_buf.shape[0], down_buf.shape[1]
-
-    def gate_copy(step):
-        rows = pl.ds(pl.multiple_of((own ^ step) * deep, deep), deep)
-        slot = lax.rem(step, ring)
+    units = gate_acc.shape[1]
+    late = list(range(first + held, count))
+    gate_ring, down_ring, down_rows = gate_buf.shape[0], down_buf.shape[0], down_buf.shape[1]
+    parts = units // down_rows
+
+    def gate_copies(at):
+        rows, slot = block_rows(late[at], deep), at % gate_ring
         return (
             pltpu.make_async_copy(gate_hbm.at[0, rows, :], gate_buf.at[slot], gate_sem.at[0, slot]),
             pltpu.make_async_copy(up_hbm.at[0, rows, :], up_buf.at[slot], gate_sem.at[1, slot]),
         )
 
-    def down_copy(step):
-        rows = pl.ds(pl.multiple_of(step * down_rows, down_rows), down_rows)
-        slot = lax.rem(step, down_ring)
-        return pltpu.make_async_copy(down_hbm.at[0, rows, :], down_buf.at[slot], down_sem.at[slot])
-
-    for step in range(staged, min(count, staged + ring)):
-        for copy in gate_copy(jnp.int32(step)):
+    down = [
+        down_copy(down_hbm, down_buf.at[at % down_ring], down_sem.at[at % down_ring], 1 + at // parts, at % parts)
+        for at in range((half - 1) * parts)
+    ]
+    for at in range(min(gate_ring, len(late))):
+        for copy in gate_copies(at):
             copy.start()
-    squares = jnp.zeros((row_refs[0].shape[0], 1), F32)
-    for step in range(count):
-        wide = row_refs[step][...].astype(F32)
-        squares = squares + jnp.sum(wide * wide, axis=1, keepdims=True)
-        scaled_ref[step] = (wide * gain_ref[own ^ step]).astype(BF16)
+    if len(late) <= gate_ring:
+        for copy in down[:down_ring]:
+            copy.start()
+    squares = squares_ref[:, 0:1]
+    gate_acc[...] = gate_in[...]
+    up_acc[...] = up_in[...]
+    for step in range(first, count):
+        more, rows = scaled_rows(row_refs[step - first], gain_ref, step)
+        squares = squares + more
+        if step < first + held:
+            gate_w, up_w = weight_refs[2 * (step - first)], weight_refs[2 * (step - first) + 1]
+        else:
+            at = step - first - held
+            for copy in gate_copies(at):
+                copy.wait()
+            gate_w, up_w = gate_buf.at[at % gate_ring], up_buf.at[at % gate_ring]
+        gate_acc[...] += jnp.dot(rows, gate_w[...], preferred_element_type=F32)
+        up_acc[...] += jnp.dot(rows, up_w[...], preferred_element_type=F32)
+        if step >= first + held and at + gate_ring < len(late):
+            for copy in gate_copies(at + gate_ring):
+                copy.start()
+            if at + gate_ring == len(late) - 1:
+                for copy in down[:down_ring]:
+                    copy.start()
     rms = lax.rsqrt(squares / D + norm_eps)
-    gate_acc[...] = jnp.zeros_like(gate_acc)
-    up_acc[...] = jnp.zeros_like(up_acc)
-
-    begin = 0
-    for at, number in enumerate(early):
-
-        def early_step(step, carry, at=at, begin=begin):
-            rows = scaled_ref[begin + step]
-            gate_acc[...] += jnp.dot(rows, early_refs[2 * at][step], preferred_element_type=F32)
-            up_acc[...] += jnp.dot(rows, early_refs[2 * at + 1][step], preferred_element_type=F32)
-            return carry
-
-        lax.fori_loop(0, number, early_step, 0)
-        begin += number
-
-    def gate_step(step, carry):
-        slot = lax.rem(step, ring)
-        for copy in gate_copy(step):
-            copy.wait()
-        rows = scaled_ref[step]
-        gate_acc[...] += jnp.dot(rows, gate_buf[slot], preferred_element_type=F32)
-        up_acc[...] += jnp.dot(rows, up_buf[slot], preferred_element_type=F32)
-
-        @pl.when(step + ring < count)
-        def _():
-            for copy in gate_copy(step + ring):
-                copy.start()
-
-        @pl.when(step + ring == count)
-        def _():
-            for index in range(down_ring):
-                down_copy(jnp.int32(index)).start()
-
-        return carry
-
-    lax.fori_loop(staged, count, gate_step, 0)
     gate = rms * gate_acc[...]
-    act = (gate / (1.0 + jnp.exp(-gate)) * (rms * up_acc[...])).astype(BF16)
-    for index in range(down_blocks):
-        act_ref[index] = act[:, index * down_rows : (index + 1) * down_rows]
-    out_acc[...] = jnp.zeros_like(out_acc)
-
-    def down_step(step, carry):
-        down_copy(step).wait()
-        slot = lax.rem(step, down_ring)
-        out_acc[...] += jnp.dot(act_ref[step], down_buf[slot], preferred_element_type=F32)
-
-        @pl.when(step + down_ring < down_blocks)
-        def _():
-            down_copy(step + down_ring).start()
-
-        return carry
-
-    lax.fori_loop(0, down_blocks, down_step, 0)
-    for step in range(count):
-        columns = pl.ds(pl.multiple_of((own ^ step) * deep, deep), deep)
-        (out_even_ref if step % 2 == 0 else out_odd_ref)[step // 2] = out_acc[:, columns].astype(BF16)
-
-
-def run_experts(early, row_blocks, gain, gate_proj, up_proj, down_proj):
-    rows, deep = row_blocks[0].shape
-    count = len(row_blocks)
+    act_ref[...] = (gate / (1.0 + jnp.exp(-gate)) * (rms * up_acc[...])).astype(BF16)
+    odd = own & 1
+    for at, copy in enumerate(down):
+        part = at % parts
+        copy.wait()
+        term = jnp.dot(
+            act_ref[:, part * down_rows : (part + 1) * down_rows],
+            down_buf[at % down_ring],
+            preferred_element_type=F32,
+        )
+        pair_acc[...] = term if part == 0 else pair_acc[...] + term
+        if at + down_ring < len(down):
+            down[at + down_ring].start()
+        if part == parts - 1:
+            store_pair(pair_acc, even_ref.at[at // parts], odd_ref.at[at // parts], odd)
+
+
+def down_copy(down_hbm, target, sem, chip, part):
+    rows, columns = target.shape
+    start = pl.multiple_of(((lax.axis_index("ctx") >> 1) ^ chip) * columns, columns)
+    return pltpu.make_async_copy(
+        down_hbm.at[0, part * rows : (part + 1) * rows, pl.ds(start, columns)], target, sem
+    )
+
+
+def store_pair(pair_acc, even_ref, odd_ref, odd):
+    deep = even_ref.shape[1]
+    even_ref[...] = pair_acc[:, pl.ds(pl.multiple_of(odd * deep, deep), deep)].astype(BF16)
+    odd_ref[...] = pair_acc[:, pl.ds(pl.multiple_of((1 - odd) * deep, deep), deep)].astype(BF16)
+
+
+def own_columns_kernel(act_ref, down_hbm, even_ref, odd_ref, pair_acc, down_buf, down_sem):
+    parts, down_rows = down_buf.shape[0], down_buf.shape[1]
+    copies = [down_copy(down_hbm, down_buf.at[part], down_sem.at[part], 0, part) for part in range(parts)]
+    for copy in copies:
+        copy.start()
+    for part, copy in enumerate(copies):
+        copy.wait()
+        term = jnp.dot(
+            act_ref[:, part * down_rows : (part + 1) * down_rows], down_buf[part], preferred_element_type=F32
+        )
+        pair_acc[...] = term if part == 0 else pair_acc[...] + term
+    store_pair(pair_acc, even_ref, odd_ref, lax.axis_index("ctx") & 1)
+
+
+def run_early(rows, gain, staged, steps, gate_proj, up_proj):
+    tokens, deep = rows[0].shape
     units = gate_proj.shape[2]
-    wide = down_proj.shape[2]
-    ring, down_blocks, down_ring = RING, 8, DOWN_RING
+    acc = pltpu.VMEM((tokens, units), F32)
+    outs = (acc, acc, pltpu.VMEM((tokens, 128), F32)) + (staged_like(steps, deep, units) if steps else ())
+    return pl.pallas_call(
+        functools.partial(early_kernel, len(rows), steps),
+        out_shape=outs,
+        in_specs=[VMEM_SPEC] * (len(rows) + 1 + len(staged)) + [HBM_SPEC] * 2,
+        out_specs=(VMEM_SPEC,) * len(outs),
+        scratch_shapes=[pltpu.SemaphoreType.DMA((2 * len(steps),))] if steps else [],
+        compiler_params=pltpu.CompilerParams(vmem_limit_bytes=5 << 20),
+        cost_estimate=pl.CostEstimate(
+            flops=4 * tokens * deep * units * len(rows),
+            bytes_accessed=4 * len(steps) * deep * units,
+            transcendentals=0,
+        ),
+        name="early",
+    )(*rows, gain, *[in_vmem(array) for array in staged], gate_proj, up_proj)
+
+
+def run_experts(rows, first, gain, staged, sums, gate_proj, up_proj, down_proj):
+    tokens, deep = rows[0].shape
+    count = first + len(rows)
+    units = gate_proj.shape[2]
+    parts = 2
     weights = 2 * (2 * gate_proj.size + down_proj.size)
+    pieces = like((count // 2 - 1, tokens, deep))
     return pl.pallas_call(
-        functools.partial(experts_kernel, tuple(gate.shape[0] for gate, _ in early)),
-        out_shape=(like((count // 2, rows, deep)),) * 2,
-        in_specs=[VMEM_SPEC] * (2 * len(early) + count + 1) + [HBM_SPEC] * 3,
-        out_specs=(VMEM_SPEC, VMEM_SPEC),
+        functools.partial(experts_kernel, first, len(staged) // 2, count),
+        out_shape=(pieces, pieces, pltpu.VMEM((tokens, units), BF16)),
+        in_specs=[VMEM_SPEC] * (len(rows) + 1 + len(staged) + 3) + [HBM_SPEC] * 3,
+        out_specs=(VMEM_SPEC,) * 3,
         scratch_shapes=[
-            pltpu.VMEM((count, rows, deep), BF16),
-            pltpu.VMEM((down_blocks, rows, units // down_blocks), BF16),
-            pltpu.VMEM((rows, units), F32),
-            pltpu.VMEM((rows, units), F32),
-            pltpu.VMEM((rows, wide), F32),
-            pltpu.VMEM((ring, deep, units), BF16),
-            pltpu.VMEM((ring, deep, units), BF16),
-            pltpu.VMEM((down_ring, units // down_blocks, wide), BF16),
-            pltpu.SemaphoreType.DMA((2, ring)),
-            pltpu.SemaphoreType.DMA((down_ring,)),
+            pltpu.VMEM((tokens, units), F32),
+            pltpu.VMEM((tokens, units), F32),
+            pltpu.VMEM((tokens, 2 * deep), F32),
+            pltpu.VMEM((GATE_RING, deep, units), BF16),
+            pltpu.VMEM((GATE_RING, deep, units), BF16),
+            pltpu.VMEM((DOWN_RING, units // parts, 2 * deep), BF16),
+            pltpu.SemaphoreType.DMA((2, GATE_RING)),
+            pltpu.SemaphoreType.DMA((DOWN_RING,)),
         ],
         compiler_params=pltpu.CompilerParams(vmem_limit_bytes=EXPERTS_MIB << 20),
-        cost_estimate=pl.CostEstimate(flops=rows * weights, bytes_accessed=weights, transcendentals=rows * units),
+        cost_estimate=pl.CostEstimate(flops=tokens * weights, bytes_accessed=weights // 2, transcendentals=tokens * units),
         name="experts",
-    )(*[in_vmem(array) for both in early for array in both], *row_blocks, gain, gate_proj, up_proj, down_proj)
+    )(*rows, gain, *[in_vmem(array) for array in staged], *sums, gate_proj, up_proj, down_proj)
 
 
 def pair_total_kernel(even_ref, other_ref, *out_refs):
@@ -563,8 +624,10 @@
 
 def combine_kernel(shape, high_ref, low_ref, *refs):
     half, mp_count = shape[0] // 2, shape[1]
-    piece_refs, kept_ref, sent_refs = refs[:half], refs[half], refs[half + 1 :]
-    pieces = jnp.concatenate([ref[...] for ref in piece_refs], axis=0)
+    piece_refs, even_ref, other_ref = refs[: half - 1], refs[half - 1], refs[half]
+    kept_ref, sent_refs = refs[half + 1], refs[half + 2 :]
+    own_piece = (even_ref[...].astype(F32) + other_ref[...].astype(F32)).astype(BF16)
+    pieces = jnp.concatenate([own_piece] + [ref[...] for ref in piece_refs], axis=0)
     experts = [expert_at(shape, lax.axis_index("ctx") ^ (2 * k)) for k in range(half)]
     total = None
     for table in (high_ref, low_ref):
@@ -607,26 +670,25 @@
     capacity = tokens * TOP // 4
     per_row = max(1, EXPERTS // mp_count)
 
-    blocks = [queries] + [swap(queries, "ctx", 2 * k) for k in range(1, half)]
+    blocks = [queries] + spread([queries] * (half - 1), "ctx", 2)
     own = [cache_keys, cache_values, new_keys, new_values]
     pair = [swap(array, "ctx", 1) for array in own]
+    held = stage(gate_hbm, up_hbm, d_local, (), *[in_hbm(array) for array in (*own, queries)])
+    held, blocks[1:], pair = lax.optimization_barrier((held, blocks[1:], pair))
     mine = device_call(
         attention_kernel,
         "attention",
         like((heads + 1, rows, head_dim)),
-        [in_vmem(array) for array in blocks] + [in_hbm(array) for array in own] + [in_vmem(array) for array in pair],
+        [in_vmem(array) for array in (held[4], *blocks[1:], *held[:4], *pair)],
         [
             pltpu.VMEM((slot_local, heads // slot_local * rows, head_dim), BF16),
             pltpu.VMEM((slot_local, 2 * tok_local, head_dim), BF16),
             pltpu.VMEM((slot_local, 2 * tok_local, head_dim), BF16),
-            *[pltpu.VMEM(array.shape, BF16) for array in own],
-            pltpu.SemaphoreType.DMA((4,)),
         ],
         flops=8 * heads * rows * (cache_local + tok_local) * head_dim,
         limit=24,
-        specs=[VMEM_SPEC] * half + [HBM_SPEC] * 4 + [VMEM_SPEC] * 4,
-    )
-    others = [swap(mine, "ctx", 2 * k) for k in range(1, half)]
+    )
+    others = spread([mine] * (half - 1), "ctx", 2)
     ids, logits, _ = lax.optimization_barrier((expert_ids.T, route_logits.T, mine))
     pick, high, low = device_call(
         functools.partial(tables_kernel, shape),
@@ -636,10 +698,11 @@
     )
     gain = norm_gain.astype(F32).reshape(ctx_count, 1, d_local)
     gate_later, _ = lax.optimization_barrier((gate_proj, mine))
-    gate_a, up_a, out_proj, residual = stage(in_hbm(gate_later), up_hbm, d_local, 0, STAGED[0], 2, in_hbm(out_proj), in_hbm(residual)
-    )
-    pick, high, low, gain, gate_a, up_a, out_proj, residual, *others = lax.optimization_barrier(
-        (pick, high, low, gain, gate_a, up_a, out_proj, residual, *others)
+    *staged, out_proj, residual = stage(
+        in_hbm(gate_later), up_hbm, d_local, STAGE_AT[0], in_hbm(out_proj), in_hbm(residual)
+    )
+    pick, high, low, gain, staged, out_proj, residual, others = lax.optimization_barrier(
+        (pick, high, low, gain, staged, out_proj, residual, others)
     )
     attn = device_call(join_kernel, "join", like((rows, heads * head_dim)), [mine] + others)
     block = like((res_rows, d_local))
@@ -652,16 +715,18 @@
         [pltpu.VMEM((tokens, heads * head_dim), BF16)],
         flops=2 * tokens * heads * head_dim * d_local,
     )
-    arrived = [swap(array, "mp", k) for k, array in enumerate(sent, 1)]
-    early = [(gate_a, up_a)]
-    if STAGED[1]:
-        gate_later, _ = lax.optimization_barrier((gate_proj, kept))
-        gate_b, up_b = stage(in_hbm(gate_later), up_hbm, d_local, STAGED[0], STAGED[1], 2)
-        gate_b, up_b, *arrived = lax.optimization_barrier((gate_b, up_b, *arrived))
-        early.append((gate_b, up_b))
-    hidden = device_call(total_kernel, "hidden", block, [kept, residual] + arrived)
-
-    everyone = [hidden] + [swap(hidden, "mp", k) for k in range(1, mp_count)]
+    arrived = spread(sent, "mp")
+    gate_later, _ = lax.optimization_barrier((gate_proj, kept))
+    more = stage(in_hbm(gate_later), up_hbm, d_local, STAGE_AT[1])
+    more, arrived = lax.optimization_barrier((more, arrived))
+    staged = [*staged, *more]
+    hidden = device_call(total_kernel, "hidden", block, [kept, residual] + arrived[::-1])
+
+    everyone = spread([hidden] * (mp_count - 1), "mp")
+    gate_later, _ = lax.optimization_barrier((gate_proj, hidden))
+    more = stage(in_hbm(gate_later), up_hbm, d_local, STAGE_AT[2])
+    more, everyone = lax.optimization_barrier((more, everyone))
+    staged, everyone = [*staged, *more], [hidden, *everyone]
     even = device_call(
         functools.partial(pack_kernel, shape),
         "pack",
@@ -669,31 +734,45 @@
         [pick] + everyone,
         [pltpu.VMEM((per_row, capacity, d_local), BF16)],
     )
-    even = [even[0]] + [swap(even[k], "ctx", 2 * k) for k in range(1, half)]
-    odd = [swap(array, "ctx", 1) for array in even]
-    out_even, out_odd = run_experts(
-        early,
-        [array for both in zip(even, odd) for array in both],
-        gain,
-        gate_hbm,
-        up_hbm,
-        down_hbm,
+    even = [even[0]] + spread(even[1:], "ctx", 2)
+    first = [even[0], swap(even[0], "ctx", 1)]
+    sums = run_early(first, gain, staged[:4], STAGE_AT[3], gate_hbm, up_hbm)
+    sums, even = lax.optimization_barrier((sums, even[1:]))
+    gate_sum, up_sum, squares, *more = sums
+    arrived = [array for piece in even for array in (piece, swap(piece, "ctx", 1))]
+    out_even, out_odd, act = run_experts(
+        arrived, 2, gain, [*staged[4:], *more], (gate_sum, up_sum, squares), gate_hbm, up_hbm, down_hbm
     )
     pieces = device_call(
         pair_total_kernel,
         "pair_total",
-        (like((capacity, d_local)),) * half,
+        (like((capacity, d_local)),) * (half - 1),
         [out_even, swap(out_odd, "ctx", 1)],
     )
-    pieces = [pieces[0]] + [swap(pieces[k], "ctx", 2 * k) for k in range(1, half)]
+    act, *pieces = lax.optimization_barrier((act, *pieces))
+    returned = spread(pieces, "ctx", 2)
+    own_even, own_odd = device_call(
+        own_columns_kernel,
+        "own_columns",
+        (like((capacity, d_local)),) * 2,
+        [act, down_hbm],
+        [
+            pltpu.VMEM((capacity, 2 * d_local), F32),
+            pltpu.VMEM((2, act.shape[1] // 2, 2 * d_local), BF16),
+            pltpu.SemaphoreType.DMA((2,)),
+        ],
+        specs=[VMEM_SPEC, HBM_SPEC],
+        moved=1,
+    )
+    pieces = returned + [own_even, swap(own_odd, "ctx", 1)]
     kept, *sent = device_call(
         functools.partial(combine_kernel, shape),
         "combine",
         (like((res_rows, d_local), F32),) + (block,) * (mp_count - 1),
         [high, low] + pieces,
     )
-    arrived = [swap(array, "mp", k) for k, array in enumerate(sent, 1)]
-    return device_call(total_kernel, "layer_out", block, [kept, hidden] + arrived)
+    arrived = spread(sent, "mp")
+    return device_call(total_kernel, "layer_out", block, [kept, hidden] + arrived[::-1])
 
 
 def on_device(*args):

time: 96.2 us -> 89 us (0.925)
  waiting for transfers between devices: 26.1 us -> 15.7 us
  Pallas kernels: 35.9 us -> 41.4 us
  local copies, waits for them, and re-layouts: 2.15 us -> 0.01 us
    ppermute x31 -> x32, waiting for transfers between devices: 26.1 us -> 15.7 us  [swap(): return lax.ppermute(array, axis_name, [(i, i ^ mask) for i in range(count)])]
    pallas_call x3 -> x6, Pallas kernels: 29.6 us -> 32.6 us  [the longest x4 15.9 us: stage(): pl.pallas_call(functools.partial(stage_kernel, steps), out_shape=staged_l...]
    pallas_call x9 -> x10, Pallas kernels: 6.35 us -> 8.79 us  [device_call(): pl.pallas_call(kernel, out_shape=outs, in_specs=specs or [VMEM_SPEC] * le...]
    unnamed x6, local copies, waits for them, and re-layouts: 2.15 us -> 0.01 us
    ppermute x31 -> x32, starting transfers between devices: 30.9 us -> 31.6 us  [swap(): return lax.ppermute(array, axis_name, [(i, i ^ mask) for i in range(count)])]
  transfers between devices with their start and end apart: 31 -> 32, of which waited for: 17 -> 15; matrix products, arithmetic and copies ran while one was open for 1% -> 0% of each run, Pallas kernels for 11% -> 25%
where the time goes in v3:
time: 89 us; the launch traced here: 88.8 us
  Pallas kernels  41.4 us (47%)
  starting transfers between devices  31.6 us (36%)
  waiting for transfers between devices  15.7 us (18%)
    ppermute x32, starting transfers between devices, swap(): return lax.ppermute(array, axis_name, [(i, i ^ mask) for i in range(count)])  31.6 us
    pallas_call x4, Pallas kernels, stage(): pl.pallas_call(functools.partial(stage_kernel, steps), out_shape=staged_l...  15.9 us
    ppermute x32, waiting for transfers between devices, swap(): return lax.ppermute(array, axis_name, [(i, i ^ mask) for i in range(count)])  15.7 us
    pallas_call x1, Pallas kernels, run_experts(): pl.pallas_call(functools.partial(experts_kernel, first, len(staged) // 2,...  14.4 us
    pallas_call x10, Pallas kernels, device_call(): pl.pallas_call(kernel, out_shape=outs, in_specs=specs or [VMEM_SPEC] * le...  8.79 us
    pallas_call x1, Pallas kernels, run_early(): pl.pallas_call(functools.partial(early_kernel, len(rows), steps), out_sha...  2.29 us
  transfers between devices with their start and end apart: 32, of which 15 were waited for; matrix products, arithmetic and copies ran while one was open for 0% of the time, Pallas kernels for 25%

profile of v3, /device:TPU:0, one launch (start us, length us, event | category | flops | bytes accessed | tf_op | source)
XLA Modules:
  0.0 88.8 jit_solution(10402518324702068993)
XLA Ops:
  1.1 2.9 %collective-permute-start = (bf16[16,1536]{1,0:T(8,128)(2,1)}, bf16[16,1536]{1,0:T(8,128)(2,1)S(1)}, u32[]{:S(2)}, u32[]{:S(2)}) collective-permute-start(bf16[16,1536]{1,0:T(8,128)(2,1)} %refs_6_.1), channel_id=1, source_target_pairs={{0,8},{4,12},{8,0},{12,4},{16,24},{20,28},{24,16},{28,20},{1,9},{5... | collective-permute-start | bytes 147464 | tf_op jit(solution)/shard_map/ppermute | solution.py:191
  4.0 2.1 %collective-permute-start.2 = (bf16[16,1536]{1,0:T(8,128)(2,1)}, bf16[16,1536]{1,0:T(8,128)(2,1)S(1)}, u32[]{:S(2)}, u32[]{:S(2)}) collective-permute-start(bf16[16,1536]{1,0:T(8,128)(2,1)} %refs_6_.1), channel_id=1, source_target_pairs={{0,24},{4,28},{8,16},{12,20},{16,8},{20,12},{24,0},{28,4},{1,25},{... | collective-permute-start | bytes 147464 | tf_op jit(solution)/shard_map/ppermute | solution.py:191
  7.7 1.6 %collective-permute-done.2.refs_3_ = bf16[16,1536]{1,0:T(8,128)(2,1)S(1)} collective-permute-done((bf16[16,1536]{1,0:T(8,128)(2,1)}, bf16[16,1536]{1,0:T(8,128)(2,1)S(1)}, u32[]{:S(2)}, u32[]{:S(2)}) %collective-permute-start.2) | collective-permute-done | bytes 49184 | tf_op jit(solution)/shard_map/ppermute | solution.py:191
  10.4 2.1 %attention.1.refs_0_ = bf16[13,64,128]{2,1,0:T(8,128)(2,1)S(1)} custom-call(bf16[16,1536]{1,0:T(8,128)(2,1)S(1)} %get-tuple-element.109.refs_0_, bf16[16,1536]{1,0:T(8,128)(2,1)S(1)} %collective-permute-done.refs_1_, bf16[16,1536]{1,0:T(8,128)(2,1)S(1)} %collective-permute-done.1.refs_2_, bf16[16,1536]{1,0:T(8,128)(2,1)S(1)} %collective-permute-done.2.refs_3_, ...), custom_call_target="tpu_custom_call" | custom-call | flops 415236096 | bytes 1277952 | tf_op jit(solution)/shard_map/attention/pallas_call | solution.py:202
  12.5 1.5 %collective-permute-start.9 = (bf16[13,64,128]{2,1,0:T(8,128)(2,1)S(1)}, bf16[13,64,128]{2,1,0:T(8,128)(2,1)S(1)}, u32[]{:S(2)}, u32[]{:S(2)}) collective-permute-start(bf16[13,64,128]{2,1,0:T(8,128)(2,1)S(1)} %attention.1.refs_0_), channel_id=1, source_target_pairs={{0,24},{4,28},{8,16},{12,20},{16,8},{20,12},{24,0},{28,4},{1,25},{... | collective-permute-start | bytes 638984 | tf_op jit(solution)/shard_map/ppermute | solution.py:191
  16.4 7.2 %stage.5 = (bf16[768,2048]{1,0:T(8,128)(2,1)S(1)}, bf16[768,2048]{1,0:T(8,128)(2,1)S(1)}, bf16[768,2048]{1,0:T(8,128)(2,1)S(1)}, bf16[768,2048]{1,0:T(8,128)(2,1...) custom-call(bf16[1,6144,2048]{2,1,0:T(8,128)(2,1)} %refs_18_.1, ...), custom_call_target="tpu_custom_call" | custom-call | bytes 18874368 | tf_op jit(solution)/shard_map/stage/pallas_call | solution.py:433
  25.1 1.4 %collective-permute-done.10.pair_ref = bf16[64,1536]{1,0:T(8,128)(2,1)S(1)} collective-permute-done((bf16[64,1536]{1,0:T(8,128)(2,1)S(1)}, bf16[64,1536]{1,0:T(8,128)(2,1)S(1)}, u32[]{:S(2)}, u32[]{:S(2)}) %collective-permute-start.10) | collective-permute-done | bytes 196640 | tf_op jit(solution)/shard_map/ppermute | solution.py:191
  27.0 1.6 %collective-permute-start.11 = (bf16[32,768]{1,0:T(8,128)(2,1)S(1)}, bf16[32,768]{1,0:T(8,128)(2,1)S(1)}, u32[]{:S(2)}, u32[]{:S(2)}) collective-permute-start(bf16[32,768]{1,0:T(8,128)(2,1)S(1)} %get-tuple-element.149), channel_id=1, source_target_pairs={{0,1},{1,0},{2,3},{3,2},{4,5},{5,4},{6,7},{7,6},{8,9},{9,8},{10,11... | collective-permute-start | bytes 147464 | tf_op jit(solution)/shard_map/ppermute | solution.py:191
  28.6 2.6 %collective-permute-start.12 = (bf16[32,768]{1,0:T(8,128)(2,1)S(1)}, bf16[32,768]{1,0:T(8,128)(2,1)S(1)}, u32[]{:S(2)}, u32[]{:S(2)}) collective-permute-start(bf16[32,768]{1,0:T(8,128)(2,1)S(1)} %get-tuple-element.150), channel_id=1, source_target_pairs={{0,2},{1,3},{2,0},{3,1},{4,6},{5,7},{6,4},{7,5},{8,10},{9,11},{10,... | collective-permute-start | bytes 147464 | tf_op jit(solution)/shard_map/ppermute | solution.py:191
  31.4 4.7 %stage.6 = (bf16[768,2048]{1,0:T(8,128)(2,1)S(1)}, bf16[768,2048]{1,0:T(8,128)(2,1)S(1)}, bf16[768,2048]{1,0:T(8,128)(2,1)S(1)}, bf16[768,2048]{1,0:T(8,128)(2,1)S(1)}) custom-call(bf16[1,6144,2048]{2,1,0:T(8,128)(2,1)} %refs_18_.1, bf16[1,6144,2048]{2,1,0:T(8,128)(2,1)} %refs_19_.1), custom_call_target="tpu_custom_call" | custom-call | bytes 12582912 | tf_op jit(solution)/shard_map/stage/pallas_call | solution.py:433
  37.1 2.7 %collective-permute-start.16 = (bf16[32,768]{1,0:T(8,128)(2,1)S(1)}, bf16[32,768]{1,0:T(8,128)(2,1)S(1)}, u32[]{:S(2)}, u32[]{:S(2)}) collective-permute-start(bf16[32,768]{1,0:T(8,128)(2,1)S(1)} %hidden.1.refs_0_.refs_1_), channel_id=1, source_target_pairs={{0,3},{1,2},{2,1},{3,0},{4,7},{5,6},{6,5},{7,4},{8,11},{9,10},{10,... | collective-permute-start | bytes 147464 | tf_op jit(solution)/shard_map/ppermute | solution.py:191
  39.9 1.7 %collective-permute-start.14 = (bf16[32,768]{1,0:T(8,128)(2,1)S(1)}, bf16[32,768]{1,0:T(8,128)(2,1)S(1)}, u32[]{:S(2)}, u32[]{:S(2)}) collective-permute-start(bf16[32,768]{1,0:T(8,128)(2,1)S(1)} %hidden.1.refs_0_.refs_1_), channel_id=1, source_target_pairs={{0,1},{1,0},{2,3},{3,2},{4,5},{5,4},{6,7},{7,6},{8,9},{9,8},{10,11... | collective-permute-start | bytes 147464 | tf_op jit(solution)/shard_map/ppermute | solution.py:191
  41.6 2.9 %stage.7 = (bf16[768,2048]{1,0:T(8,128)(2,1)S(1)}, bf16[768,2048]{1,0:T(8,128)(2,1)S(1)}) custom-call(bf16[1,6144,2048]{2,1,0:T(8,128)(2,1)} %refs_18_.1, bf16[1,6144,2048]{2,1,0:T(8,128)(2,1)} %refs_19_.1), custom_call_target="tpu_custom_call" | custom-call | bytes 6291456 | tf_op jit(solution)/shard_map/stage/pallas_call | solution.py:433
  47.3 1.4 %collective-permute-start.20 = (bf16[64,768]{1,0:T(8,128)(2,1)S(1)}, bf16[64,768]{1,0:T(8,128)(2,1)S(1)}, u32[]{:S(2)}, u32[]{:S(2)}) collective-permute-start(bf16[64,768]{1,0:T(8,128)(2,1)S(1)} %get-tuple-element.172), channel_id=1, source_target_pairs={{0,24},{4,28},{8,16},{12,20},{16,8},{20,12},{24,0},{28,4},{1,25},{... | collective-permute-start | bytes 294920 | tf_op jit(solution)/shard_map/ppermute | solution.py:191
  48.8 2.3 %early.1 = (f32[64,2048]{1,0:T(8,128)S(1)}, f32[64,2048]{1,0:T(8,128)S(1)}, f32[64,128]{1,0:T(8,128)S(1)}) custom-call(bf16[64,768]{1,0:T(8,128)(2,1)S(1)} %get-tuple-element.161.refs_0_, bf16[64,768]{1,0:T(8,128)(2,1)S(1)} %collective-permute-done.17.refs_1_, f32[8,1,768]{2,1,0:T(1,128)S(1)} %bitcast.3, bf16[768,2048]{1,0:T(8,128)(2,1)S(1)} %get-tuple-element.163.refs_3_, ...), custom_call_target="tpu_custom_call" | custom-call | flops 805306368 | tf_op jit(solution)/shard_map/early/pallas_call | solution.py:576
  51.1 2.3 %collective-permute-done.19.refs_2_ = bf16[64,768]{1,0:T(8,128)(2,1)S(1)} collective-permute-done((bf16[64,768]{1,0:T(8,128)(2,1)S(1)}, bf16[64,768]{1,0:T(8,128)(2,1)S(1)}, u32[]{:S(2)}, u32[]{:S(2)}) %collective-permute-start.19) | collective-permute-done | bytes 98336 | tf_op jit(solution)/shard_map/ppermute | solution.py:191
  55.1 14.4 %experts.1 = (bf16[3,64,768]{2,1,0:T(8,128)(2,1)S(1)}, bf16[3,64,768]{2,1,0:T(8,128)(2,1)S(1)}, bf16[64,2048]{1,0:T(8,128)(2,1)S(1)}) custom-call(bf16[64,768]{1,0:T(8,128)(2,1)S(1)} %collective-permute-done.18.refs_0_, bf16[64,768]{1,0:T(8,128)(2,1)S(1)} %collective-permute-done.21.refs_1_, bf16[64,768]{1,0:T(8,128)(2,1)S(1)} %collective-permute-done.19.refs_2_, ...), custom_call_target="tpu_custom_call" | custom-call | flops 4831838208 | bytes 37748736 | tf_op jit(solution)/shard_map/experts/pallas_call | solution.py:599
  69.8 1.4 %collective-permute-done.24.other_ref = bf16[3,64,768]{2,1,0:T(8,128)(2,1)S(1)} collective-permute-done((bf16[3,64,768]{2,1,0:T(8,128)(2,1)S(1)}, bf16[3,64,768]{2,1,0:T(8,128)(2,1)S(1)}, u32[]{:S(2)}, u32[]{:S(2)}) %collective-permute-start.24) | collective-permute-done | bytes 294944 | tf_op jit(solution)/shard_map/ppermute | solution.py:191
  73.4 1.5 %collective-permute-start.27 = (bf16[64,768]{1,0:T(8,128)(2,1)S(1)}, bf16[64,768]{1,0:T(8,128)(2,1)S(1)}, u32[]{:S(2)}, u32[]{:S(2)}) collective-permute-start(bf16[64,768]{1,0:T(8,128)(2,1)S(1)} %get-tuple-element.195), channel_id=1, source_target_pairs={{0,24},{4,28},{8,16},{12,20},{16,8},{20,12},{24,0},{28,4},{1,25},{... | collective-permute-start | bytes 294920 | tf_op jit(solution)/shard_map/ppermute | solution.py:191
  74.9 3.6 %own_columns.1 = (bf16[64,768]{1,0:T(8,128)(2,1)S(1)}, bf16[64,768]{1,0:T(8,128)(2,1)S(1)}) custom-call(bf16[64,2048]{1,0:T(8,128)(2,1)S(1)} %get-tuple-element.196.act_ref, bf16[1,2048,6144]{2,1,0:T(8,128)(2,1)} %down_hbm.1), custom_call_target="tpu_custom_call" | custom-call | bytes 1 | tf_op jit(solution)/shard_map/own_columns/pallas_call | solution.py:202
  80.1 2.4 %collective-permute-start.29 = (bf16[32,768]{1,0:T(8,128)(2,1)S(1)}, bf16[32,768]{1,0:T(8,128)(2,1)S(1)}, u32[]{:S(2)}, u32[]{:S(2)}) collective-permute-start(bf16[32,768]{1,0:T(8,128)(2,1)S(1)} %get-tuple-element.200), channel_id=1, source_target_pairs={{0,3},{1,2},{2,1},{3,0},{4,7},{5,6},{6,5},{7,4},{8,11},{9,10},{10,... | collective-permute-start | bytes 147464 | tf_op jit(solution)/shard_map/ppermute | solution.py:191
  82.5 2.1 %collective-permute-start.31 = (bf16[32,768]{1,0:T(8,128)(2,1)S(1)}, bf16[32,768]{1,0:T(8,128)(2,1)S(1)}, u32[]{:S(2)}, u32[]{:S(2)}) collective-permute-start(bf16[32,768]{1,0:T(8,128)(2,1)S(1)} %get-tuple-element.202), channel_id=1, source_target_pairs={{0,1},{1,0},{2,3},{3,2},{4,5},{5,4},{6,7},{7,6},{8,9},{9,8},{10,11... | collective-permute-start | bytes 147464 | tf_op jit(solution)/shard_map/ppermute | solution.py:191
  84.6 2.1 %collective-permute-done.29.refs_2_ = bf16[32,768]{1,0:T(8,128)(2,1)S(1)} collective-permute-done((bf16[32,768]{1,0:T(8,128)(2,1)S(1)}, bf16[32,768]{1,0:T(8,128)(2,1)S(1)}, u32[]{:S(2)}, u32[]{:S(2)}) %collective-permute-start.29) | collective-permute-done | bytes 49184 | tf_op jit(solution)/shard_map/ppermute | solution.py:191
  86.6 1.5 %collective-permute-done.30.refs_3_ = bf16[32,768]{1,0:T(8,128)(2,1)S(1)} collective-permute-done((bf16[32,768]{1,0:T(8,128)(2,1)S(1)}, bf16[32,768]{1,0:T(8,128)(2,1)S(1)}, u32[]{:S(2)}, u32[]{:S(2)}) %collective-permute-start.30) | collective-permute-done | bytes 49184 | tf_op jit(solution)/shard_map/ppermute | solution.py:191
  (63 shorter events, 18.7 us)
Async XLA Ops:
  0.0 10.4 %collective-permute-start.3 = (bf16[2,512,128]{2,1,0:T(8,128)(2,1)}, bf16[2,512,128]{2,1,0:T(8,128)(2,1)S(1)}, u32[]{:S(2)}, u32[]{:S(2)}) collective-permute-start(bf16[2,512,128]{2,1,0:T(8,128)(2,1)} %refs_2_.2), channel_id=1, source_target_pairs={{0,4},{4,0},{8,12},{12,8},{16,20},{20,16},{24,28},{28,24},{1,5},{5... | collective-permute-start | bytes 786440 | tf_op jit(solution)/shard_map/ppermute | solution.py:191
  0.5 9.9 %collective-permute-start.4 = (bf16[2,512,128]{2,1,0:T(8,128)(2,1)}, bf16[2,512,128]{2,1,0:T(8,128)(2,1)S(1)}, u32[]{:S(2)}, u32[]{:S(2)}) collective-permute-start(bf16[2,512,128]{2,1,0:T(8,128)(2,1)} %refs_3_.2), channel_id=1, source_target_pairs={{0,4},{4,0},{8,12},{12,8},{16,20},{20,16},{24,28},{28,24},{1,5},{5... | collective-permute-start | bytes 786440 | tf_op jit(solution)/shard_map/ppermute | solution.py:191
  1.0 5.1 %collective-permute-start.6 = (bf16[2,16,128]{2,1,0:T(8,128)(2,1)}, bf16[2,16,128]{2,1,0:T(8,128)(2,1)S(1)}, u32[]{:S(2)}, u32[]{:S(2)}) collective-permute-start(bf16[2,16,128]{2,1,0:T(8,128)(2,1)} %refs_5_.1), channel_id=1, source_target_pairs={{0,4},{4,0},{8,12},{12,8},{16,20},{20,16},{24,28},{28,24},{1,5},{5... | collective-permute-start | bytes 24584 | tf_op jit(solution)/shard_map/ppermute | solution.py:191
  1.1 6.6 %collective-permute-start = (bf16[16,1536]{1,0:T(8,128)(2,1)}, bf16[16,1536]{1,0:T(8,128)(2,1)S(1)}, u32[]{:S(2)}, u32[]{:S(2)}) collective-permute-start(bf16[16,1536]{1,0:T(8,128)(2,1)} %refs_6_.1), channel_id=1, source_target_pairs={{0,8},{4,12},{8,0},{12,4},{16,24},{20,28},{24,16},{28,20},{1,9},{5... | collective-permute-start | bytes 147464 | tf_op jit(solution)/shard_map/ppermute | solution.py:191
  4.0 5.2 %collective-permute-start.2 = (bf16[16,1536]{1,0:T(8,128)(2,1)}, bf16[16,1536]{1,0:T(8,128)(2,1)S(1)}, u32[]{:S(2)}, u32[]{:S(2)}) collective-permute-start(bf16[16,1536]{1,0:T(8,128)(2,1)} %refs_6_.1), channel_id=1, source_target_pairs={{0,24},{4,28},{8,16},{12,20},{16,8},{20,12},{24,0},{28,4},{1,25},{... | collective-permute-start | bytes 147464 | tf_op jit(solution)/shard_map/ppermute | solution.py:191
  6.1 4.3 %collective-permute-start.1 = (bf16[16,1536]{1,0:T(8,128)(2,1)}, bf16[16,1536]{1,0:T(8,128)(2,1)S(1)}, u32[]{:S(2)}, u32[]{:S(2)}) collective-permute-start(bf16[16,1536]{1,0:T(8,128)(2,1)} %refs_6_.1), channel_id=1, source_target_pairs={{0,16},{4,20},{8,24},{12,28},{16,0},{20,4},{24,8},{28,12},{1,17},{... | collective-permute-start | bytes 147464 | tf_op jit(solution)/shard_map/ppermute | solution.py:191
  12.5 11.1 %collective-permute-start.9 = (bf16[13,64,128]{2,1,0:T(8,128)(2,1)S(1)}, bf16[13,64,128]{2,1,0:T(8,128)(2,1)S(1)}, u32[]{:S(2)}, u32[]{:S(2)}) collective-permute-start(bf16[13,64,128]{2,1,0:T(8,128)(2,1)S(1)} %attention.1.refs_0_), channel_id=1, source_target_pairs={{0,24},{4,28},{8,16},{12,20},{16,8},{20,12},{24,0},{28,4},{1,25},{... | collective-permute-start | bytes 638984 | tf_op jit(solution)/shard_map/ppermute | solution.py:191
  13.9 9.9 %collective-permute-start.8 = (bf16[13,64,128]{2,1,0:T(8,128)(2,1)S(1)}, bf16[13,64,128]{2,1,0:T(8,128)(2,1)S(1)}, u32[]{:S(2)}, u32[]{:S(2)}) collective-permute-start(bf16[13,64,128]{2,1,0:T(8,128)(2,1)S(1)} %attention.1.refs_0_), channel_id=1, source_target_pairs={{0,16},{4,20},{8,24},{12,28},{16,0},{20,4},{24,8},{28,12},{1,17},{... | collective-permute-start | bytes 638984 | tf_op jit(solution)/shard_map/ppermute | solution.py:191
  14.9 9.0 %collective-permute-start.7 = (bf16[13,64,128]{2,1,0:T(8,128)(2,1)S(1)}, bf16[13,64,128]{2,1,0:T(8,128)(2,1)S(1)}, u32[]{:S(2)}, u32[]{:S(2)}) collective-permute-start(bf16[13,64,128]{2,1,0:T(8,128)(2,1)S(1)} %attention.1.refs_0_), channel_id=1, source_target_pairs={{0,8},{4,12},{8,0},{12,4},{16,24},{20,28},{24,16},{28,20},{1,9},{5... | collective-permute-start | bytes 638984 | tf_op jit(solution)/shard_map/ppermute | solution.py:191
  27.0 9.2 %collective-permute-start.11 = (bf16[32,768]{1,0:T(8,128)(2,1)S(1)}, bf16[32,768]{1,0:T(8,128)(2,1)S(1)}, u32[]{:S(2)}, u32[]{:S(2)}) collective-permute-start(bf16[32,768]{1,0:T(8,128)(2,1)S(1)} %get-tuple-element.149), channel_id=1, source_target_pairs={{0,1},{1,0},{2,3},{3,2},{4,5},{5,4},{6,7},{7,6},{8,9},{9,8},{10,11... | collective-permute-start | bytes 147464 | tf_op jit(solution)/shard_map/ppermute | solution.py:191
  28.6 7.5 %collective-permute-start.12 = (bf16[32,768]{1,0:T(8,128)(2,1)S(1)}, bf16[32,768]{1,0:T(8,128)(2,1)S(1)}, u32[]{:S(2)}, u32[]{:S(2)}) collective-permute-start(bf16[32,768]{1,0:T(8,128)(2,1)S(1)} %get-tuple-element.150), channel_id=1, source_target_pairs={{0,2},{1,3},{2,0},{3,1},{4,6},{5,7},{6,4},{7,5},{8,10},{9,11},{10,... | collective-permute-start | bytes 147464 | tf_op jit(solution)/shard_map/ppermute | solution.py:191
  31.2 5.9 %collective-permute-start.13 = (bf16[32,768]{1,0:T(8,128)(2,1)S(1)}, bf16[32,768]{1,0:T(8,128)(2,1)S(1)}, u32[]{:S(2)}, u32[]{:S(2)}) collective-permute-start(bf16[32,768]{1,0:T(8,128)(2,1)S(1)} %get-tuple-element.151), channel_id=1, source_target_pairs={{0,3},{1,2},{2,1},{3,0},{4,7},{5,6},{6,5},{7,4},{8,11},{9,10},{10,... | collective-permute-start | bytes 147464 | tf_op jit(solution)/shard_map/ppermute | solution.py:191
  37.1 7.3 %collective-permute-start.16 = (bf16[32,768]{1,0:T(8,128)(2,1)S(1)}, bf16[32,768]{1,0:T(8,128)(2,1)S(1)}, u32[]{:S(2)}, u32[]{:S(2)}) collective-permute-start(bf16[32,768]{1,0:T(8,128)(2,1)S(1)} %hidden.1.refs_0_.refs_1_), channel_id=1, source_target_pairs={{0,3},{1,2},{2,1},{3,0},{4,7},{5,6},{6,5},{7,4},{8,11},{9,10},{10,... | collective-permute-start | bytes 147464 | tf_op jit(solution)/shard_map/ppermute | solution.py:191
  39.9 5.0 %collective-permute-start.15 = (bf16[32,768]{1,0:T(8,128)(2,1)S(1)}, bf16[32,768]{1,0:T(8,128)(2,1)S(1)}, u32[]{:S(2)}, u32[]{:S(2)}) collective-permute-start(bf16[32,768]{1,0:T(8,128)(2,1)S(1)} %hidden.1.refs_0_.refs_1_), channel_id=1, source_target_pairs={{0,2},{1,3},{2,0},{3,1},{4,6},{5,7},{6,4},{7,5},{8,10},{9,11},{10,... | collective-permute-start | bytes 147464 | tf_op jit(solution)/shard_map/ppermute | solution.py:191
  39.9 5.0 %collective-permute-start.14 = (bf16[32,768]{1,0:T(8,128)(2,1)S(1)}, bf16[32,768]{1,0:T(8,128)(2,1)S(1)}, u32[]{:S(2)}, u32[]{:S(2)}) collective-permute-start(bf16[32,768]{1,0:T(8,128)(2,1)S(1)} %hidden.1.refs_0_.refs_1_), channel_id=1, source_target_pairs={{0,1},{1,0},{2,3},{3,2},{4,5},{5,4},{6,7},{7,6},{8,9},{9,8},{10,11... | collective-permute-start | bytes 147464 | tf_op jit(solution)/shard_map/ppermute | solution.py:191
  45.2 5.9 %collective-permute-start.18 = (bf16[64,768]{1,0:T(8,128)(2,1)S(1)}, bf16[64,768]{1,0:T(8,128)(2,1)S(1)}, u32[]{:S(2)}, u32[]{:S(2)}) collective-permute-start(bf16[64,768]{1,0:T(8,128)(2,1)S(1)} %get-tuple-element.170), channel_id=1, source_target_pairs={{0,8},{4,12},{8,0},{12,4},{16,24},{20,28},{24,16},{28,20},{1,9},{5... | collective-permute-start | bytes 294920 | tf_op jit(solution)/shard_map/ppermute | solution.py:191
  46.4 7.0 %collective-permute-start.19 = (bf16[64,768]{1,0:T(8,128)(2,1)S(1)}, bf16[64,768]{1,0:T(8,128)(2,1)S(1)}, u32[]{:S(2)}, u32[]{:S(2)}) collective-permute-start(bf16[64,768]{1,0:T(8,128)(2,1)S(1)} %get-tuple-element.171), channel_id=1, source_target_pairs={{0,16},{4,20},{8,24},{12,28},{16,0},{20,4},{24,8},{28,12},{1,17},{... | collective-permute-start | bytes 294920 | tf_op jit(solution)/shard_map/ppermute | solution.py:191
  47.3 6.0 %collective-permute-start.20 = (bf16[64,768]{1,0:T(8,128)(2,1)S(1)}, bf16[64,768]{1,0:T(8,128)(2,1)S(1)}, u32[]{:S(2)}, u32[]{:S(2)}) collective-permute-start(bf16[64,768]{1,0:T(8,128)(2,1)S(1)} %get-tuple-element.172), channel_id=1, source_target_pairs={{0,24},{4,28},{8,16},{12,20},{16,8},{20,12},{24,0},{28,4},{1,25},{... | collective-permute-start | bytes 294920 | tf_op jit(solution)/shard_map/ppermute | solution.py:191
  71.3 7.2 %collective-permute-start.25 = (bf16[64,768]{1,0:T(8,128)(2,1)S(1)}, bf16[64,768]{1,0:T(8,128)(2,1)S(1)}, u32[]{:S(2)}, u32[]{:S(2)}) collective-permute-start(bf16[64,768]{1,0:T(8,128)(2,1)S(1)} %get-tuple-element.193), channel_id=1, source_target_pairs={{0,8},{4,12},{8,0},{12,4},{16,24},{20,28},{24,16},{28,20},{1,9},{5... | collective-permute-start | bytes 294920 | tf_op jit(solution)/shard_map/ppermute | solution.py:191
  72.3 6.7 %collective-permute-start.26 = (bf16[64,768]{1,0:T(8,128)(2,1)S(1)}, bf16[64,768]{1,0:T(8,128)(2,1)S(1)}, u32[]{:S(2)}, u32[]{:S(2)}) collective-permute-start(bf16[64,768]{1,0:T(8,128)(2,1)S(1)} %get-tuple-element.194), channel_id=1, source_target_pairs={{0,16},{4,20},{8,24},{12,28},{16,0},{20,4},{24,8},{28,12},{1,17},{... | collective-permute-start | bytes 294920 | tf_op jit(solution)/shard_map/ppermute | solution.py:191
  73.4 5.7 %collective-permute-start.27 = (bf16[64,768]{1,0:T(8,128)(2,1)S(1)}, bf16[64,768]{1,0:T(8,128)(2,1)S(1)}, u32[]{:S(2)}, u32[]{:S(2)}) collective-permute-start(bf16[64,768]{1,0:T(8,128)(2,1)S(1)} %get-tuple-element.195), channel_id=1, source_target_pairs={{0,24},{4,28},{8,16},{12,20},{16,8},{20,12},{24,0},{28,4},{1,25},{... | collective-permute-start | bytes 294920 | tf_op jit(solution)/shard_map/ppermute | solution.py:191
  80.1 6.5 %collective-permute-start.29 = (bf16[32,768]{1,0:T(8,128)(2,1)S(1)}, bf16[32,768]{1,0:T(8,128)(2,1)S(1)}, u32[]{:S(2)}, u32[]{:S(2)}) collective-permute-start(bf16[32,768]{1,0:T(8,128)(2,1)S(1)} %get-tuple-element.200), channel_id=1, source_target_pairs={{0,3},{1,2},{2,1},{3,0},{4,7},{5,6},{6,5},{7,4},{8,11},{9,10},{10,... | collective-permute-start | bytes 147464 | tf_op jit(solution)/shard_map/ppermute | solution.py:191
  82.5 5.7 %collective-permute-start.30 = (bf16[32,768]{1,0:T(8,128)(2,1)S(1)}, bf16[32,768]{1,0:T(8,128)(2,1)S(1)}, u32[]{:S(2)}, u32[]{:S(2)}) collective-permute-start(bf16[32,768]{1,0:T(8,128)(2,1)S(1)} %get-tuple-element.201), channel_id=1, source_target_pairs={{0,2},{1,3},{2,0},{3,1},{4,6},{5,7},{6,4},{7,5},{8,10},{9,11},{10,... | collective-permute-start | bytes 147464 | tf_op jit(solution)/shard_map/ppermute | solution.py:191
  82.5 5.7 %collective-permute-start.31 = (bf16[32,768]{1,0:T(8,128)(2,1)S(1)}, bf16[32,768]{1,0:T(8,128)(2,1)S(1)}, u32[]{:S(2)}, u32[]{:S(2)}) collective-permute-start(bf16[32,768]{1,0:T(8,128)(2,1)S(1)} %get-tuple-element.202), channel_id=1, source_target_pairs={{0,1},{1,0},{2,3},{3,2},{4,5},{5,4},{6,7},{7,6},{8,9},{9,8},{10,11... | collective-permute-start | bytes 147464 | tf_op jit(solution)/shard_map/ppermute | solution.py:191
  (11 other events, 63.8 us)

commit v4 on v3

--- a/solution.py
+++ b/solution.py
@@ -180,10 +180,11 @@
 VMEM_SPEC = pl.BlockSpec(memory_space=pltpu.VMEM)
 HBM_SPEC = pl.BlockSpec(memory_space=pl.ANY)
 SMALL_MIB = 12
-STAGE_AT = ((0, 1, 2), (3, 4), (5,), ())
-GATE_RING = 2
-DOWN_RING = 4
-EXPERTS_MIB = 27
+STAGE_AT = ((0, 1, 2), (4, 6), (3,), (7,), (5,))
+GATE_RING = 1
+DOWN_RING = 5
+DOWN_FLIGHT = 3
+EXPERTS_MIB = 19
 
 
 def swap(array, axis_name, mask):
@@ -395,6 +396,10 @@
         out_refs[k][...] = packed[expert_at(shape, lax.axis_index("ctx") ^ (2 * k))]
 
 
+def own_block(body):
+    pl.when(lax.axis_index("ctx") >= 0)(body)
+
+
 def block_rows(step, deep):
     return pl.ds(pl.multiple_of((lax.axis_index("ctx") ^ step) * deep, deep), deep)
 
@@ -451,35 +456,47 @@
     return squares, (wide * gain_ref[lax.axis_index("ctx") ^ step]).astype(BF16)
 
 
-def early_kernel(count, steps, *refs):
+def early_kernel(numbers, steps, *refs):
+    count, begun = len(numbers), 0 not in numbers
     row_refs, gain_ref, weight_refs, refs = refs[:count], refs[count], refs[count + 1 : 3 * count + 1], refs[3 * count + 1 :]
+    sums_in, refs = (refs[:3], refs[3:]) if begun else (None, refs)
     gate_hbm, up_hbm, gate_acc, up_acc, squares_ref = refs[:5]
-    copies = stage_copies(steps, gate_hbm, up_hbm, refs[5:-1], refs[-1]) if steps else []
+    scaled_ref = refs[-1]
+    copies = stage_copies(steps, gate_hbm, up_hbm, refs[5:-2], refs[-2]) if steps else []
     for copy in copies:
         copy.start()
-    squares = 0.0
-    for step in range(count):
-        more, rows = scaled_rows(row_refs[step], gain_ref, step)
+    squares = sums_in[2][:, 0:1] if begun else 0.0
+    for at, number in enumerate(numbers):
+        more, scaled_ref[at] = scaled_rows(row_refs[at], gain_ref, number)
         squares = squares + more
-        for acc, weights in ((gate_acc, weight_refs[2 * step]), (up_acc, weight_refs[2 * step + 1])):
-            term = jnp.dot(rows, weights[...], preferred_element_type=F32)
-            acc[...] = term if step == 0 else acc[...] + term
+    for at in range(count):
+
+        @own_block
+        def _():
+            for which, acc in enumerate((gate_acc, up_acc)):
+                term = jnp.dot(scaled_ref[at], weight_refs[2 * at + which][...], preferred_element_type=F32)
+                if at:
+                    term = acc[...] + term
+                elif begun:
+                    term = sums_in[which][...] + term
+                acc[...] = term
+
     squares_ref[...] = jnp.broadcast_to(squares, squares_ref.shape)
     for copy in copies:
         copy.wait()
 
 
-def experts_kernel(first, held, count, *refs):
-    own_rows = count - first
+def experts_kernel(numbers, held, count, *refs):
+    own_rows = len(numbers)
     row_refs, gain_ref = refs[:own_rows], refs[own_rows]
     weight_refs, refs = refs[own_rows + 1 : own_rows + 1 + 2 * held], refs[own_rows + 1 + 2 * held :]
     gate_in, up_in, squares_ref, gate_hbm, up_hbm, down_hbm, even_ref, odd_ref, act_ref = refs[:9]
-    gate_acc, up_acc, pair_acc, gate_buf, up_buf, down_buf, gate_sem, down_sem = refs[9:]
+    gate_acc, up_acc, pair_acc, scaled_ref, squares_acc, gate_buf, up_buf, down_buf, gate_sem, down_sem = refs[9:]
     own = lax.axis_index("ctx")
     half = count // 2
     deep = row_refs[0].shape[1]
     units = gate_acc.shape[1]
-    late = list(range(first + held, count))
+    late = numbers[held:]
     gate_ring, down_ring, down_rows = gate_buf.shape[0], down_buf.shape[0], down_buf.shape[1]
     parts = units // down_rows
 
@@ -497,45 +514,55 @@
     for at in range(min(gate_ring, len(late))):
         for copy in gate_copies(at):
             copy.start()
-    if len(late) <= gate_ring:
-        for copy in down[:down_ring]:
+    flight = min(DOWN_FLIGHT, down_ring - 1)
+    if not late:
+        for copy in down[:flight]:
             copy.start()
     squares = squares_ref[:, 0:1]
-    gate_acc[...] = gate_in[...]
-    up_acc[...] = up_in[...]
-    for step in range(first, count):
-        more, rows = scaled_rows(row_refs[step - first], gain_ref, step)
+    for order, number in enumerate(numbers):
+        more, scaled_ref[order] = scaled_rows(row_refs[order], gain_ref, number)
         squares = squares + more
-        if step < first + held:
-            gate_w, up_w = weight_refs[2 * (step - first)], weight_refs[2 * (step - first) + 1]
+    squares_acc[...] = jnp.broadcast_to(squares, squares_acc.shape)
+    for order, number in enumerate(numbers):
+        at = order - held
+        if at < 0:
+            gate_w, up_w = weight_refs[2 * order], weight_refs[2 * order + 1]
         else:
-            at = step - first - held
             for copy in gate_copies(at):
                 copy.wait()
             gate_w, up_w = gate_buf.at[at % gate_ring], up_buf.at[at % gate_ring]
-        gate_acc[...] += jnp.dot(rows, gate_w[...], preferred_element_type=F32)
-        up_acc[...] += jnp.dot(rows, up_w[...], preferred_element_type=F32)
-        if step >= first + held and at + gate_ring < len(late):
+
+        @own_block
+        def _():
+            for acc, start, weights in ((gate_acc, gate_in, gate_w), (up_acc, up_in, up_w)):
+                former = acc if order else start
+                acc[...] = former[...] + jnp.dot(scaled_ref[order], weights[...], preferred_element_type=F32)
+
+        if 0 <= at and at + gate_ring < len(late):
             for copy in gate_copies(at + gate_ring):
                 copy.start()
-            if at + gate_ring == len(late) - 1:
-                for copy in down[:down_ring]:
-                    copy.start()
-    rms = lax.rsqrt(squares / D + norm_eps)
+        elif late and at == len(late) - gate_ring - 1:
+            for copy in down[:flight]:
+                copy.start()
+    rms = lax.rsqrt(squares_acc[:, 0:1] / D + norm_eps)
     gate = rms * gate_acc[...]
     act_ref[...] = (gate / (1.0 + jnp.exp(-gate)) * (rms * up_acc[...])).astype(BF16)
     odd = own & 1
     for at, copy in enumerate(down):
         part = at % parts
         copy.wait()
-        term = jnp.dot(
-            act_ref[:, part * down_rows : (part + 1) * down_rows],
-            down_buf[at % down_ring],
-            preferred_element_type=F32,
-        )
-        pair_acc[...] = term if part == 0 else pair_acc[...] + term
-        if at + down_ring < len(down):
-            down[at + down_ring].start()
+        if at + flight < len(down):
+            down[at + flight].start()
+
+        @own_block
+        def _():
+            term = jnp.dot(
+                act_ref[:, part * down_rows : (part + 1) * down_rows],
+                down_buf[at % down_ring],
+                preferred_element_type=F32,
+            )
+            pair_acc[...] = term if part == 0 else pair_acc[...] + term
+
         if part == parts - 1:
             store_pair(pair_acc, even_ref.at[at // parts], odd_ref.at[at // parts], odd)
 
@@ -561,24 +588,29 @@
         copy.start()
     for part, copy in enumerate(copies):
         copy.wait()
-        term = jnp.dot(
-            act_ref[:, part * down_rows : (part + 1) * down_rows], down_buf[part], preferred_element_type=F32
-        )
-        pair_acc[...] = term if part == 0 else pair_acc[...] + term
+
+        @own_block
+        def _():
+            term = jnp.dot(
+                act_ref[:, part * down_rows : (part + 1) * down_rows], down_buf[part], preferred_element_type=F32
+            )
+            pair_acc[...] = term if part == 0 else pair_acc[...] + term
+
     store_pair(pair_acc, even_ref, odd_ref, lax.axis_index("ctx") & 1)
 
 
-def run_early(rows, gain, staged, steps, gate_proj, up_proj):
+def run_early(numbers, rows, gain, staged, sums, steps, gate_proj, up_proj):
     tokens, deep = rows[0].shape
     units = gate_proj.shape[2]
     acc = pltpu.VMEM((tokens, units), F32)
     outs = (acc, acc, pltpu.VMEM((tokens, 128), F32)) + (staged_like(steps, deep, units) if steps else ())
     return pl.pallas_call(
-        functools.partial(early_kernel, len(rows), steps),
+        functools.partial(early_kernel, numbers, steps),
         out_shape=outs,
-        in_specs=[VMEM_SPEC] * (len(rows) + 1 + len(staged)) + [HBM_SPEC] * 2,
+        in_specs=[VMEM_SPEC] * (len(rows) + 1 + len(staged) + len(sums)) + [HBM_SPEC] * 2,
         out_specs=(VMEM_SPEC,) * len(outs),
-        scratch_shapes=[pltpu.SemaphoreType.DMA((2 * len(steps),))] if steps else [],
+        scratch_shapes=([pltpu.SemaphoreType.DMA((2 * len(steps),))] if steps else [])
+        + [pltpu.VMEM((len(rows), tokens, deep), BF16)],
         compiler_params=pltpu.CompilerParams(vmem_limit_bytes=5 << 20),
         cost_estimate=pl.CostEstimate(
             flops=4 * tokens * deep * units * len(rows),
@@ -586,18 +618,18 @@
             transcendentals=0,
         ),
         name="early",
-    )(*rows, gain, *[in_vmem(array) for array in staged], gate_proj, up_proj)
-
-
-def run_experts(rows, first, gain, staged, sums, gate_proj, up_proj, down_proj):
+    )(*rows, gain, *[in_vmem(array) for array in staged], *sums, gate_proj, up_proj)
+
+
+def run_experts(numbers, rows, count, gain, staged, sums, gate_proj, up_proj, down_proj):
     tokens, deep = rows[0].shape
-    count = first + len(rows)
     units = gate_proj.shape[2]
     parts = 2
     weights = 2 * (2 * gate_proj.size + down_proj.size)
     pieces = like((count // 2 - 1, tokens, deep))
+    late_rows = deep if len(staged) < 2 * len(rows) else 16
     return pl.pallas_call(
-        functools.partial(experts_kernel, first, len(staged) // 2, count),
+        functools.partial(experts_kernel, numbers, len(staged) // 2, count),
         out_shape=(pieces, pieces, pltpu.VMEM((tokens, units), BF16)),
         in_specs=[VMEM_SPEC] * (len(rows) + 1 + len(staged) + 3) + [HBM_SPEC] * 3,
         out_specs=(VMEM_SPEC,) * 3,
@@ -605,8 +637,10 @@
             pltpu.VMEM((tokens, units), F32),
             pltpu.VMEM((tokens, units), F32),
             pltpu.VMEM((tokens, 2 * deep), F32),
-            pltpu.VMEM((GATE_RING, deep, units), BF16),
-            pltpu.VMEM((GATE_RING, deep, units), BF16),
+            pltpu.VMEM((len(rows), tokens, deep), BF16),
+            pltpu.VMEM((tokens, 128), F32),
+            pltpu.VMEM((GATE_RING, late_rows, units), BF16),
+            pltpu.VMEM((GATE_RING, late_rows, units), BF16),
             pltpu.VMEM((DOWN_RING, units // parts, 2 * deep), BF16),
             pltpu.SemaphoreType.DMA((2, GATE_RING)),
             pltpu.SemaphoreType.DMA((DOWN_RING,)),
@@ -735,13 +769,27 @@
         [pltpu.VMEM((per_row, capacity, d_local), BF16)],
     )
     even = [even[0]] + spread(even[1:], "ctx", 2)
-    first = [even[0], swap(even[0], "ctx", 1)]
-    sums = run_early(first, gain, staged[:4], STAGE_AT[3], gate_hbm, up_hbm)
+    numbered = [number for steps in STAGE_AT for number in steps]
+    odd = swap(even[0], "ctx", 1)
+    sums = run_early((0, 1), [even[0], odd], gain, staged[:4], (), STAGE_AT[3], gate_hbm, up_hbm)
     sums, even = lax.optimization_barrier((sums, even[1:]))
-    gate_sum, up_sum, squares, *more = sums
-    arrived = [array for piece in even for array in (piece, swap(piece, "ctx", 1))]
+    staged, sums = [*staged, *sums[3:]], sums[:3]
+    odd = [swap(piece, "ctx", 1) for piece in even]
+    held = {number: staged[2 * at : 2 * at + 2] for at, number in enumerate(numbered[: len(staged) // 2])}
+    numbers = tuple(range(2, ctx_count, 2))
+    *sums, gate_last, up_last = run_early(
+        numbers, even, gain, [array for number in numbers for array in held[number]], sums, STAGE_AT[4], gate_hbm, up_hbm
+    )
     out_even, out_odd, act = run_experts(
-        arrived, 2, gain, [*staged[4:], *more], (gate_sum, up_sum, squares), gate_hbm, up_hbm, down_hbm
+        tuple(range(3, ctx_count, 2)),
+        odd,
+        ctx_count,
+        gain,
+        [*held[3], gate_last, up_last, *held.get(7, ())],
+        sums,
+        gate_hbm,
+        up_hbm,
+        down_hbm,
     )
     pieces = device_call(
         pair_total_kernel,

time: 89 us -> 85.5 us (0.961)
  waiting for transfers between devices: 15.7 us -> 13.5 us
  Pallas kernels: 41.4 us -> 39.6 us
    ppermute x32, waiting for transfers between devices: 15.7 us -> 13.5 us  [swap(): return lax.ppermute(array, axis_name, [(i, i ^ mask) for i in range(count)])]
    pallas_call x2 -> x3, Pallas kernels: 16.7 us -> 15 us  [the longest x1 8.87 us: run_experts(): pl.pallas_call(functools.partial(experts_kernel, numbers, len(staged) //...]
  transfers between devices with their start and end apart: 32 -> 32, of which waited for: 15 -> 12; matrix products, arithmetic and copies ran while one was open for 0% -> 0% of each run, Pallas kernels for 25% -> 30%
where the time goes in v4:
time: 85.5 us; the launch traced here: 85.4 us
  Pallas kernels  39.6 us (46%)
  starting transfers between devices  31.9 us (37%)
  waiting for transfers between devices  13.5 us (16%)
    ppermute x32, starting transfers between devices, swap(): return lax.ppermute(array, axis_name, [(i, i ^ mask) for i in range(count)])  31.9 us
    pallas_call x4, Pallas kernels, stage(): pl.pallas_call(functools.partial(stage_kernel, steps), out_shape=staged_l...  15.9 us
    ppermute x32, waiting for transfers between devices, swap(): return lax.ppermute(array, axis_name, [(i, i ^ mask) for i in range(count)])  13.5 us
    pallas_call x1, Pallas kernels, run_experts(): pl.pallas_call(functools.partial(experts_kernel, numbers, len(staged) //...  8.87 us
    pallas_call x10, Pallas kernels, device_call(): pl.pallas_call(kernel, out_shape=outs, in_specs=specs or [VMEM_SPEC] * le...  8.78 us
    pallas_call x2, Pallas kernels, run_early(): pl.pallas_call(functools.partial(early_kernel, numbers, steps), out_shape...  6.12 us
  transfers between devices with their start and end apart: 32, of which 12 were waited for; matrix products, arithmetic and copies ran while one was open for 0% of the time, Pallas kernels for 30%

profile of v4, /device:TPU:0, one launch (start us, length us, event | category | flops | bytes accessed | tf_op | source)
XLA Modules:
  0.0 85.4 jit_solution(10941454403253203536)
XLA Ops:
  1.1 2.9 %collective-permute-start = (bf16[16,1536]{1,0:T(8,128)(2,1)}, bf16[16,1536]{1,0:T(8,128)(2,1)S(1)}, u32[]{:S(2)}, u32[]{:S(2)}) collective-permute-start(bf16[16,1536]{1,0:T(8,128)(2,1)} %refs_6_.1), channel_id=1, source_target_pairs={{0,8},{4,12},{8,0},{12,4},{16,24},{20,28},{24,16},{28,20},{1,9},{5... | collective-permute-start | bytes 147464 | tf_op jit(solution)/shard_map/ppermute | solution.py:192
  4.0 2.1 %collective-permute-start.2 = (bf16[16,1536]{1,0:T(8,128)(2,1)}, bf16[16,1536]{1,0:T(8,128)(2,1)S(1)}, u32[]{:S(2)}, u32[]{:S(2)}) collective-permute-start(bf16[16,1536]{1,0:T(8,128)(2,1)} %refs_6_.1), channel_id=1, source_target_pairs={{0,24},{4,28},{8,16},{12,20},{16,8},{20,12},{24,0},{28,4},{1,25},{... | collective-permute-start | bytes 147464 | tf_op jit(solution)/shard_map/ppermute | solution.py:192
  7.7 1.6 %collective-permute-done.2.refs_3_ = bf16[16,1536]{1,0:T(8,128)(2,1)S(1)} collective-permute-done((bf16[16,1536]{1,0:T(8,128)(2,1)}, bf16[16,1536]{1,0:T(8,128)(2,1)S(1)}, u32[]{:S(2)}, u32[]{:S(2)}) %collective-permute-start.2) | collective-permute-done | bytes 49184 | tf_op jit(solution)/shard_map/ppermute | solution.py:192
  10.4 2.1 %attention.1.refs_0_ = bf16[13,64,128]{2,1,0:T(8,128)(2,1)S(1)} custom-call(bf16[16,1536]{1,0:T(8,128)(2,1)S(1)} %get-tuple-element.118.refs_0_, bf16[16,1536]{1,0:T(8,128)(2,1)S(1)} %collective-permute-done.refs_1_, bf16[16,1536]{1,0:T(8,128)(2,1)S(1)} %collective-permute-done.1.refs_2_, bf16[16,1536]{1,0:T(8,128)(2,1)S(1)} %collective-permute-done.2.refs_3_, ...), custom_call_target="tpu_custom_call" | custom-call | flops 415236096 | bytes 1277952 | tf_op jit(solution)/shard_map/attention/pallas_call | solution.py:203
  12.5 1.5 %collective-permute-start.9 = (bf16[13,64,128]{2,1,0:T(8,128)(2,1)S(1)}, bf16[13,64,128]{2,1,0:T(8,128)(2,1)S(1)}, u32[]{:S(2)}, u32[]{:S(2)}) collective-permute-start(bf16[13,64,128]{2,1,0:T(8,128)(2,1)S(1)} %attention.1.refs_0_), channel_id=1, source_target_pairs={{0,24},{4,28},{8,16},{12,20},{16,8},{20,12},{24,0},{28,4},{1,25},{... | collective-permute-start | bytes 638984 | tf_op jit(solution)/shard_map/ppermute | solution.py:192
  16.4 7.2 %stage.5 = (bf16[768,2048]{1,0:T(8,128)(2,1)S(1)}, bf16[768,2048]{1,0:T(8,128)(2,1)S(1)}, bf16[768,2048]{1,0:T(8,128)(2,1)S(1)}, bf16[768,2048]{1,0:T(8,128)(2,1...) custom-call(bf16[1,6144,2048]{2,1,0:T(8,128)(2,1)} %refs_13_.3, ...), custom_call_target="tpu_custom_call" | custom-call | bytes 18874368 | tf_op jit(solution)/shard_map/stage/pallas_call | solution.py:438
  25.1 1.4 %collective-permute-done.10.pair_ref = bf16[64,1536]{1,0:T(8,128)(2,1)S(1)} collective-permute-done((bf16[64,1536]{1,0:T(8,128)(2,1)S(1)}, bf16[64,1536]{1,0:T(8,128)(2,1)S(1)}, u32[]{:S(2)}, u32[]{:S(2)}) %collective-permute-start.10) | collective-permute-done | bytes 196640 | tf_op jit(solution)/shard_map/ppermute | solution.py:192
  27.0 1.6 %collective-permute-start.11 = (bf16[32,768]{1,0:T(8,128)(2,1)S(1)}, bf16[32,768]{1,0:T(8,128)(2,1)S(1)}, u32[]{:S(2)}, u32[]{:S(2)}) collective-permute-start(bf16[32,768]{1,0:T(8,128)(2,1)S(1)} %get-tuple-element.158), channel_id=1, source_target_pairs={{0,1},{1,0},{2,3},{3,2},{4,5},{5,4},{6,7},{7,6},{8,9},{9,8},{10,11... | collective-permute-start | bytes 147464 | tf_op jit(solution)/shard_map/ppermute | solution.py:192
  28.6 2.6 %collective-permute-start.12 = (bf16[32,768]{1,0:T(8,128)(2,1)S(1)}, bf16[32,768]{1,0:T(8,128)(2,1)S(1)}, u32[]{:S(2)}, u32[]{:S(2)}) collective-permute-start(bf16[32,768]{1,0:T(8,128)(2,1)S(1)} %get-tuple-element.159), channel_id=1, source_target_pairs={{0,2},{1,3},{2,0},{3,1},{4,6},{5,7},{6,4},{7,5},{8,10},{9,11},{10,... | collective-permute-start | bytes 147464 | tf_op jit(solution)/shard_map/ppermute | solution.py:192
  31.5 4.7 %stage.6 = (bf16[768,2048]{1,0:T(8,128)(2,1)S(1)}, bf16[768,2048]{1,0:T(8,128)(2,1)S(1)}, bf16[768,2048]{1,0:T(8,128)(2,1)S(1)}, bf16[768,2048]{1,0:T(8,128)(2,1)S(1)}) custom-call(bf16[1,6144,2048]{2,1,0:T(8,128)(2,1)} %refs_13_.3, bf16[1,6144,2048]{2,1,0:T(8,128)(2,1)} %refs_14_.3), custom_call_target="tpu_custom_call" | custom-call | bytes 12582912 | tf_op jit(solution)/shard_map/stage/pallas_call | solution.py:438
  37.2 2.7 %collective-permute-start.16 = (bf16[32,768]{1,0:T(8,128)(2,1)S(1)}, bf16[32,768]{1,0:T(8,128)(2,1)S(1)}, u32[]{:S(2)}, u32[]{:S(2)}) collective-permute-start(bf16[32,768]{1,0:T(8,128)(2,1)S(1)} %hidden.1.refs_0_.refs_1_), channel_id=1, source_target_pairs={{0,3},{1,2},{2,1},{3,0},{4,7},{5,6},{6,5},{7,4},{8,11},{9,10},{10,... | collective-permute-start | bytes 147464 | tf_op jit(solution)/shard_map/ppermute | solution.py:192
  39.9 1.7 %collective-permute-start.14 = (bf16[32,768]{1,0:T(8,128)(2,1)S(1)}, bf16[32,768]{1,0:T(8,128)(2,1)S(1)}, u32[]{:S(2)}, u32[]{:S(2)}) collective-permute-start(bf16[32,768]{1,0:T(8,128)(2,1)S(1)} %hidden.1.refs_0_.refs_1_), channel_id=1, source_target_pairs={{0,1},{1,0},{2,3},{3,2},{4,5},{5,4},{6,7},{7,6},{8,9},{9,8},{10,11... | collective-permute-start | bytes 147464 | tf_op jit(solution)/shard_map/ppermute | solution.py:192
  41.6 2.9 %stage.7 = (bf16[768,2048]{1,0:T(8,128)(2,1)S(1)}, bf16[768,2048]{1,0:T(8,128)(2,1)S(1)}) custom-call(bf16[1,6144,2048]{2,1,0:T(8,128)(2,1)} %refs_13_.3, bf16[1,6144,2048]{2,1,0:T(8,128)(2,1)} %refs_14_.3), custom_call_target="tpu_custom_call" | custom-call | bytes 6291456 | tf_op jit(solution)/shard_map/stage/pallas_call | solution.py:438
  47.3 1.4 %collective-permute-start.20 = (bf16[64,768]{1,0:T(8,128)(2,1)S(1)}, bf16[64,768]{1,0:T(8,128)(2,1)S(1)}, u32[]{:S(2)}, u32[]{:S(2)}) collective-permute-start(bf16[64,768]{1,0:T(8,128)(2,1)S(1)} %get-tuple-element.183), channel_id=1, source_target_pairs={{0,24},{4,28},{8,16},{12,20},{16,8},{20,12},{24,0},{28,4},{1,25},{... | collective-permute-start | bytes 294920 | tf_op jit(solution)/shard_map/ppermute | solution.py:192
  48.8 2.9 %early.2 = (f32[64,2048]{1,0:T(8,128)S(1)}, f32[64,2048]{1,0:T(8,128)S(1)}, f32[64,128]{1,0:T(8,128)S(1)}, bf16[768,2048]{1,0:T(8,128)(2,1)S(1)}, bf16[768,2048]{1,0:T(8,128)(2,1)S(1)}) custom-call(bf16[64,768]{1,0:T(8,128)(2,1)S(1)} %get-tuple-element.170.refs_0_, bf16[64,768]{1,0:T(8,128)(2,1)S(1)} %collective-permute-done.17.refs_1_, ...), custom_call_target="tpu_custom_call" | custom-call | flops 805306368 | bytes 6291456 | tf_op jit(solution)/shard_map/early/pallas_call | solution.py:607
  51.7 1.6 %collective-permute-done.19.refs_1_ = bf16[64,768]{1,0:T(8,128)(2,1)S(1)} collective-permute-done((bf16[64,768]{1,0:T(8,128)(2,1)S(1)}, bf16[64,768]{1,0:T(8,128)(2,1)S(1)}, u32[]{:S(2)}, u32[]{:S(2)}) %collective-permute-start.19) | collective-permute-done | bytes 98336 | tf_op jit(solution)/shard_map/ppermute | solution.py:192
  53.9 3.2 %early.3 = (f32[64,2048]{1,0:T(8,128)S(1)}, f32[64,2048]{1,0:T(8,128)S(1)}, f32[64,128]{1,0:T(8,128)S(1)}, bf16[768,2048]{1,0:T(8,128)(2,1)S(1)}, bf16[768,2048]{1,0:T(8,128)(2,1)S(1)}) custom-call(bf16[64,768]{1,0:T(8,128)(2,1)S(1)} %collective-permute-done.18.refs_0_, bf16[64,768]{1,0:T(8,128)(2,1)S(1)} %collective-permute-done.19.refs_1_, ...), custom_call_target="tpu_custom_call" | custom-call | flops 1207959552 | bytes 6291456 | tf_op jit(solution)/shard_map/early/pallas_call | solution.py:607
  57.1 8.9 %experts.1 = (bf16[3,64,768]{2,1,0:T(8,128)(2,1)S(1)}, bf16[3,64,768]{2,1,0:T(8,128)(2,1)S(1)}, bf16[64,2048]{1,0:T(8,128)(2,1)S(1)}) custom-call(bf16[64,768]{1,0:T(8,128)(2,1)S(1)} %collective-permute-done.21.refs_0_, bf16[64,768]{1,0:T(8,128)(2,1)S(1)} %collective-permute-done.22.refs_1_, bf16[64,768]{1,0:T(8,128)(2,1)S(1)} %collective-permute-done.23.refs_2_, ...), custom_call_target="tpu_custom_call" | custom-call | flops 4831838208 | bytes 37748736 | tf_op jit(solution)/shard_map/experts/pallas_call | solution.py:631
  69.9 1.5 %collective-permute-start.27 = (bf16[64,768]{1,0:T(8,128)(2,1)S(1)}, bf16[64,768]{1,0:T(8,128)(2,1)S(1)}, u32[]{:S(2)}, u32[]{:S(2)}) collective-permute-start(bf16[64,768]{1,0:T(8,128)(2,1)S(1)} %get-tuple-element.213), channel_id=1, source_target_pairs={{0,24},{4,28},{8,16},{12,20},{16,8},{20,12},{24,0},{28,4},{1,25},{... | collective-permute-start | bytes 294920 | tf_op jit(solution)/shard_map/ppermute | solution.py:192
  71.4 3.5 %own_columns.1 = (bf16[64,768]{1,0:T(8,128)(2,1)S(1)}, bf16[64,768]{1,0:T(8,128)(2,1)S(1)}) custom-call(bf16[64,2048]{1,0:T(8,128)(2,1)S(1)} %get-tuple-element.214.act_ref, bf16[1,2048,6144]{2,1,0:T(8,128)(2,1)} %down_hbm.1), custom_call_target="tpu_custom_call" | custom-call | bytes 1 | tf_op jit(solution)/shard_map/own_columns/pallas_call | solution.py:203
  76.6 2.4 %collective-permute-start.29 = (bf16[32,768]{1,0:T(8,128)(2,1)S(1)}, bf16[32,768]{1,0:T(8,128)(2,1)S(1)}, u32[]{:S(2)}, u32[]{:S(2)}) collective-permute-start(bf16[32,768]{1,0:T(8,128)(2,1)S(1)} %get-tuple-element.218), channel_id=1, source_target_pairs={{0,3},{1,2},{2,1},{3,0},{4,7},{5,6},{6,5},{7,4},{8,11},{9,10},{10,... | collective-permute-start | bytes 147464 | tf_op jit(solution)/shard_map/ppermute | solution.py:192
  79.0 2.1 %collective-permute-start.31 = (bf16[32,768]{1,0:T(8,128)(2,1)S(1)}, bf16[32,768]{1,0:T(8,128)(2,1)S(1)}, u32[]{:S(2)}, u32[]{:S(2)}) collective-permute-start(bf16[32,768]{1,0:T(8,128)(2,1)S(1)} %get-tuple-element.220), channel_id=1, source_target_pairs={{0,1},{1,0},{2,3},{3,2},{4,5},{5,4},{6,7},{7,6},{8,9},{9,8},{10,11... | collective-permute-start | bytes 147464 | tf_op jit(solution)/shard_map/ppermute | solution.py:192
  81.1 2.1 %collective-permute-done.29.refs_2_ = bf16[32,768]{1,0:T(8,128)(2,1)S(1)} collective-permute-done((bf16[32,768]{1,0:T(8,128)(2,1)S(1)}, bf16[32,768]{1,0:T(8,128)(2,1)S(1)}, u32[]{:S(2)}, u32[]{:S(2)}) %collective-permute-start.29) | collective-permute-done | bytes 49184 | tf_op jit(solution)/shard_map/ppermute | solution.py:192
  83.2 1.5 %collective-permute-done.30.refs_3_ = bf16[32,768]{1,0:T(8,128)(2,1)S(1)} collective-permute-done((bf16[32,768]{1,0:T(8,128)(2,1)S(1)}, bf16[32,768]{1,0:T(8,128)(2,1)S(1)}, u32[]{:S(2)}, u32[]{:S(2)}) %collective-permute-start.30) | collective-permute-done | bytes 49184 | tf_op jit(solution)/shard_map/ppermute | solution.py:192
  (64 shorter events, 19.0 us)
Async XLA Ops:
  0.0 10.4 %collective-permute-start.3 = (bf16[2,512,128]{2,1,0:T(8,128)(2,1)}, bf16[2,512,128]{2,1,0:T(8,128)(2,1)S(1)}, u32[]{:S(2)}, u32[]{:S(2)}) collective-permute-start(bf16[2,512,128]{2,1,0:T(8,128)(2,1)} %refs_2_.2), channel_id=1, source_target_pairs={{0,4},{4,0},{8,12},{12,8},{16,20},{20,16},{24,28},{28,24},{1,5},{5... | collective-permute-start | bytes 786440 | tf_op jit(solution)/shard_map/ppermute | solution.py:192
  0.5 9.9 %collective-permute-start.4 = (bf16[2,512,128]{2,1,0:T(8,128)(2,1)}, bf16[2,512,128]{2,1,0:T(8,128)(2,1)S(1)}, u32[]{:S(2)}, u32[]{:S(2)}) collective-permute-start(bf16[2,512,128]{2,1,0:T(8,128)(2,1)} %refs_3_.2), channel_id=1, source_target_pairs={{0,4},{4,0},{8,12},{12,8},{16,20},{20,16},{24,28},{28,24},{1,5},{5... | collective-permute-start | bytes 786440 | tf_op jit(solution)/shard_map/ppermute | solution.py:192
  1.0 5.1 %collective-permute-start.6 = (bf16[2,16,128]{2,1,0:T(8,128)(2,1)}, bf16[2,16,128]{2,1,0:T(8,128)(2,1)S(1)}, u32[]{:S(2)}, u32[]{:S(2)}) collective-permute-start(bf16[2,16,128]{2,1,0:T(8,128)(2,1)} %refs_5_.1), channel_id=1, source_target_pairs={{0,4},{4,0},{8,12},{12,8},{16,20},{20,16},{24,28},{28,24},{1,5},{5... | collective-permute-start | bytes 24584 | tf_op jit(solution)/shard_map/ppermute | solution.py:192
  1.1 6.6 %collective-permute-start = (bf16[16,1536]{1,0:T(8,128)(2,1)}, bf16[16,1536]{1,0:T(8,128)(2,1)S(1)}, u32[]{:S(2)}, u32[]{:S(2)}) collective-permute-start(bf16[16,1536]{1,0:T(8,128)(2,1)} %refs_6_.1), channel_id=1, source_target_pairs={{0,8},{4,12},{8,0},{12,4},{16,24},{20,28},{24,16},{28,20},{1,9},{5... | collective-permute-start | bytes 147464 | tf_op jit(solution)/shard_map/ppermute | solution.py:192
  4.0 5.2 %collective-permute-start.2 = (bf16[16,1536]{1,0:T(8,128)(2,1)}, bf16[16,1536]{1,0:T(8,128)(2,1)S(1)}, u32[]{:S(2)}, u32[]{:S(2)}) collective-permute-start(bf16[16,1536]{1,0:T(8,128)(2,1)} %refs_6_.1), channel_id=1, source_target_pairs={{0,24},{4,28},{8,16},{12,20},{16,8},{20,12},{24,0},{28,4},{1,25},{... | collective-permute-start | bytes 147464 | tf_op jit(solution)/shard_map/ppermute | solution.py:192
  6.1 4.3 %collective-permute-start.1 = (bf16[16,1536]{1,0:T(8,128)(2,1)}, bf16[16,1536]{1,0:T(8,128)(2,1)S(1)}, u32[]{:S(2)}, u32[]{:S(2)}) collective-permute-start(bf16[16,1536]{1,0:T(8,128)(2,1)} %refs_6_.1), channel_id=1, source_target_pairs={{0,16},{4,20},{8,24},{12,28},{16,0},{20,4},{24,8},{28,12},{1,17},{... | collective-permute-start | bytes 147464 | tf_op jit(solution)/shard_map/ppermute | solution.py:192
  12.5 11.1 %collective-permute-start.9 = (bf16[13,64,128]{2,1,0:T(8,128)(2,1)S(1)}, bf16[13,64,128]{2,1,0:T(8,128)(2,1)S(1)}, u32[]{:S(2)}, u32[]{:S(2)}) collective-permute-start(bf16[13,64,128]{2,1,0:T(8,128)(2,1)S(1)} %attention.1.refs_0_), channel_id=1, source_target_pairs={{0,24},{4,28},{8,16},{12,20},{16,8},{20,12},{24,0},{28,4},{1,25},{... | collective-permute-start | bytes 638984 | tf_op jit(solution)/shard_map/ppermute | solution.py:192
  13.9 9.9 %collective-permute-start.8 = (bf16[13,64,128]{2,1,0:T(8,128)(2,1)S(1)}, bf16[13,64,128]{2,1,0:T(8,128)(2,1)S(1)}, u32[]{:S(2)}, u32[]{:S(2)}) collective-permute-start(bf16[13,64,128]{2,1,0:T(8,128)(2,1)S(1)} %attention.1.refs_0_), channel_id=1, source_target_pairs={{0,16},{4,20},{8,24},{12,28},{16,0},{20,4},{24,8},{28,12},{1,17},{... | collective-permute-start | bytes 638984 | tf_op jit(solution)/shard_map/ppermute | solution.py:192
  14.9 9.0 %collective-permute-start.7 = (bf16[13,64,128]{2,1,0:T(8,128)(2,1)S(1)}, bf16[13,64,128]{2,1,0:T(8,128)(2,1)S(1)}, u32[]{:S(2)}, u32[]{:S(2)}) collective-permute-start(bf16[13,64,128]{2,1,0:T(8,128)(2,1)S(1)} %attention.1.refs_0_), channel_id=1, source_target_pairs={{0,8},{4,12},{8,0},{12,4},{16,24},{20,28},{24,16},{28,20},{1,9},{5... | collective-permute-start | bytes 638984 | tf_op jit(solution)/shard_map/ppermute | solution.py:192
  27.0 9.2 %collective-permute-start.11 = (bf16[32,768]{1,0:T(8,128)(2,1)S(1)}, bf16[32,768]{1,0:T(8,128)(2,1)S(1)}, u32[]{:S(2)}, u32[]{:S(2)}) collective-permute-start(bf16[32,768]{1,0:T(8,128)(2,1)S(1)} %get-tuple-element.158), channel_id=1, source_target_pairs={{0,1},{1,0},{2,3},{3,2},{4,5},{5,4},{6,7},{7,6},{8,9},{9,8},{10,11... | collective-permute-start | bytes 147464 | tf_op jit(solution)/shard_map/ppermute | solution.py:192
  28.6 7.5 %collective-permute-start.12 = (bf16[32,768]{1,0:T(8,128)(2,1)S(1)}, bf16[32,768]{1,0:T(8,128)(2,1)S(1)}, u32[]{:S(2)}, u32[]{:S(2)}) collective-permute-start(bf16[32,768]{1,0:T(8,128)(2,1)S(1)} %get-tuple-element.159), channel_id=1, source_target_pairs={{0,2},{1,3},{2,0},{3,1},{4,6},{5,7},{6,4},{7,5},{8,10},{9,11},{10,... | collective-permute-start | bytes 147464 | tf_op jit(solution)/shard_map/ppermute | solution.py:192
  31.2 5.9 %collective-permute-start.13 = (bf16[32,768]{1,0:T(8,128)(2,1)S(1)}, bf16[32,768]{1,0:T(8,128)(2,1)S(1)}, u32[]{:S(2)}, u32[]{:S(2)}) collective-permute-start(bf16[32,768]{1,0:T(8,128)(2,1)S(1)} %get-tuple-element.160), channel_id=1, source_target_pairs={{0,3},{1,2},{2,1},{3,0},{4,7},{5,6},{6,5},{7,4},{8,11},{9,10},{10,... | collective-permute-start | bytes 147464 | tf_op jit(solution)/shard_map/ppermute | solution.py:192
  37.2 7.3 %collective-permute-start.16 = (bf16[32,768]{1,0:T(8,128)(2,1)S(1)}, bf16[32,768]{1,0:T(8,128)(2,1)S(1)}, u32[]{:S(2)}, u32[]{:S(2)}) collective-permute-start(bf16[32,768]{1,0:T(8,128)(2,1)S(1)} %hidden.1.refs_0_.refs_1_), channel_id=1, source_target_pairs={{0,3},{1,2},{2,1},{3,0},{4,7},{5,6},{6,5},{7,4},{8,11},{9,10},{10,... | collective-permute-start | bytes 147464 | tf_op jit(solution)/shard_map/ppermute | solution.py:192
  39.9 5.0 %collective-permute-start.15 = (bf16[32,768]{1,0:T(8,128)(2,1)S(1)}, bf16[32,768]{1,0:T(8,128)(2,1)S(1)}, u32[]{:S(2)}, u32[]{:S(2)}) collective-permute-start(bf16[32,768]{1,0:T(8,128)(2,1)S(1)} %hidden.1.refs_0_.refs_1_), channel_id=1, source_target_pairs={{0,2},{1,3},{2,0},{3,1},{4,6},{5,7},{6,4},{7,5},{8,10},{9,11},{10,... | collective-permute-start | bytes 147464 | tf_op jit(solution)/shard_map/ppermute | solution.py:192
  39.9 5.0 %collective-permute-start.14 = (bf16[32,768]{1,0:T(8,128)(2,1)S(1)}, bf16[32,768]{1,0:T(8,128)(2,1)S(1)}, u32[]{:S(2)}, u32[]{:S(2)}) collective-permute-start(bf16[32,768]{1,0:T(8,128)(2,1)S(1)} %hidden.1.refs_0_.refs_1_), channel_id=1, source_target_pairs={{0,1},{1,0},{2,3},{3,2},{4,5},{5,4},{6,7},{7,6},{8,9},{9,8},{10,11... | collective-permute-start | bytes 147464 | tf_op jit(solution)/shard_map/ppermute | solution.py:192
  45.2 6.5 %collective-permute-start.18 = (bf16[64,768]{1,0:T(8,128)(2,1)S(1)}, bf16[64,768]{1,0:T(8,128)(2,1)S(1)}, u32[]{:S(2)}, u32[]{:S(2)}) collective-permute-start(bf16[64,768]{1,0:T(8,128)(2,1)S(1)} %get-tuple-element.181), channel_id=1, source_target_pairs={{0,8},{4,12},{8,0},{12,4},{16,24},{20,28},{24,16},{28,20},{1,9},{5... | collective-permute-start | bytes 294920 | tf_op jit(solution)/shard_map/ppermute | solution.py:192
  46.4 7.0 %collective-permute-start.19 = (bf16[64,768]{1,0:T(8,128)(2,1)S(1)}, bf16[64,768]{1,0:T(8,128)(2,1)S(1)}, u32[]{:S(2)}, u32[]{:S(2)}) collective-permute-start(bf16[64,768]{1,0:T(8,128)(2,1)S(1)} %get-tuple-element.182), channel_id=1, source_target_pairs={{0,16},{4,20},{8,24},{12,28},{16,0},{20,4},{24,8},{28,12},{1,17},{... | collective-permute-start | bytes 294920 | tf_op jit(solution)/shard_map/ppermute | solution.py:192
  47.3 6.0 %collective-permute-start.20 = (bf16[64,768]{1,0:T(8,128)(2,1)S(1)}, bf16[64,768]{1,0:T(8,128)(2,1)S(1)}, u32[]{:S(2)}, u32[]{:S(2)}) collective-permute-start(bf16[64,768]{1,0:T(8,128)(2,1)S(1)} %get-tuple-element.183), channel_id=1, source_target_pairs={{0,24},{4,28},{8,16},{12,20},{16,8},{20,12},{24,0},{28,4},{1,25},{... | collective-permute-start | bytes 294920 | tf_op jit(solution)/shard_map/ppermute | solution.py:192
  67.8 7.2 %collective-permute-start.25 = (bf16[64,768]{1,0:T(8,128)(2,1)S(1)}, bf16[64,768]{1,0:T(8,128)(2,1)S(1)}, u32[]{:S(2)}, u32[]{:S(2)}) collective-permute-start(bf16[64,768]{1,0:T(8,128)(2,1)S(1)} %get-tuple-element.211), channel_id=1, source_target_pairs={{0,8},{4,12},{8,0},{12,4},{16,24},{20,28},{24,16},{28,20},{1,9},{5... | collective-permute-start | bytes 294920 | tf_op jit(solution)/shard_map/ppermute | solution.py:192
  68.8 6.9 %collective-permute-start.26 = (bf16[64,768]{1,0:T(8,128)(2,1)S(1)}, bf16[64,768]{1,0:T(8,128)(2,1)S(1)}, u32[]{:S(2)}, u32[]{:S(2)}) collective-permute-start(bf16[64,768]{1,0:T(8,128)(2,1)S(1)} %get-tuple-element.212), channel_id=1, source_target_pairs={{0,16},{4,20},{8,24},{12,28},{16,0},{20,4},{24,8},{28,12},{1,17},{... | collective-permute-start | bytes 294920 | tf_op jit(solution)/shard_map/ppermute | solution.py:192
  69.9 5.8 %collective-permute-start.27 = (bf16[64,768]{1,0:T(8,128)(2,1)S(1)}, bf16[64,768]{1,0:T(8,128)(2,1)S(1)}, u32[]{:S(2)}, u32[]{:S(2)}) collective-permute-start(bf16[64,768]{1,0:T(8,128)(2,1)S(1)} %get-tuple-element.213), channel_id=1, source_target_pairs={{0,24},{4,28},{8,16},{12,20},{16,8},{20,12},{24,0},{28,4},{1,25},{... | collective-permute-start | bytes 294920 | tf_op jit(solution)/shard_map/ppermute | solution.py:192
  76.6 6.5 %collective-permute-start.29 = (bf16[32,768]{1,0:T(8,128)(2,1)S(1)}, bf16[32,768]{1,0:T(8,128)(2,1)S(1)}, u32[]{:S(2)}, u32[]{:S(2)}) collective-permute-start(bf16[32,768]{1,0:T(8,128)(2,1)S(1)} %get-tuple-element.218), channel_id=1, source_target_pairs={{0,3},{1,2},{2,1},{3,0},{4,7},{5,6},{6,5},{7,4},{8,11},{9,10},{10,... | collective-permute-start | bytes 147464 | tf_op jit(solution)/shard_map/ppermute | solution.py:192
  79.0 5.7 %collective-permute-start.30 = (bf16[32,768]{1,0:T(8,128)(2,1)S(1)}, bf16[32,768]{1,0:T(8,128)(2,1)S(1)}, u32[]{:S(2)}, u32[]{:S(2)}) collective-permute-start(bf16[32,768]{1,0:T(8,128)(2,1)S(1)} %get-tuple-element.219), channel_id=1, source_target_pairs={{0,2},{1,3},{2,0},{3,1},{4,6},{5,7},{6,4},{7,5},{8,10},{9,11},{10,... | collective-permute-start | bytes 147464 | tf_op jit(solution)/shard_map/ppermute | solution.py:192
  79.0 5.7 %collective-permute-start.31 = (bf16[32,768]{1,0:T(8,128)(2,1)S(1)}, bf16[32,768]{1,0:T(8,128)(2,1)S(1)}, u32[]{:S(2)}, u32[]{:S(2)}) collective-permute-start(bf16[32,768]{1,0:T(8,128)(2,1)S(1)} %get-tuple-element.220), channel_id=1, source_target_pairs={{0,1},{1,0},{2,3},{3,2},{4,5},{5,4},{6,7},{7,6},{8,9},{9,8},{10,11... | collective-permute-start | bytes 147464 | tf_op jit(solution)/shard_map/ppermute | solution.py:192
  (11 other events, 70.6 us)

commit v5 on v4

--- a/solution.py
+++ b/solution.py
@@ -179,12 +179,9 @@
 F32 = jnp.float32
 VMEM_SPEC = pl.BlockSpec(memory_space=pltpu.VMEM)
 HBM_SPEC = pl.BlockSpec(memory_space=pl.ANY)
-SMALL_MIB = 12
+SMALL_MIB = 8
 STAGE_AT = ((0, 1, 2), (4, 6), (3,), (7,), (5,))
-GATE_RING = 1
-DOWN_RING = 5
-DOWN_FLIGHT = 3
-EXPERTS_MIB = 19
+EXPERTS_MIB = 12
 
 
 def swap(array, axis_name, mask):
@@ -486,85 +483,53 @@
         copy.wait()
 
 
-def experts_kernel(numbers, held, count, *refs):
-    own_rows = len(numbers)
-    row_refs, gain_ref = refs[:own_rows], refs[own_rows]
-    weight_refs, refs = refs[own_rows + 1 : own_rows + 1 + 2 * held], refs[own_rows + 1 + 2 * held :]
-    gate_in, up_in, squares_ref, gate_hbm, up_hbm, down_hbm, even_ref, odd_ref, act_ref = refs[:9]
-    gate_acc, up_acc, pair_acc, scaled_ref, squares_acc, gate_buf, up_buf, down_buf, gate_sem, down_sem = refs[9:]
-    own = lax.axis_index("ctx")
-    half = count // 2
-    deep = row_refs[0].shape[1]
-    units = gate_acc.shape[1]
-    late = numbers[held:]
-    gate_ring, down_ring, down_rows = gate_buf.shape[0], down_buf.shape[0], down_buf.shape[1]
-    parts = units // down_rows
-
-    def gate_copies(at):
-        rows, slot = block_rows(late[at], deep), at % gate_ring
-        return (
-            pltpu.make_async_copy(gate_hbm.at[0, rows, :], gate_buf.at[slot], gate_sem.at[0, slot]),
-            pltpu.make_async_copy(up_hbm.at[0, rows, :], up_buf.at[slot], gate_sem.at[1, slot]),
-        )
-
-    down = [
-        down_copy(down_hbm, down_buf.at[at % down_ring], down_sem.at[at % down_ring], 1 + at // parts, at % parts)
-        for at in range((half - 1) * parts)
+def experts_kernel(numbers, *refs):
+    count = len(numbers)
+    row_refs, gain_ref, weight_refs, refs = refs[:count], refs[count], refs[count + 1 : 3 * count + 1], refs[3 * count + 1 :]
+    gate_in, up_in, squares_ref, down_hbm, odd_ref, act_ref = refs[:6]
+    even_refs, (gate_acc, up_acc, scaled_ref, squares_acc, odd_buf, sem) = refs[6:-6], refs[-6:]
+    chips = len(even_refs)
+    deep = odd_ref.shape[2]
+    targets = [(2 * k + 3, odd_buf.at[k]) for k in range(chips)] + [(2 * k + 2, ref) for k, ref in enumerate(even_refs)]
+    copies = [
+        pltpu.make_async_copy(down_hbm.at[0, :, block_rows(number, deep)], target, sem.at[at])
+        for at, (number, target) in enumerate(targets)
     ]
-    for at in range(min(gate_ring, len(late))):
-        for copy in gate_copies(at):
-            copy.start()
-    flight = min(DOWN_FLIGHT, down_ring - 1)
-    if not late:
-        for copy in down[:flight]:
-            copy.start()
+    for copy in copies[:chips]:
+        copy.start()
     squares = squares_ref[:, 0:1]
     for order, number in enumerate(numbers):
         more, scaled_ref[order] = scaled_rows(row_refs[order], gain_ref, number)
         squares = squares + more
     squares_acc[...] = jnp.broadcast_to(squares, squares_acc.shape)
-    for order, number in enumerate(numbers):
-        at = order - held
-        if at < 0:
-            gate_w, up_w = weight_refs[2 * order], weight_refs[2 * order + 1]
-        else:
-            for copy in gate_copies(at):
-                copy.wait()
-            gate_w, up_w = gate_buf.at[at % gate_ring], up_buf.at[at % gate_ring]
+    for order in range(count):
 
         @own_block
         def _():
-            for acc, start, weights in ((gate_acc, gate_in, gate_w), (up_acc, up_in, up_w)):
+            for which, (acc, start) in enumerate(((gate_acc, gate_in), (up_acc, up_in))):
                 former = acc if order else start
+                weights = weight_refs[2 * order + which]
                 acc[...] = former[...] + jnp.dot(scaled_ref[order], weights[...], preferred_element_type=F32)
 
-        if 0 <= at and at + gate_ring < len(late):
-            for copy in gate_copies(at + gate_ring):
-                copy.start()
-        elif late and at == len(late) - gate_ring - 1:
-            for copy in down[:flight]:
-                copy.start()
+        for copy in copies[chips + order : chips + order + 1]:
+            copy.start()
     rms = lax.rsqrt(squares_acc[:, 0:1] / D + norm_eps)
     gate = rms * gate_acc[...]
     act_ref[...] = (gate / (1.0 + jnp.exp(-gate)) * (rms * up_acc[...])).astype(BF16)
-    odd = own & 1
-    for at, copy in enumerate(down):
-        part = at % parts
-        copy.wait()
-        if at + flight < len(down):
-            down[at + flight].start()
+    for k in range(chips):
+        copies[k].wait()
 
         @own_block
         def _():
-            term = jnp.dot(
-                act_ref[:, part * down_rows : (part + 1) * down_rows],
-                down_buf[at % down_ring],
-                preferred_element_type=F32,
-            )
-            pair_acc[...] = term if part == 0 else pair_acc[...] + term
-
-        if part == parts - 1:
-            store_pair(pair_acc, even_ref.at[at // parts], odd_ref.at[at // parts], odd)
+            odd_ref[k] = jnp.dot(act_ref[...], odd_buf[k], preferred_element_type=F32).astype(BF16)
+
+    for copy in copies[chips:]:
+        copy.wait()
+
+
+def even_columns_kernel(act_ref, *refs):
+    for k, weight_ref in enumerate(refs[:-1]):
+        refs[-1][k] = jnp.dot(act_ref[...], weight_ref[...], preferred_element_type=F32).astype(BF16)
 
 
 def down_copy(down_hbm, target, sem, chip, part):
@@ -621,34 +586,32 @@
     )(*rows, gain, *[in_vmem(array) for array in staged], *sums, gate_proj, up_proj)
 
 
-def run_experts(numbers, rows, count, gain, staged, sums, gate_proj, up_proj, down_proj):
+def run_experts(numbers, rows, gain, staged, sums, down_proj):
     tokens, deep = rows[0].shape
-    units = gate_proj.shape[2]
-    parts = 2
-    weights = 2 * (2 * gate_proj.size + down_proj.size)
-    pieces = like((count // 2 - 1, tokens, deep))
-    late_rows = deep if len(staged) < 2 * len(rows) else 16
+    units = down_proj.shape[1]
+    count = len(rows)
     return pl.pallas_call(
-        functools.partial(experts_kernel, numbers, len(staged) // 2, count),
-        out_shape=(pieces, pieces, pltpu.VMEM((tokens, units), BF16)),
-        in_specs=[VMEM_SPEC] * (len(rows) + 1 + len(staged) + 3) + [HBM_SPEC] * 3,
-        out_specs=(VMEM_SPEC,) * 3,
+        functools.partial(experts_kernel, numbers),
+        out_shape=(like((count, tokens, deep)), pltpu.VMEM((tokens, units), BF16))
+        + (pltpu.VMEM((units, deep), BF16),) * count,
+        in_specs=[VMEM_SPEC] * (3 * count + 1 + 3) + [HBM_SPEC],
+        out_specs=(VMEM_SPEC,) * (count + 2),
         scratch_shapes=[
             pltpu.VMEM((tokens, units), F32),
             pltpu.VMEM((tokens, units), F32),
-            pltpu.VMEM((tokens, 2 * deep), F32),
-            pltpu.VMEM((len(rows), tokens, deep), BF16),
+            pltpu.VMEM((count, tokens, deep), BF16),
             pltpu.VMEM((tokens, 128), F32),
-            pltpu.VMEM((GATE_RING, late_rows, units), BF16),
-            pltpu.VMEM((GATE_RING, late_rows, units), BF16),
-            pltpu.VMEM((DOWN_RING, units // parts, 2 * deep), BF16),
-            pltpu.SemaphoreType.DMA((2, GATE_RING)),
-            pltpu.SemaphoreType.DMA((DOWN_RING,)),
+            pltpu.VMEM((count, units, deep), BF16),
+            pltpu.SemaphoreType.DMA((2 * count,)),
         ],
         compiler_params=pltpu.CompilerParams(vmem_limit_bytes=EXPERTS_MIB << 20),
-        cost_estimate=pl.CostEstimate(flops=tokens * weights, bytes_accessed=weights // 2, transcendentals=tokens * units),
+        cost_estimate=pl.CostEstimate(
+            flops=6 * count * tokens * units * deep,
+            bytes_accessed=4 * count * units * deep,
+            transcendentals=tokens * units,
+        ),
         name="experts",
-    )(*rows, gain, *[in_vmem(array) for array in staged], *sums, gate_proj, up_proj, down_proj)
+    )(*rows, gain, *[in_vmem(array) for array in staged], *sums, down_proj)
 
 
 def pair_total_kernel(even_ref, other_ref, *out_refs):
@@ -658,7 +621,7 @@
 
 def combine_kernel(shape, high_ref, low_ref, *refs):
     half, mp_count = shape[0] // 2, shape[1]
-    piece_refs, even_ref, other_ref = refs[: half - 1], refs[half - 1], refs[half]
+    piece_refs, even_ref, other_ref = refs[: half - 1][::-1], refs[half - 1], refs[half]
     kept_ref, sent_refs = refs[half + 1], refs[half + 2 :]
     own_piece = (even_ref[...].astype(F32) + other_ref[...].astype(F32)).astype(BF16)
     pieces = jnp.concatenate([own_piece] + [ref[...] for ref in piece_refs], axis=0)
@@ -752,7 +715,8 @@
     arrived = spread(sent, "mp")
     gate_later, _ = lax.optimization_barrier((gate_proj, kept))
     more = stage(in_hbm(gate_later), up_hbm, d_local, STAGE_AT[1])
-    more, arrived = lax.optimization_barrier((more, arrived))
+    more, arrived = lax.optimization_barrier((more, arrived[::-1]))
+    arrived = arrived[::-1]
     staged = [*staged, *more]
     hidden = device_call(total_kernel, "hidden", block, [kept, residual] + arrived[::-1])
 
@@ -772,7 +736,8 @@
     numbered = [number for steps in STAGE_AT for number in steps]
     odd = swap(even[0], "ctx", 1)
     sums = run_early((0, 1), [even[0], odd], gain, staged[:4], (), STAGE_AT[3], gate_hbm, up_hbm)
-    sums, even = lax.optimization_barrier((sums, even[1:]))
+    sums, even = lax.optimization_barrier((sums, even[:0:-1]))
+    even = even[::-1]
     staged, sums = [*staged, *sums[3:]], sums[:3]
     odd = [swap(piece, "ctx", 1) for piece in even]
     held = {number: staged[2 * at : 2 * at + 2] for at, number in enumerate(numbered[: len(staged) // 2])}
@@ -780,16 +745,16 @@
     *sums, gate_last, up_last = run_early(
         numbers, even, gain, [array for number in numbers for array in held[number]], sums, STAGE_AT[4], gate_hbm, up_hbm
     )
-    out_even, out_odd, act = run_experts(
-        tuple(range(3, ctx_count, 2)),
-        odd,
-        ctx_count,
-        gain,
-        [*held[3], gate_last, up_last, *held.get(7, ())],
-        sums,
-        gate_hbm,
-        up_hbm,
-        down_hbm,
+    odd_numbers = tuple(range(3, ctx_count, 2))
+    held[5] = (gate_last, up_last)
+    out_odd, act, *even_weights = run_experts(
+        odd_numbers, odd, gain, [array for number in odd_numbers for array in held[number]], sums, down_hbm
+    )
+    out_even = device_call(
+        even_columns_kernel,
+        "even_columns",
+        like((half - 1, capacity, d_local)),
+        [in_vmem(array) for array in (act, *even_weights)],
     )
     pieces = device_call(
         pair_total_kernel,
@@ -812,7 +777,7 @@
         specs=[VMEM_SPEC, HBM_SPEC],
         moved=1,
     )
-    pieces = returned + [own_even, swap(own_odd, "ctx", 1)]
+    pieces = returned[::-1] + [own_even, swap(own_odd, "ctx", 1)]
     kept, *sent = device_call(
         functools.partial(combine_kernel, shape),
         "combine",

time: 85.5 us -> 84.1 us (0.984)
  waiting for transfers between devices: 13.5 us -> 12.4 us
    pallas_call x1, Pallas kernels: 8.87 us -> 6.89 us  [run_experts(): pl.pallas_call(functools.partial(experts_kernel, numbers), out_shape=(lik...]
    pallas_call x10 -> x11, Pallas kernels: 8.78 us -> 10.5 us  [device_call(): pl.pallas_call(kernel, out_shape=outs, in_specs=specs or [VMEM_SPEC] * le...]
    ppermute x32, waiting for transfers between devices: 13.5 us -> 12.4 us  [swap(): return lax.ppermute(array, axis_name, [(i, i ^ mask) for i in range(count)])]
  transfers between devices with their start and end apart: 32 -> 32, of which waited for: 12 -> 11; matrix products, arithmetic and copies ran while one was open for 0% -> 0% of each run, Pallas kernels for 30% -> 33%
where the time goes in v5:
time: 84.1 us; the launch traced here: 84 us
  Pallas kernels  39.4 us (47%)
  starting transfers between devices  31.9 us (38%)
  waiting for transfers between devices  12.4 us (15%)
    ppermute x32, starting transfers between devices, swap(): return lax.ppermute(array, axis_name, [(i, i ^ mask) for i in range(count)])  31.9 us
    pallas_call x4, Pallas kernels, stage(): pl.pallas_call(functools.partial(stage_kernel, steps), out_shape=staged_l...  15.9 us
    ppermute x32, waiting for transfers between devices, swap(): return lax.ppermute(array, axis_name, [(i, i ^ mask) for i in range(count)])  12.4 us
    pallas_call x11, Pallas kernels, device_call(): pl.pallas_call(kernel, out_shape=outs, in_specs=specs or [VMEM_SPEC] * le...  10.5 us
    pallas_call x1, Pallas kernels, run_experts(): pl.pallas_call(functools.partial(experts_kernel, numbers), out_shape=(lik...  6.89 us
    pallas_call x2, Pallas kernels, run_early(): pl.pallas_call(functools.partial(early_kernel, numbers, steps), out_shape...  6.12 us
  transfers between devices with their start and end apart: 32, of which 11 were waited for; matrix products, arithmetic and copies ran while one was open for 0% of the time, Pallas kernels for 33%

profile of v5, /device:TPU:0, one launch (start us, length us, event | category | flops | bytes accessed | tf_op | source)
XLA Modules:
  0.0 84.0 jit_solution(7053609387846808830)
XLA Ops:
  1.1 2.9 %collective-permute-start = (bf16[16,1536]{1,0:T(8,128)(2,1)}, bf16[16,1536]{1,0:T(8,128)(2,1)S(1)}, u32[]{:S(2)}, u32[]{:S(2)}) collective-permute-start(bf16[16,1536]{1,0:T(8,128)(2,1)} %refs_6_.1), channel_id=1, source_target_pairs={{0,8},{4,12},{8,0},{12,4},{16,24},{20,28},{24,16},{28,20},{1,9},{5... | collective-permute-start | bytes 147464 | tf_op jit(solution)/shard_map/ppermute | solution.py:189
  4.0 2.1 %collective-permute-start.2 = (bf16[16,1536]{1,0:T(8,128)(2,1)}, bf16[16,1536]{1,0:T(8,128)(2,1)S(1)}, u32[]{:S(2)}, u32[]{:S(2)}) collective-permute-start(bf16[16,1536]{1,0:T(8,128)(2,1)} %refs_6_.1), channel_id=1, source_target_pairs={{0,24},{4,28},{8,16},{12,20},{16,8},{20,12},{24,0},{28,4},{1,25},{... | collective-permute-start | bytes 147464 | tf_op jit(solution)/shard_map/ppermute | solution.py:189
  7.7 1.6 %collective-permute-done.2.refs_3_ = bf16[16,1536]{1,0:T(8,128)(2,1)S(1)} collective-permute-done((bf16[16,1536]{1,0:T(8,128)(2,1)}, bf16[16,1536]{1,0:T(8,128)(2,1)S(1)}, u32[]{:S(2)}, u32[]{:S(2)}) %collective-permute-start.2) | collective-permute-done | bytes 49184 | tf_op jit(solution)/shard_map/ppermute | solution.py:189
  10.4 2.1 %attention.1.refs_0_ = bf16[13,64,128]{2,1,0:T(8,128)(2,1)S(1)} custom-call(bf16[16,1536]{1,0:T(8,128)(2,1)S(1)} %get-tuple-element.120.refs_0_, bf16[16,1536]{1,0:T(8,128)(2,1)S(1)} %collective-permute-done.refs_1_, bf16[16,1536]{1,0:T(8,128)(2,1)S(1)} %collective-permute-done.1.refs_2_, bf16[16,1536]{1,0:T(8,128)(2,1)S(1)} %collective-permute-done.2.refs_3_, ...), custom_call_target="tpu_custom_call" | custom-call | flops 415236096 | bytes 1277952 | tf_op jit(solution)/shard_map/attention/pallas_call | solution.py:200
  12.5 1.5 %collective-permute-start.9 = (bf16[13,64,128]{2,1,0:T(8,128)(2,1)S(1)}, bf16[13,64,128]{2,1,0:T(8,128)(2,1)S(1)}, u32[]{:S(2)}, u32[]{:S(2)}) collective-permute-start(bf16[13,64,128]{2,1,0:T(8,128)(2,1)S(1)} %attention.1.refs_0_), channel_id=1, source_target_pairs={{0,24},{4,28},{8,16},{12,20},{16,8},{20,12},{24,0},{28,4},{1,25},{... | collective-permute-start | bytes 638984 | tf_op jit(solution)/shard_map/ppermute | solution.py:189
  16.4 7.2 %stage.5 = (bf16[768,2048]{1,0:T(8,128)(2,1)S(1)}, bf16[768,2048]{1,0:T(8,128)(2,1)S(1)}, bf16[768,2048]{1,0:T(8,128)(2,1)S(1)}, bf16[768,2048]{1,0:T(8,128)(2,1...) custom-call(bf16[1,6144,2048]{2,1,0:T(8,128)(2,1)} %refs_13_.2, ...), custom_call_target="tpu_custom_call" | custom-call | bytes 18874368 | tf_op jit(solution)/shard_map/stage/pallas_call | solution.py:435
  25.1 1.4 %collective-permute-done.10.pair_ref = bf16[64,1536]{1,0:T(8,128)(2,1)S(1)} collective-permute-done((bf16[64,1536]{1,0:T(8,128)(2,1)S(1)}, bf16[64,1536]{1,0:T(8,128)(2,1)S(1)}, u32[]{:S(2)}, u32[]{:S(2)}) %collective-permute-start.10) | collective-permute-done | bytes 196640 | tf_op jit(solution)/shard_map/ppermute | solution.py:189
  27.0 3.7 %collective-permute-start.11 = (bf16[32,768]{1,0:T(8,128)(2,1)S(1)}, bf16[32,768]{1,0:T(8,128)(2,1)S(1)}, u32[]{:S(2)}, u32[]{:S(2)}) collective-permute-start(bf16[32,768]{1,0:T(8,128)(2,1)S(1)} %get-tuple-element.160), channel_id=1, source_target_pairs={{0,3},{1,2},{2,1},{3,0},{4,7},{5,6},{6,5},{7,4},{8,11},{9,10},{10,... | collective-permute-start | bytes 147464 | tf_op jit(solution)/shard_map/ppermute | solution.py:189
  31.4 4.7 %stage.6 = (bf16[768,2048]{1,0:T(8,128)(2,1)S(1)}, bf16[768,2048]{1,0:T(8,128)(2,1)S(1)}, bf16[768,2048]{1,0:T(8,128)(2,1)S(1)}, bf16[768,2048]{1,0:T(8,128)(2,1)S(1)}) custom-call(bf16[1,6144,2048]{2,1,0:T(8,128)(2,1)} %refs_13_.2, bf16[1,6144,2048]{2,1,0:T(8,128)(2,1)} %refs_14_.1), custom_call_target="tpu_custom_call" | custom-call | bytes 12582912 | tf_op jit(solution)/shard_map/stage/pallas_call | solution.py:435
  36.2 3.7 %collective-permute-start.16 = (bf16[32,768]{1,0:T(8,128)(2,1)S(1)}, bf16[32,768]{1,0:T(8,128)(2,1)S(1)}, u32[]{:S(2)}, u32[]{:S(2)}) collective-permute-start(bf16[32,768]{1,0:T(8,128)(2,1)S(1)} %hidden.1.refs_0_.refs_1_), channel_id=1, source_target_pairs={{0,3},{1,2},{2,1},{3,0},{4,7},{5,6},{6,5},{7,4},{8,11},{9,10},{10,... | collective-permute-start | bytes 147464 | tf_op jit(solution)/shard_map/ppermute | solution.py:189
  40.7 2.9 %stage.7 = (bf16[768,2048]{1,0:T(8,128)(2,1)S(1)}, bf16[768,2048]{1,0:T(8,128)(2,1)S(1)}) custom-call(bf16[1,6144,2048]{2,1,0:T(8,128)(2,1)} %refs_13_.2, bf16[1,6144,2048]{2,1,0:T(8,128)(2,1)} %refs_14_.1), custom_call_target="tpu_custom_call" | custom-call | bytes 6291456 | tf_op jit(solution)/shard_map/stage/pallas_call | solution.py:435
  43.6 1.3 %collective-permute-done.15.refs_2_ = bf16[32,768]{1,0:T(8,128)(2,1)S(1)} collective-permute-done((bf16[32,768]{1,0:T(8,128)(2,1)S(1)}, bf16[32,768]{1,0:T(8,128)(2,1)S(1)}, u32[]{:S(2)}, u32[]{:S(2)}) %collective-permute-start.15) | collective-permute-done | bytes 49184 | tf_op jit(solution)/shard_map/ppermute | solution.py:189
  45.2 1.6 %collective-permute-start.18 = (bf16[64,768]{1,0:T(8,128)(2,1)S(1)}, bf16[64,768]{1,0:T(8,128)(2,1)S(1)}, u32[]{:S(2)}, u32[]{:S(2)}) collective-permute-start(bf16[64,768]{1,0:T(8,128)(2,1)S(1)} %get-tuple-element.183), channel_id=1, source_target_pairs={{0,24},{4,28},{8,16},{12,20},{16,8},{20,12},{24,0},{28,4},{1,25},{... | collective-permute-start | bytes 294920 | tf_op jit(solution)/shard_map/ppermute | solution.py:189
  48.8 2.9 %early.2 = (f32[64,2048]{1,0:T(8,128)S(1)}, f32[64,2048]{1,0:T(8,128)S(1)}, f32[64,128]{1,0:T(8,128)S(1)}, bf16[768,2048]{1,0:T(8,128)(2,1)S(1)}, bf16[768,2048]{1,0:T(8,128)(2,1)S(1)}) custom-call(bf16[64,768]{1,0:T(8,128)(2,1)S(1)} %get-tuple-element.172.refs_0_, bf16[64,768]{1,0:T(8,128)(2,1)S(1)} %collective-permute-done.17.refs_1_, ...), custom_call_target="tpu_custom_call" | custom-call | flops 805306368 | bytes 6291456 | tf_op jit(solution)/shard_map/early/pallas_call | solution.py:572
  51.8 1.7 %collective-permute-done.19.refs_1_ = bf16[64,768]{1,0:T(8,128)(2,1)S(1)} collective-permute-done((bf16[64,768]{1,0:T(8,128)(2,1)S(1)}, bf16[64,768]{1,0:T(8,128)(2,1)S(1)}, u32[]{:S(2)}, u32[]{:S(2)}) %collective-permute-start.19) | collective-permute-done | bytes 98336 | tf_op jit(solution)/shard_map/ppermute | solution.py:189
  54.0 3.2 %early.3 = (f32[64,2048]{1,0:T(8,128)S(1)}, f32[64,2048]{1,0:T(8,128)S(1)}, f32[64,128]{1,0:T(8,128)S(1)}, bf16[768,2048]{1,0:T(8,128)(2,1)S(1)}, bf16[768,2048]{1,0:T(8,128)(2,1)S(1)}) custom-call(bf16[64,768]{1,0:T(8,128)(2,1)S(1)} %collective-permute-done.20.refs_0_, bf16[64,768]{1,0:T(8,128)(2,1)S(1)} %collective-permute-done.19.refs_1_, ...), custom_call_target="tpu_custom_call" | custom-call | flops 1207959552 | bytes 6291456 | tf_op jit(solution)/shard_map/early/pallas_call | solution.py:572
  57.2 6.9 %experts.1 = (bf16[3,64,768]{2,1,0:T(8,128)(2,1)S(1)}, bf16[64,2048]{1,0:T(8,128)(2,1)S(1)}, bf16[2048,768]{1,0:T(8,128)(2,1)S(1)}, bf16[2048,768]{1,0:T(8,128)(2,1)S(1)}, bf16[2048,768]{1,0:T(8,128)(2,1)S(1)}) custom-call(bf16[64,768]{1,0:T(8,128)(2,1)S(1)} %collective-permute-done.21.refs_0_, bf16[64,768]{1,0:T(8,128)(2,1)S(1)} %collective-permute-done.22.refs_1_, ...), custom_call_target="tpu_custom_call" | custom-call | flops 1811939328 | bytes 18874368 | tf_op jit(solution)/shard_map/experts/pallas_call | solution.py:593
  64.7 1.7 %even_columns.1.even_ref = bf16[3,64,768]{2,1,0:T(8,128)(2,1)S(1)} custom-call(bf16[64,2048]{1,0:T(8,128)(2,1)S(1)} %get-tuple-element.218.act_ref, bf16[2048,768]{1,0:T(8,128)(2,1)S(1)} %get-tuple-element.208.refs_0_, bf16[2048,768]{1,0:T(8,128)(2,1)S(1)} %get-tuple-element.209.refs_1_, bf16[2048,768]{1,0:T(8,128)(2,1)S(1)} %get-tuple-element.210.refs_2_), custom_call_target="tpu_custom_call" | custom-call | bytes 9699328 | tf_op jit(solution)/shard_map/even_columns/pallas_call | solution.py:200
  66.5 1.6 %collective-permute-start.25 = (bf16[64,768]{1,0:T(8,128)(2,1)S(1)}, bf16[64,768]{1,0:T(8,128)(2,1)S(1)}, u32[]{:S(2)}, u32[]{:S(2)}) collective-permute-start(bf16[64,768]{1,0:T(8,128)(2,1)S(1)} %get-tuple-element.215), channel_id=1, source_target_pairs={{0,24},{4,28},{8,16},{12,20},{16,8},{20,12},{24,0},{28,4},{1,25},{... | collective-permute-start | bytes 294920 | tf_op jit(solution)/shard_map/ppermute | solution.py:189
  70.0 3.5 %own_columns.1 = (bf16[64,768]{1,0:T(8,128)(2,1)S(1)}, bf16[64,768]{1,0:T(8,128)(2,1)S(1)}) custom-call(bf16[64,2048]{1,0:T(8,128)(2,1)S(1)} %get-tuple-element.218.act_ref, bf16[1,2048,6144]{2,1,0:T(8,128)(2,1)} %down_hbm.1), custom_call_target="tpu_custom_call" | custom-call | bytes 1 | tf_op jit(solution)/shard_map/own_columns/pallas_call | solution.py:200
  75.3 2.4 %collective-permute-start.29 = (bf16[32,768]{1,0:T(8,128)(2,1)S(1)}, bf16[32,768]{1,0:T(8,128)(2,1)S(1)}, u32[]{:S(2)}, u32[]{:S(2)}) collective-permute-start(bf16[32,768]{1,0:T(8,128)(2,1)S(1)} %get-tuple-element.222), channel_id=1, source_target_pairs={{0,3},{1,2},{2,1},{3,0},{4,7},{5,6},{6,5},{7,4},{8,11},{9,10},{10,... | collective-permute-start | bytes 147464 | tf_op jit(solution)/shard_map/ppermute | solution.py:189
  77.7 2.1 %collective-permute-start.31 = (bf16[32,768]{1,0:T(8,128)(2,1)S(1)}, bf16[32,768]{1,0:T(8,128)(2,1)S(1)}, u32[]{:S(2)}, u32[]{:S(2)}) collective-permute-start(bf16[32,768]{1,0:T(8,128)(2,1)S(1)} %get-tuple-element.224), channel_id=1, source_target_pairs={{0,1},{1,0},{2,3},{3,2},{4,5},{5,4},{6,7},{7,6},{8,9},{9,8},{10,11... | collective-permute-start | bytes 147464 | tf_op jit(solution)/shard_map/ppermute | solution.py:189
  79.7 2.1 %collective-permute-done.29.refs_2_ = bf16[32,768]{1,0:T(8,128)(2,1)S(1)} collective-permute-done((bf16[32,768]{1,0:T(8,128)(2,1)S(1)}, bf16[32,768]{1,0:T(8,128)(2,1)S(1)}, u32[]{:S(2)}, u32[]{:S(2)}) %collective-permute-start.29) | collective-permute-done | bytes 49184 | tf_op jit(solution)/shard_map/ppermute | solution.py:189
  81.8 1.5 %collective-permute-done.30.refs_3_ = bf16[32,768]{1,0:T(8,128)(2,1)S(1)} collective-permute-done((bf16[32,768]{1,0:T(8,128)(2,1)S(1)}, bf16[32,768]{1,0:T(8,128)(2,1)S(1)}, u32[]{:S(2)}, u32[]{:S(2)}) %collective-permute-start.30) | collective-permute-done | bytes 49184 | tf_op jit(solution)/shard_map/ppermute | solution.py:189
  (65 shorter events, 17.7 us)
Async XLA Ops:
  0.0 10.4 %collective-permute-start.3 = (bf16[2,512,128]{2,1,0:T(8,128)(2,1)}, bf16[2,512,128]{2,1,0:T(8,128)(2,1)S(1)}, u32[]{:S(2)}, u32[]{:S(2)}) collective-permute-start(bf16[2,512,128]{2,1,0:T(8,128)(2,1)} %refs_2_.2), channel_id=1, source_target_pairs={{0,4},{4,0},{8,12},{12,8},{16,20},{20,16},{24,28},{28,24},{1,5},{5... | collective-permute-start | bytes 786440 | tf_op jit(solution)/shard_map/ppermute | solution.py:189
  0.5 9.9 %collective-permute-start.4 = (bf16[2,512,128]{2,1,0:T(8,128)(2,1)}, bf16[2,512,128]{2,1,0:T(8,128)(2,1)S(1)}, u32[]{:S(2)}, u32[]{:S(2)}) collective-permute-start(bf16[2,512,128]{2,1,0:T(8,128)(2,1)} %refs_3_.2), channel_id=1, source_target_pairs={{0,4},{4,0},{8,12},{12,8},{16,20},{20,16},{24,28},{28,24},{1,5},{5... | collective-permute-start | bytes 786440 | tf_op jit(solution)/shard_map/ppermute | solution.py:189
  1.0 5.1 %collective-permute-start.6 = (bf16[2,16,128]{2,1,0:T(8,128)(2,1)}, bf16[2,16,128]{2,1,0:T(8,128)(2,1)S(1)}, u32[]{:S(2)}, u32[]{:S(2)}) collective-permute-start(bf16[2,16,128]{2,1,0:T(8,128)(2,1)} %refs_5_.1), channel_id=1, source_target_pairs={{0,4},{4,0},{8,12},{12,8},{16,20},{20,16},{24,28},{28,24},{1,5},{5... | collective-permute-start | bytes 24584 | tf_op jit(solution)/shard_map/ppermute | solution.py:189
  1.1 6.6 %collective-permute-start = (bf16[16,1536]{1,0:T(8,128)(2,1)}, bf16[16,1536]{1,0:T(8,128)(2,1)S(1)}, u32[]{:S(2)}, u32[]{:S(2)}) collective-permute-start(bf16[16,1536]{1,0:T(8,128)(2,1)} %refs_6_.1), channel_id=1, source_target_pairs={{0,8},{4,12},{8,0},{12,4},{16,24},{20,28},{24,16},{28,20},{1,9},{5... | collective-permute-start | bytes 147464 | tf_op jit(solution)/shard_map/ppermute | solution.py:189
  4.0 5.2 %collective-permute-start.2 = (bf16[16,1536]{1,0:T(8,128)(2,1)}, bf16[16,1536]{1,0:T(8,128)(2,1)S(1)}, u32[]{:S(2)}, u32[]{:S(2)}) collective-permute-start(bf16[16,1536]{1,0:T(8,128)(2,1)} %refs_6_.1), channel_id=1, source_target_pairs={{0,24},{4,28},{8,16},{12,20},{16,8},{20,12},{24,0},{28,4},{1,25},{... | collective-permute-start | bytes 147464 | tf_op jit(solution)/shard_map/ppermute | solution.py:189
  6.1 4.3 %collective-permute-start.1 = (bf16[16,1536]{1,0:T(8,128)(2,1)}, bf16[16,1536]{1,0:T(8,128)(2,1)S(1)}, u32[]{:S(2)}, u32[]{:S(2)}) collective-permute-start(bf16[16,1536]{1,0:T(8,128)(2,1)} %refs_6_.1), channel_id=1, source_target_pairs={{0,16},{4,20},{8,24},{12,28},{16,0},{20,4},{24,8},{28,12},{1,17},{... | collective-permute-start | bytes 147464 | tf_op jit(solution)/shard_map/ppermute | solution.py:189
  12.5 11.1 %collective-permute-start.9 = (bf16[13,64,128]{2,1,0:T(8,128)(2,1)S(1)}, bf16[13,64,128]{2,1,0:T(8,128)(2,1)S(1)}, u32[]{:S(2)}, u32[]{:S(2)}) collective-permute-start(bf16[13,64,128]{2,1,0:T(8,128)(2,1)S(1)} %attention.1.refs_0_), channel_id=1, source_target_pairs={{0,24},{4,28},{8,16},{12,20},{16,8},{20,12},{24,0},{28,4},{1,25},{... | collective-permute-start | bytes 638984 | tf_op jit(solution)/shard_map/ppermute | solution.py:189
  13.9 9.9 %collective-permute-start.8 = (bf16[13,64,128]{2,1,0:T(8,128)(2,1)S(1)}, bf16[13,64,128]{2,1,0:T(8,128)(2,1)S(1)}, u32[]{:S(2)}, u32[]{:S(2)}) collective-permute-start(bf16[13,64,128]{2,1,0:T(8,128)(2,1)S(1)} %attention.1.refs_0_), channel_id=1, source_target_pairs={{0,16},{4,20},{8,24},{12,28},{16,0},{20,4},{24,8},{28,12},{1,17},{... | collective-permute-start | bytes 638984 | tf_op jit(solution)/shard_map/ppermute | solution.py:189
  14.9 9.0 %collective-permute-start.7 = (bf16[13,64,128]{2,1,0:T(8,128)(2,1)S(1)}, bf16[13,64,128]{2,1,0:T(8,128)(2,1)S(1)}, u32[]{:S(2)}, u32[]{:S(2)}) collective-permute-start(bf16[13,64,128]{2,1,0:T(8,128)(2,1)S(1)} %attention.1.refs_0_), channel_id=1, source_target_pairs={{0,8},{4,12},{8,0},{12,4},{16,24},{20,28},{24,16},{28,20},{1,9},{5... | collective-permute-start | bytes 638984 | tf_op jit(solution)/shard_map/ppermute | solution.py:189
  27.0 9.2 %collective-permute-start.11 = (bf16[32,768]{1,0:T(8,128)(2,1)S(1)}, bf16[32,768]{1,0:T(8,128)(2,1)S(1)}, u32[]{:S(2)}, u32[]{:S(2)}) collective-permute-start(bf16[32,768]{1,0:T(8,128)(2,1)S(1)} %get-tuple-element.160), channel_id=1, source_target_pairs={{0,3},{1,2},{2,1},{3,0},{4,7},{5,6},{6,5},{7,4},{8,11},{9,10},{10,... | collective-permute-start | bytes 147464 | tf_op jit(solution)/shard_map/ppermute | solution.py:189
  30.7 5.5 %collective-permute-start.12 = (bf16[32,768]{1,0:T(8,128)(2,1)S(1)}, bf16[32,768]{1,0:T(8,128)(2,1)S(1)}, u32[]{:S(2)}, u32[]{:S(2)}) collective-permute-start(bf16[32,768]{1,0:T(8,128)(2,1)S(1)} %get-tuple-element.161), channel_id=1, source_target_pairs={{0,2},{1,3},{2,0},{3,1},{4,6},{5,7},{6,4},{7,5},{8,10},{9,11},{10,... | collective-permute-start | bytes 147464 | tf_op jit(solution)/shard_map/ppermute | solution.py:189
  30.7 5.5 %collective-permute-start.13 = (bf16[32,768]{1,0:T(8,128)(2,1)S(1)}, bf16[32,768]{1,0:T(8,128)(2,1)S(1)}, u32[]{:S(2)}, u32[]{:S(2)}) collective-permute-start(bf16[32,768]{1,0:T(8,128)(2,1)S(1)} %get-tuple-element.162), channel_id=1, source_target_pairs={{0,1},{1,0},{2,3},{3,2},{4,5},{5,4},{6,7},{7,6},{8,9},{9,8},{10,11... | collective-permute-start | bytes 147464 | tf_op jit(solution)/shard_map/ppermute | solution.py:189
  36.2 7.3 %collective-permute-start.16 = (bf16[32,768]{1,0:T(8,128)(2,1)S(1)}, bf16[32,768]{1,0:T(8,128)(2,1)S(1)}, u32[]{:S(2)}, u32[]{:S(2)}) collective-permute-start(bf16[32,768]{1,0:T(8,128)(2,1)S(1)} %hidden.1.refs_0_.refs_1_), channel_id=1, source_target_pairs={{0,3},{1,2},{2,1},{3,0},{4,7},{5,6},{6,5},{7,4},{8,11},{9,10},{10,... | collective-permute-start | bytes 147464 | tf_op jit(solution)/shard_map/ppermute | solution.py:189
  39.9 5.0 %collective-permute-start.15 = (bf16[32,768]{1,0:T(8,128)(2,1)S(1)}, bf16[32,768]{1,0:T(8,128)(2,1)S(1)}, u32[]{:S(2)}, u32[]{:S(2)}) collective-permute-start(bf16[32,768]{1,0:T(8,128)(2,1)S(1)} %hidden.1.refs_0_.refs_1_), channel_id=1, source_target_pairs={{0,2},{1,3},{2,0},{3,1},{4,6},{5,7},{6,4},{7,5},{8,10},{9,11},{10,... | collective-permute-start | bytes 147464 | tf_op jit(solution)/shard_map/ppermute | solution.py:189
  39.9 5.0 %collective-permute-start.14 = (bf16[32,768]{1,0:T(8,128)(2,1)S(1)}, bf16[32,768]{1,0:T(8,128)(2,1)S(1)}, u32[]{:S(2)}, u32[]{:S(2)}) collective-permute-start(bf16[32,768]{1,0:T(8,128)(2,1)S(1)} %hidden.1.refs_0_.refs_1_), channel_id=1, source_target_pairs={{0,1},{1,0},{2,3},{3,2},{4,5},{5,4},{6,7},{7,6},{8,9},{9,8},{10,11... | collective-permute-start | bytes 147464 | tf_op jit(solution)/shard_map/ppermute | solution.py:189
  45.2 6.6 %collective-permute-start.18 = (bf16[64,768]{1,0:T(8,128)(2,1)S(1)}, bf16[64,768]{1,0:T(8,128)(2,1)S(1)}, u32[]{:S(2)}, u32[]{:S(2)}) collective-permute-start(bf16[64,768]{1,0:T(8,128)(2,1)S(1)} %get-tuple-element.183), channel_id=1, source_target_pairs={{0,24},{4,28},{8,16},{12,20},{16,8},{20,12},{24,0},{28,4},{1,25},{... | collective-permute-start | bytes 294920 | tf_op jit(solution)/shard_map/ppermute | solution.py:189
  46.8 6.7 %collective-permute-start.19 = (bf16[64,768]{1,0:T(8,128)(2,1)S(1)}, bf16[64,768]{1,0:T(8,128)(2,1)S(1)}, u32[]{:S(2)}, u32[]{:S(2)}) collective-permute-start(bf16[64,768]{1,0:T(8,128)(2,1)S(1)} %get-tuple-element.184), channel_id=1, source_target_pairs={{0,16},{4,20},{8,24},{12,28},{16,0},{20,4},{24,8},{28,12},{1,17},{... | collective-permute-start | bytes 294920 | tf_op jit(solution)/shard_map/ppermute | solution.py:189
  47.8 5.6 %collective-permute-start.20 = (bf16[64,768]{1,0:T(8,128)(2,1)S(1)}, bf16[64,768]{1,0:T(8,128)(2,1)S(1)}, u32[]{:S(2)}, u32[]{:S(2)}) collective-permute-start(bf16[64,768]{1,0:T(8,128)(2,1)S(1)} %get-tuple-element.185), channel_id=1, source_target_pairs={{0,8},{4,12},{8,0},{12,4},{16,24},{20,28},{24,16},{28,20},{1,9},{5... | collective-permute-start | bytes 294920 | tf_op jit(solution)/shard_map/ppermute | solution.py:189
  66.5 7.2 %collective-permute-start.25 = (bf16[64,768]{1,0:T(8,128)(2,1)S(1)}, bf16[64,768]{1,0:T(8,128)(2,1)S(1)}, u32[]{:S(2)}, u32[]{:S(2)}) collective-permute-start(bf16[64,768]{1,0:T(8,128)(2,1)S(1)} %get-tuple-element.215), channel_id=1, source_target_pairs={{0,24},{4,28},{8,16},{12,20},{16,8},{20,12},{24,0},{28,4},{1,25},{... | collective-permute-start | bytes 294920 | tf_op jit(solution)/shard_map/ppermute | solution.py:189
  68.1 6.2 %collective-permute-start.26 = (bf16[64,768]{1,0:T(8,128)(2,1)S(1)}, bf16[64,768]{1,0:T(8,128)(2,1)S(1)}, u32[]{:S(2)}, u32[]{:S(2)}) collective-permute-start(bf16[64,768]{1,0:T(8,128)(2,1)S(1)} %get-tuple-element.216), channel_id=1, source_target_pairs={{0,16},{4,20},{8,24},{12,28},{16,0},{20,4},{24,8},{28,12},{1,17},{... | collective-permute-start | bytes 294920 | tf_op jit(solution)/shard_map/ppermute | solution.py:189
  69.1 5.2 %collective-permute-start.27 = (bf16[64,768]{1,0:T(8,128)(2,1)S(1)}, bf16[64,768]{1,0:T(8,128)(2,1)S(1)}, u32[]{:S(2)}, u32[]{:S(2)}) collective-permute-start(bf16[64,768]{1,0:T(8,128)(2,1)S(1)} %get-tuple-element.217), channel_id=1, source_target_pairs={{0,8},{4,12},{8,0},{12,4},{16,24},{20,28},{24,16},{28,20},{1,9},{5... | collective-permute-start | bytes 294920 | tf_op jit(solution)/shard_map/ppermute | solution.py:189
  75.3 6.5 %collective-permute-start.29 = (bf16[32,768]{1,0:T(8,128)(2,1)S(1)}, bf16[32,768]{1,0:T(8,128)(2,1)S(1)}, u32[]{:S(2)}, u32[]{:S(2)}) collective-permute-start(bf16[32,768]{1,0:T(8,128)(2,1)S(1)} %get-tuple-element.222), channel_id=1, source_target_pairs={{0,3},{1,2},{2,1},{3,0},{4,7},{5,6},{6,5},{7,4},{8,11},{9,10},{10,... | collective-permute-start | bytes 147464 | tf_op jit(solution)/shard_map/ppermute | solution.py:189
  77.7 5.7 %collective-permute-start.30 = (bf16[32,768]{1,0:T(8,128)(2,1)S(1)}, bf16[32,768]{1,0:T(8,128)(2,1)S(1)}, u32[]{:S(2)}, u32[]{:S(2)}) collective-permute-start(bf16[32,768]{1,0:T(8,128)(2,1)S(1)} %get-tuple-element.223), channel_id=1, source_target_pairs={{0,2},{1,3},{2,0},{3,1},{4,6},{5,7},{6,4},{7,5},{8,10},{9,11},{10,... | collective-permute-start | bytes 147464 | tf_op jit(solution)/shard_map/ppermute | solution.py:189
  77.7 5.7 %collective-permute-start.31 = (bf16[32,768]{1,0:T(8,128)(2,1)S(1)}, bf16[32,768]{1,0:T(8,128)(2,1)S(1)}, u32[]{:S(2)}, u32[]{:S(2)}) collective-permute-start(bf16[32,768]{1,0:T(8,128)(2,1)S(1)} %get-tuple-element.224), channel_id=1, source_target_pairs={{0,1},{1,0},{2,3},{3,2},{4,5},{5,4},{6,7},{7,6},{8,9},{9,8},{10,11... | collective-permute-start | bytes 147464 | tf_op jit(solution)/shard_map/ppermute | solution.py:189
  (11 other events, 71.2 us)

commit v6 on v5

--- a/solution.py
+++ b/solution.py
@@ -180,7 +180,7 @@
 VMEM_SPEC = pl.BlockSpec(memory_space=pltpu.VMEM)
 HBM_SPEC = pl.BlockSpec(memory_space=pl.ANY)
 SMALL_MIB = 8
-STAGE_AT = ((0, 1, 2), (4, 6), (3,), (7,), (5,))
+STAGE_AT = ((0,), (1, 2, 4), (6,), (3,), (7,), (5,))
 EXPERTS_MIB = 12
 
 
@@ -528,40 +528,38 @@
 
 
 def even_columns_kernel(act_ref, *refs):
-    for k, weight_ref in enumerate(refs[:-1]):
-        refs[-1][k] = jnp.dot(act_ref[...], weight_ref[...], preferred_element_type=F32).astype(BF16)
-
-
-def down_copy(down_hbm, target, sem, chip, part):
-    rows, columns = target.shape
-    start = pl.multiple_of(((lax.axis_index("ctx") >> 1) ^ chip) * columns, columns)
-    return pltpu.make_async_copy(
-        down_hbm.at[0, part * rows : (part + 1) * rows, pl.ds(start, columns)], target, sem
-    )
-
-
-def store_pair(pair_acc, even_ref, odd_ref, odd):
-    deep = even_ref.shape[1]
-    even_ref[...] = pair_acc[:, pl.ds(pl.multiple_of(odd * deep, deep), deep)].astype(BF16)
-    odd_ref[...] = pair_acc[:, pl.ds(pl.multiple_of((1 - odd) * deep, deep), deep)].astype(BF16)
-
-
-def own_columns_kernel(act_ref, down_hbm, even_ref, odd_ref, pair_acc, down_buf, down_sem):
-    parts, down_rows = down_buf.shape[0], down_buf.shape[1]
-    copies = [down_copy(down_hbm, down_buf.at[part], down_sem.at[part], 0, part) for part in range(parts)]
+    weight_refs, (down_hbm, even_ref, odd_weight_ref, sem) = refs[:-4], refs[-4:]
+    copy = pltpu.make_async_copy(down_hbm.at[0, :, block_rows(1, odd_weight_ref.shape[1])], odd_weight_ref, sem)
+    copy.start()
+    for k, weight_ref in enumerate(weight_refs):
+
+        @own_block
+        def _():
+            even_ref[k] = jnp.dot(act_ref[...], weight_ref[...], preferred_element_type=F32).astype(BF16)
+
+    copy.wait()
+
+
+def own_columns_kernel(act_ref, odd_weight_ref, down_hbm, even_ref, odd_ref, even_weight, sem):
+    parts, rows = even_weight.shape[0], even_weight.shape[1]
+    columns = block_rows(0, even_weight.shape[2])
+    copies = [
+        pltpu.make_async_copy(down_hbm.at[0, part * rows : (part + 1) * rows, columns], even_weight.at[part], sem.at[part])
+        for part in range(parts)
+    ]
     for copy in copies:
         copy.start()
-    for part, copy in enumerate(copies):
+
+    @own_block
+    def _():
+        odd_ref[...] = jnp.dot(act_ref[...], odd_weight_ref[...], preferred_element_type=F32).astype(BF16)
+
+    total = 0.0
+    for copy in copies:
         copy.wait()
-
-        @own_block
-        def _():
-            term = jnp.dot(
-                act_ref[:, part * down_rows : (part + 1) * down_rows], down_buf[part], preferred_element_type=F32
-            )
-            pair_acc[...] = term if part == 0 else pair_acc[...] + term
-
-    store_pair(pair_acc, even_ref, odd_ref, lax.axis_index("ctx") & 1)
+    for part in range(parts):
+        total += jnp.dot(act_ref[:, part * rows : (part + 1) * rows], even_weight[part], preferred_element_type=F32)
+    even_ref[...] = total.astype(BF16)
 
 
 def run_early(numbers, rows, gain, staged, sums, steps, gate_proj, up_proj):
@@ -670,8 +668,9 @@
     blocks = [queries] + spread([queries] * (half - 1), "ctx", 2)
     own = [cache_keys, cache_values, new_keys, new_values]
     pair = [swap(array, "ctx", 1) for array in own]
-    held = stage(gate_hbm, up_hbm, d_local, (), *[in_hbm(array) for array in (*own, queries)])
+    held = stage(gate_hbm, up_hbm, d_local, STAGE_AT[0], *[in_hbm(array) for array in (*own, queries)])
     held, blocks[1:], pair = lax.optimization_barrier((held, blocks[1:], pair))
+    begun, held = held[: 2 * len(STAGE_AT[0])], held[2 * len(STAGE_AT[0]) :]
     mine = device_call(
         attention_kernel,
         "attention",
@@ -696,8 +695,9 @@
     gain = norm_gain.astype(F32).reshape(ctx_count, 1, d_local)
     gate_later, _ = lax.optimization_barrier((gate_proj, mine))
     *staged, out_proj, residual = stage(
-        in_hbm(gate_later), up_hbm, d_local, STAGE_AT[0], in_hbm(out_proj), in_hbm(residual)
-    )
+        in_hbm(gate_later), up_hbm, d_local, STAGE_AT[1], in_hbm(out_proj), in_hbm(residual)
+    )
+    staged = [*begun, *staged]
     pick, high, low, gain, staged, out_proj, residual, others = lax.optimization_barrier(
         (pick, high, low, gain, staged, out_proj, residual, others)
     )
@@ -714,7 +714,7 @@
     )
     arrived = spread(sent, "mp")
     gate_later, _ = lax.optimization_barrier((gate_proj, kept))
-    more = stage(in_hbm(gate_later), up_hbm, d_local, STAGE_AT[1])
+    more = stage(in_hbm(gate_later), up_hbm, d_local, STAGE_AT[2])
     more, arrived = lax.optimization_barrier((more, arrived[::-1]))
     arrived = arrived[::-1]
     staged = [*staged, *more]
@@ -722,7 +722,7 @@
 
     everyone = spread([hidden] * (mp_count - 1), "mp")
     gate_later, _ = lax.optimization_barrier((gate_proj, hidden))
-    more = stage(in_hbm(gate_later), up_hbm, d_local, STAGE_AT[2])
+    more = stage(in_hbm(gate_later), up_hbm, d_local, STAGE_AT[3])
     more, everyone = lax.optimization_barrier((more, everyone))
     staged, everyone = [*staged, *more], [hidden, *everyone]
     even = device_call(
@@ -735,7 +735,7 @@
     even = [even[0]] + spread(even[1:], "ctx", 2)
     numbered = [number for steps in STAGE_AT for number in steps]
     odd = swap(even[0], "ctx", 1)
-    sums = run_early((0, 1), [even[0], odd], gain, staged[:4], (), STAGE_AT[3], gate_hbm, up_hbm)
+    sums = run_early((0, 1), [even[0], odd], gain, staged[:4], (), STAGE_AT[4], gate_hbm, up_hbm)
     sums, even = lax.optimization_barrier((sums, even[:0:-1]))
     even = even[::-1]
     staged, sums = [*staged, *sums[3:]], sums[:3]
@@ -743,18 +743,21 @@
     held = {number: staged[2 * at : 2 * at + 2] for at, number in enumerate(numbered[: len(staged) // 2])}
     numbers = tuple(range(2, ctx_count, 2))
     *sums, gate_last, up_last = run_early(
-        numbers, even, gain, [array for number in numbers for array in held[number]], sums, STAGE_AT[4], gate_hbm, up_hbm
+        numbers, even, gain, [array for number in numbers for array in held[number]], sums, STAGE_AT[5], gate_hbm, up_hbm
     )
     odd_numbers = tuple(range(3, ctx_count, 2))
     held[5] = (gate_last, up_last)
     out_odd, act, *even_weights = run_experts(
         odd_numbers, odd, gain, [array for number in odd_numbers for array in held[number]], sums, down_hbm
     )
-    out_even = device_call(
+    out_even, odd_weight = device_call(
         even_columns_kernel,
         "even_columns",
-        like((half - 1, capacity, d_local)),
-        [in_vmem(array) for array in (act, *even_weights)],
+        (like((half - 1, capacity, d_local)), pltpu.VMEM((act.shape[1], d_local), BF16)),
+        [in_vmem(array) for array in (act, *even_weights)] + [down_hbm],
+        [pltpu.SemaphoreType.DMA(())],
+        specs=[VMEM_SPEC] * half + [HBM_SPEC],
+        moved=2 * act.shape[1] * d_local,
     )
     pieces = device_call(
         pair_total_kernel,
@@ -768,13 +771,9 @@
         own_columns_kernel,
         "own_columns",
         (like((capacity, d_local)),) * 2,
-        [act, down_hbm],
-        [
-            pltpu.VMEM((capacity, 2 * d_local), F32),
-            pltpu.VMEM((2, act.shape[1] // 2, 2 * d_local), BF16),
-            pltpu.SemaphoreType.DMA((2,)),
-        ],
-        specs=[VMEM_SPEC, HBM_SPEC],
+        [act, in_vmem(odd_weight), down_hbm],
+        [pltpu.VMEM((2, act.shape[1] // 2, d_local), BF16), pltpu.SemaphoreType.DMA((2,))],
+        specs=[VMEM_SPEC, VMEM_SPEC, HBM_SPEC],
         moved=1,
     )
     pieces = returned[::-1] + [own_even, swap(own_odd, "ctx", 1)]

time: 84.1 us -> 82.1 us (0.976)
  waiting for transfers between devices: 12.4 us -> 11 us
    ppermute x32, waiting for transfers between devices: 12.4 us -> 11 us  [swap(): return lax.ppermute(array, axis_name, [(i, i ^ mask) for i in range(count)])]
where the time goes in v6:
time: 82.1 us; the launch traced here: 82 us
  Pallas kernels  38.8 us (47%)
  starting transfers between devices  31.9 us (39%)
  waiting for transfers between devices  11 us (13%)
    ppermute x32, starting transfers between devices, swap(): return lax.ppermute(array, axis_name, [(i, i ^ mask) for i in range(count)])  31.9 us
    pallas_call x4, Pallas kernels, stage(): pl.pallas_call(functools.partial(stage_kernel, steps), out_shape=staged_l...  16.1 us
    ppermute x32, waiting for transfers between devices, swap(): return lax.ppermute(array, axis_name, [(i, i ^ mask) for i in range(count)])  11 us
    pallas_call x11, Pallas kernels, device_call(): pl.pallas_call(kernel, out_shape=outs, in_specs=specs or [VMEM_SPEC] * le...  9.71 us
    pallas_call x1, Pallas kernels, run_experts(): pl.pallas_call(functools.partial(experts_kernel, numbers), out_shape=(lik...  6.89 us
    pallas_call x2, Pallas kernels, run_early(): pl.pallas_call(functools.partial(early_kernel, numbers, steps), out_shape...  6.08 us
  transfers between devices with their start and end apart: 32, of which 11 were waited for; matrix products, arithmetic and copies ran while one was open for 0% of the time, Pallas kernels for 33%

profile of v6, /device:TPU:0, one launch (start us, length us, event | category | flops | bytes accessed | tf_op | source)
XLA Modules:
  0.0 82.0 jit_solution(7854786224436557267)
XLA Ops:
  1.1 2.9 %collective-permute-start = (bf16[16,1536]{1,0:T(8,128)(2,1)}, bf16[16,1536]{1,0:T(8,128)(2,1)S(1)}, u32[]{:S(2)}, u32[]{:S(2)}) collective-permute-start(bf16[16,1536]{1,0:T(8,128)(2,1)} %refs_6_.1), channel_id=1, source_target_pairs={{0,8},{4,12},{8,0},{12,4},{16,24},{20,28},{24,16},{28,20},{1,9},{5... | collective-permute-start | bytes 147464 | tf_op jit(solution)/shard_map/ppermute | solution.py:189
  4.0 2.1 %collective-permute-start.2 = (bf16[16,1536]{1,0:T(8,128)(2,1)}, bf16[16,1536]{1,0:T(8,128)(2,1)S(1)}, u32[]{:S(2)}, u32[]{:S(2)}) collective-permute-start(bf16[16,1536]{1,0:T(8,128)(2,1)} %refs_6_.1), channel_id=1, source_target_pairs={{0,24},{4,28},{8,16},{12,20},{16,8},{20,12},{24,0},{28,4},{1,25},{... | collective-permute-start | bytes 147464 | tf_op jit(solution)/shard_map/ppermute | solution.py:189
  6.6 3.1 %stage.4 = (bf16[768,2048]{1,0:T(8,128)(2,1)S(1)}, bf16[768,2048]{1,0:T(8,128)(2,1)S(1)}, bf16[2,512,128]{2,1,0:T(8,128)(2,1)S(1)}, bf16[2,512,128]{2,1,0:T(8,12...) custom-call(bf16[1,6144,2048]{2,1,0:T(8,128)(2,1)} %refs_13_.2, ...), custom_call_target="tpu_custom_call" | custom-call | bytes 6291456 | tf_op jit(solution)/shard_map/stage/pallas_call | solution.py:435
  10.4 2.1 %attention.1.refs_0_ = bf16[13,64,128]{2,1,0:T(8,128)(2,1)S(1)} custom-call(bf16[16,1536]{1,0:T(8,128)(2,1)S(1)} %get-tuple-element.126.refs_0_, bf16[16,1536]{1,0:T(8,128)(2,1)S(1)} %collective-permute-done.refs_1_, bf16[16,1536]{1,0:T(8,128)(2,1)S(1)} %collective-permute-done.1.refs_2_, bf16[16,1536]{1,0:T(8,128)(2,1)S(1)} %collective-permute-done.2.refs_3_, ...), custom_call_target="tpu_custom_call" | custom-call | flops 415236096 | bytes 1277952 | tf_op jit(solution)/shard_map/attention/pallas_call | solution.py:200
  12.5 1.5 %collective-permute-start.9 = (bf16[13,64,128]{2,1,0:T(8,128)(2,1)S(1)}, bf16[13,64,128]{2,1,0:T(8,128)(2,1)S(1)}, u32[]{:S(2)}, u32[]{:S(2)}) collective-permute-start(bf16[13,64,128]{2,1,0:T(8,128)(2,1)S(1)} %attention.1.refs_0_), channel_id=1, source_target_pairs={{0,24},{4,28},{8,16},{12,20},{16,8},{20,12},{24,0},{28,4},{1,25},{... | collective-permute-start | bytes 638984 | tf_op jit(solution)/shard_map/ppermute | solution.py:189
  16.4 7.2 %stage.5 = (bf16[768,2048]{1,0:T(8,128)(2,1)S(1)}, bf16[768,2048]{1,0:T(8,128)(2,1)S(1)}, bf16[768,2048]{1,0:T(8,128)(2,1)S(1)}, bf16[768,2048]{1,0:T(8,128)(2,1...) custom-call(bf16[1,6144,2048]{2,1,0:T(8,128)(2,1)} %refs_13_.2, ...), custom_call_target="tpu_custom_call" | custom-call | bytes 18874368 | tf_op jit(solution)/shard_map/stage/pallas_call | solution.py:435
  25.5 1.4 %collective-permute-done.10.pair_ref = bf16[64,1536]{1,0:T(8,128)(2,1)S(1)} collective-permute-done((bf16[64,1536]{1,0:T(8,128)(2,1)S(1)}, bf16[64,1536]{1,0:T(8,128)(2,1)S(1)}, u32[]{:S(2)}, u32[]{:S(2)}) %collective-permute-start.10) | collective-permute-done | bytes 196640 | tf_op jit(solution)/shard_map/ppermute | solution.py:189
  27.5 3.7 %collective-permute-start.11 = (bf16[32,768]{1,0:T(8,128)(2,1)S(1)}, bf16[32,768]{1,0:T(8,128)(2,1)S(1)}, u32[]{:S(2)}, u32[]{:S(2)}) collective-permute-start(bf16[32,768]{1,0:T(8,128)(2,1)S(1)} %get-tuple-element.166), channel_id=1, source_target_pairs={{0,3},{1,2},{2,1},{3,0},{4,7},{5,6},{6,5},{7,4},{8,11},{9,10},{10,... | collective-permute-start | bytes 147464 | tf_op jit(solution)/shard_map/ppermute | solution.py:189
  31.9 2.9 %stage.6 = (bf16[768,2048]{1,0:T(8,128)(2,1)S(1)}, bf16[768,2048]{1,0:T(8,128)(2,1)S(1)}) custom-call(bf16[1,6144,2048]{2,1,0:T(8,128)(2,1)} %refs_13_.2, bf16[1,6144,2048]{2,1,0:T(8,128)(2,1)} %refs_14_.1), custom_call_target="tpu_custom_call" | custom-call | bytes 6291456 | tf_op jit(solution)/shard_map/stage/pallas_call | solution.py:435
  36.1 2.4 %collective-permute-start.16 = (bf16[32,768]{1,0:T(8,128)(2,1)S(1)}, bf16[32,768]{1,0:T(8,128)(2,1)S(1)}, u32[]{:S(2)}, u32[]{:S(2)}) collective-permute-start(bf16[32,768]{1,0:T(8,128)(2,1)S(1)} %hidden.1.refs_0_.refs_1_), channel_id=1, source_target_pairs={{0,3},{1,2},{2,1},{3,0},{4,7},{5,6},{6,5},{7,4},{8,11},{9,10},{10,... | collective-permute-start | bytes 147464 | tf_op jit(solution)/shard_map/ppermute | solution.py:189
  38.6 2.0 %collective-permute-start.14 = (bf16[32,768]{1,0:T(8,128)(2,1)S(1)}, bf16[32,768]{1,0:T(8,128)(2,1)S(1)}, u32[]{:S(2)}, u32[]{:S(2)}) collective-permute-start(bf16[32,768]{1,0:T(8,128)(2,1)S(1)} %hidden.1.refs_0_.refs_1_), channel_id=1, source_target_pairs={{0,1},{1,0},{2,3},{3,2},{4,5},{5,4},{6,7},{7,6},{8,9},{9,8},{10,11... | collective-permute-start | bytes 147464 | tf_op jit(solution)/shard_map/ppermute | solution.py:189
  40.6 2.9 %stage.7 = (bf16[768,2048]{1,0:T(8,128)(2,1)S(1)}, bf16[768,2048]{1,0:T(8,128)(2,1)S(1)}) custom-call(bf16[1,6144,2048]{2,1,0:T(8,128)(2,1)} %refs_13_.2, bf16[1,6144,2048]{2,1,0:T(8,128)(2,1)} %refs_14_.1), custom_call_target="tpu_custom_call" | custom-call | bytes 6291456 | tf_op jit(solution)/shard_map/stage/pallas_call | solution.py:435
  44.1 1.4 %collective-permute-start.18 = (bf16[64,768]{1,0:T(8,128)(2,1)S(1)}, bf16[64,768]{1,0:T(8,128)(2,1)S(1)}, u32[]{:S(2)}, u32[]{:S(2)}) collective-permute-start(bf16[64,768]{1,0:T(8,128)(2,1)S(1)} %get-tuple-element.189), channel_id=1, source_target_pairs={{0,24},{4,28},{8,16},{12,20},{16,8},{20,12},{24,0},{28,4},{1,25},{... | collective-permute-start | bytes 294920 | tf_op jit(solution)/shard_map/ppermute | solution.py:189
  47.7 2.9 %early.2 = (f32[64,2048]{1,0:T(8,128)S(1)}, f32[64,2048]{1,0:T(8,128)S(1)}, f32[64,128]{1,0:T(8,128)S(1)}, bf16[768,2048]{1,0:T(8,128)(2,1)S(1)}, bf16[768,2048]{1,0:T(8,128)(2,1)S(1)}) custom-call(bf16[64,768]{1,0:T(8,128)(2,1)S(1)} %get-tuple-element.178.refs_0_, bf16[64,768]{1,0:T(8,128)(2,1)S(1)} %collective-permute-done.17.refs_1_, ...), custom_call_target="tpu_custom_call" | custom-call | flops 805306368 | bytes 6291456 | tf_op jit(solution)/shard_map/early/pallas_call | solution.py:570
  50.7 1.7 %collective-permute-done.19.refs_1_ = bf16[64,768]{1,0:T(8,128)(2,1)S(1)} collective-permute-done((bf16[64,768]{1,0:T(8,128)(2,1)S(1)}, bf16[64,768]{1,0:T(8,128)(2,1)S(1)}, u32[]{:S(2)}, u32[]{:S(2)}) %collective-permute-start.19) | collective-permute-done | bytes 98336 | tf_op jit(solution)/shard_map/ppermute | solution.py:189
  52.9 3.2 %early.3 = (f32[64,2048]{1,0:T(8,128)S(1)}, f32[64,2048]{1,0:T(8,128)S(1)}, f32[64,128]{1,0:T(8,128)S(1)}, bf16[768,2048]{1,0:T(8,128)(2,1)S(1)}, bf16[768,2048]{1,0:T(8,128)(2,1)S(1)}) custom-call(bf16[64,768]{1,0:T(8,128)(2,1)S(1)} %collective-permute-done.20.refs_0_, bf16[64,768]{1,0:T(8,128)(2,1)S(1)} %collective-permute-done.19.refs_1_, ...), custom_call_target="tpu_custom_call" | custom-call | flops 1207959552 | bytes 6291456 | tf_op jit(solution)/shard_map/early/pallas_call | solution.py:570
  56.1 6.9 %experts.1 = (bf16[3,64,768]{2,1,0:T(8,128)(2,1)S(1)}, bf16[64,2048]{1,0:T(8,128)(2,1)S(1)}, bf16[2048,768]{1,0:T(8,128)(2,1)S(1)}, bf16[2048,768]{1,0:T(8,128)(2,1)S(1)}, bf16[2048,768]{1,0:T(8,128)(2,1)S(1)}) custom-call(bf16[64,768]{1,0:T(8,128)(2,1)S(1)} %collective-permute-done.21.refs_0_, bf16[64,768]{1,0:T(8,128)(2,1)S(1)} %collective-permute-done.22.refs_1_, ...), custom_call_target="tpu_custom_call" | custom-call | flops 1811939328 | bytes 18874368 | tf_op jit(solution)/shard_map/experts/pallas_call | solution.py:591
  63.5 1.9 %even_columns.1 = (bf16[3,64,768]{2,1,0:T(8,128)(2,1)S(1)}, bf16[2048,768]{1,0:T(8,128)(2,1)S(1)}) custom-call(bf16[64,2048]{1,0:T(8,128)(2,1)S(1)} %get-tuple-element.225.act_ref, bf16[2048,768]{1,0:T(8,128)(2,1)S(1)} %get-tuple-element.214.refs_0_, bf16[2048,768]{1,0:T(8,128)(2,1)S(1)} %get-tuple-element.215.refs_1_, ...), custom_call_target="tpu_custom_call" | custom-call | bytes 3145728 | tf_op jit(solution)/shard_map/even_columns/pallas_call | solution.py:200
  65.5 1.4 %collective-permute-start.25 = (bf16[64,768]{1,0:T(8,128)(2,1)S(1)}, bf16[64,768]{1,0:T(8,128)(2,1)S(1)}, u32[]{:S(2)}, u32[]{:S(2)}) collective-permute-start(bf16[64,768]{1,0:T(8,128)(2,1)S(1)} %get-tuple-element.222), channel_id=1, source_target_pairs={{0,24},{4,28},{8,16},{12,20},{16,8},{20,12},{24,0},{28,4},{1,25},{... | collective-permute-start | bytes 294920 | tf_op jit(solution)/shard_map/ppermute | solution.py:189
  69.1 2.6 %own_columns.1 = (bf16[64,768]{1,0:T(8,128)(2,1)S(1)}, bf16[64,768]{1,0:T(8,128)(2,1)S(1)}) custom-call(bf16[64,2048]{1,0:T(8,128)(2,1)S(1)} %get-tuple-element.225.act_ref, bf16[2048,768]{1,0:T(8,128)(2,1)S(1)} %get-tuple-element.226.odd_weight_ref, bf16[1,2048,6144]{2,1,0:T(8,128)(2,1)} %down_hbm.1), custom_call_target="tpu_custom_call" | custom-call | bytes 1 | tf_op jit(solution)/shard_map/own_columns/pallas_call | solution.py:200
  73.7 2.2 %collective-permute-start.29 = (bf16[32,768]{1,0:T(8,128)(2,1)S(1)}, bf16[32,768]{1,0:T(8,128)(2,1)S(1)}, u32[]{:S(2)}, u32[]{:S(2)}) collective-permute-start(bf16[32,768]{1,0:T(8,128)(2,1)S(1)} %get-tuple-element.230), channel_id=1, source_target_pairs={{0,3},{1,2},{2,1},{3,0},{4,7},{5,6},{6,5},{7,4},{8,11},{9,10},{10,... | collective-permute-start | bytes 147464 | tf_op jit(solution)/shard_map/ppermute | solution.py:189
  76.1 2.0 %collective-permute-start.31 = (bf16[32,768]{1,0:T(8,128)(2,1)S(1)}, bf16[32,768]{1,0:T(8,128)(2,1)S(1)}, u32[]{:S(2)}, u32[]{:S(2)}) collective-permute-start(bf16[32,768]{1,0:T(8,128)(2,1)S(1)} %get-tuple-element.232), channel_id=1, source_target_pairs={{0,1},{1,0},{2,3},{3,2},{4,5},{5,4},{6,7},{7,6},{8,9},{9,8},{10,11... | collective-permute-start | bytes 147464 | tf_op jit(solution)/shard_map/ppermute | solution.py:189
  78.1 1.7 %collective-permute-done.29.refs_2_ = bf16[32,768]{1,0:T(8,128)(2,1)S(1)} collective-permute-done((bf16[32,768]{1,0:T(8,128)(2,1)S(1)}, bf16[32,768]{1,0:T(8,128)(2,1)S(1)}, u32[]{:S(2)}, u32[]{:S(2)}) %collective-permute-start.29) | collective-permute-done | bytes 49184 | tf_op jit(solution)/shard_map/ppermute | solution.py:189
  79.8 1.5 %collective-permute-done.30.refs_3_ = bf16[32,768]{1,0:T(8,128)(2,1)S(1)} collective-permute-done((bf16[32,768]{1,0:T(8,128)(2,1)S(1)}, bf16[32,768]{1,0:T(8,128)(2,1)S(1)}, u32[]{:S(2)}, u32[]{:S(2)}) %collective-permute-start.30) | collective-permute-done | bytes 49184 | tf_op jit(solution)/shard_map/ppermute | solution.py:189
  (65 shorter events, 18.4 us)
Async XLA Ops:
  0.0 10.4 %collective-permute-start.3 = (bf16[2,512,128]{2,1,0:T(8,128)(2,1)}, bf16[2,512,128]{2,1,0:T(8,128)(2,1)S(1)}, u32[]{:S(2)}, u32[]{:S(2)}) collective-permute-start(bf16[2,512,128]{2,1,0:T(8,128)(2,1)} %refs_2_.2), channel_id=1, source_target_pairs={{0,4},{4,0},{8,12},{12,8},{16,20},{20,16},{24,28},{28,24},{1,5},{5... | collective-permute-start | bytes 786440 | tf_op jit(solution)/shard_map/ppermute | solution.py:189
  0.5 9.9 %collective-permute-start.4 = (bf16[2,512,128]{2,1,0:T(8,128)(2,1)}, bf16[2,512,128]{2,1,0:T(8,128)(2,1)S(1)}, u32[]{:S(2)}, u32[]{:S(2)}) collective-permute-start(bf16[2,512,128]{2,1,0:T(8,128)(2,1)} %refs_3_.3), channel_id=1, source_target_pairs={{0,4},{4,0},{8,12},{12,8},{16,20},{20,16},{24,28},{28,24},{1,5},{5... | collective-permute-start | bytes 786440 | tf_op jit(solution)/shard_map/ppermute | solution.py:189
  1.0 5.1 %collective-permute-start.6 = (bf16[2,16,128]{2,1,0:T(8,128)(2,1)}, bf16[2,16,128]{2,1,0:T(8,128)(2,1)S(1)}, u32[]{:S(2)}, u32[]{:S(2)}) collective-permute-start(bf16[2,16,128]{2,1,0:T(8,128)(2,1)} %refs_5_.1), channel_id=1, source_target_pairs={{0,4},{4,0},{8,12},{12,8},{16,20},{20,16},{24,28},{28,24},{1,5},{5... | collective-permute-start | bytes 24584 | tf_op jit(solution)/shard_map/ppermute | solution.py:189
  1.1 8.6 %collective-permute-start = (bf16[16,1536]{1,0:T(8,128)(2,1)}, bf16[16,1536]{1,0:T(8,128)(2,1)S(1)}, u32[]{:S(2)}, u32[]{:S(2)}) collective-permute-start(bf16[16,1536]{1,0:T(8,128)(2,1)} %refs_6_.1), channel_id=1, source_target_pairs={{0,8},{4,12},{8,0},{12,4},{16,24},{20,28},{24,16},{28,20},{1,9},{5... | collective-permute-start | bytes 147464 | tf_op jit(solution)/shard_map/ppermute | solution.py:189
  4.0 5.7 %collective-permute-start.2 = (bf16[16,1536]{1,0:T(8,128)(2,1)}, bf16[16,1536]{1,0:T(8,128)(2,1)S(1)}, u32[]{:S(2)}, u32[]{:S(2)}) collective-permute-start(bf16[16,1536]{1,0:T(8,128)(2,1)} %refs_6_.1), channel_id=1, source_target_pairs={{0,24},{4,28},{8,16},{12,20},{16,8},{20,12},{24,0},{28,4},{1,25},{... | collective-permute-start | bytes 147464 | tf_op jit(solution)/shard_map/ppermute | solution.py:189
  6.1 4.3 %collective-permute-start.1 = (bf16[16,1536]{1,0:T(8,128)(2,1)}, bf16[16,1536]{1,0:T(8,128)(2,1)S(1)}, u32[]{:S(2)}, u32[]{:S(2)}) collective-permute-start(bf16[16,1536]{1,0:T(8,128)(2,1)} %refs_6_.1), channel_id=1, source_target_pairs={{0,16},{4,20},{8,24},{12,28},{16,0},{20,4},{24,8},{28,12},{1,17},{... | collective-permute-start | bytes 147464 | tf_op jit(solution)/shard_map/ppermute | solution.py:189
  12.5 11.1 %collective-permute-start.9 = (bf16[13,64,128]{2,1,0:T(8,128)(2,1)S(1)}, bf16[13,64,128]{2,1,0:T(8,128)(2,1)S(1)}, u32[]{:S(2)}, u32[]{:S(2)}) collective-permute-start(bf16[13,64,128]{2,1,0:T(8,128)(2,1)S(1)} %attention.1.refs_0_), channel_id=1, source_target_pairs={{0,24},{4,28},{8,16},{12,20},{16,8},{20,12},{24,0},{28,4},{1,25},{... | collective-permute-start | bytes 638984 | tf_op jit(solution)/shard_map/ppermute | solution.py:189
  13.9 10.4 %collective-permute-start.8 = (bf16[13,64,128]{2,1,0:T(8,128)(2,1)S(1)}, bf16[13,64,128]{2,1,0:T(8,128)(2,1)S(1)}, u32[]{:S(2)}, u32[]{:S(2)}) collective-permute-start(bf16[13,64,128]{2,1,0:T(8,128)(2,1)S(1)} %attention.1.refs_0_), channel_id=1, source_target_pairs={{0,16},{4,20},{8,24},{12,28},{16,0},{20,4},{24,8},{28,12},{1,17},{... | collective-permute-start | bytes 638984 | tf_op jit(solution)/shard_map/ppermute | solution.py:189
  14.9 9.4 %collective-permute-start.7 = (bf16[13,64,128]{2,1,0:T(8,128)(2,1)S(1)}, bf16[13,64,128]{2,1,0:T(8,128)(2,1)S(1)}, u32[]{:S(2)}, u32[]{:S(2)}) collective-permute-start(bf16[13,64,128]{2,1,0:T(8,128)(2,1)S(1)} %attention.1.refs_0_), channel_id=1, source_target_pairs={{0,8},{4,12},{8,0},{12,4},{16,24},{20,28},{24,16},{28,20},{1,9},{5... | collective-permute-start | bytes 638984 | tf_op jit(solution)/shard_map/ppermute | solution.py:189
  27.5 7.3 %collective-permute-start.11 = (bf16[32,768]{1,0:T(8,128)(2,1)S(1)}, bf16[32,768]{1,0:T(8,128)(2,1)S(1)}, u32[]{:S(2)}, u32[]{:S(2)}) collective-permute-start(bf16[32,768]{1,0:T(8,128)(2,1)S(1)} %get-tuple-element.166), channel_id=1, source_target_pairs={{0,3},{1,2},{2,1},{3,0},{4,7},{5,6},{6,5},{7,4},{8,11},{9,10},{10,... | collective-permute-start | bytes 147464 | tf_op jit(solution)/shard_map/ppermute | solution.py:189
  31.1 5.0 %collective-permute-start.12 = (bf16[32,768]{1,0:T(8,128)(2,1)S(1)}, bf16[32,768]{1,0:T(8,128)(2,1)S(1)}, u32[]{:S(2)}, u32[]{:S(2)}) collective-permute-start(bf16[32,768]{1,0:T(8,128)(2,1)S(1)} %get-tuple-element.167), channel_id=1, source_target_pairs={{0,2},{1,3},{2,0},{3,1},{4,6},{5,7},{6,4},{7,5},{8,10},{9,11},{10,... | collective-permute-start | bytes 147464 | tf_op jit(solution)/shard_map/ppermute | solution.py:189
  31.1 5.0 %collective-permute-start.13 = (bf16[32,768]{1,0:T(8,128)(2,1)S(1)}, bf16[32,768]{1,0:T(8,128)(2,1)S(1)}, u32[]{:S(2)}, u32[]{:S(2)}) collective-permute-start(bf16[32,768]{1,0:T(8,128)(2,1)S(1)} %get-tuple-element.168), channel_id=1, source_target_pairs={{0,1},{1,0},{2,3},{3,2},{4,5},{5,4},{6,7},{7,6},{8,9},{9,8},{10,11... | collective-permute-start | bytes 147464 | tf_op jit(solution)/shard_map/ppermute | solution.py:189
  36.1 7.3 %collective-permute-start.16 = (bf16[32,768]{1,0:T(8,128)(2,1)S(1)}, bf16[32,768]{1,0:T(8,128)(2,1)S(1)}, u32[]{:S(2)}, u32[]{:S(2)}) collective-permute-start(bf16[32,768]{1,0:T(8,128)(2,1)S(1)} %hidden.1.refs_0_.refs_1_), channel_id=1, source_target_pairs={{0,3},{1,2},{2,1},{3,0},{4,7},{5,6},{6,5},{7,4},{8,11},{9,10},{10,... | collective-permute-start | bytes 147464 | tf_op jit(solution)/shard_map/ppermute | solution.py:189
  38.5 5.3 %collective-permute-start.15 = (bf16[32,768]{1,0:T(8,128)(2,1)S(1)}, bf16[32,768]{1,0:T(8,128)(2,1)S(1)}, u32[]{:S(2)}, u32[]{:S(2)}) collective-permute-start(bf16[32,768]{1,0:T(8,128)(2,1)S(1)} %hidden.1.refs_0_.refs_1_), channel_id=1, source_target_pairs={{0,2},{1,3},{2,0},{3,1},{4,6},{5,7},{6,4},{7,5},{8,10},{9,11},{10,... | collective-permute-start | bytes 147464 | tf_op jit(solution)/shard_map/ppermute | solution.py:189
  38.6 5.2 %collective-permute-start.14 = (bf16[32,768]{1,0:T(8,128)(2,1)S(1)}, bf16[32,768]{1,0:T(8,128)(2,1)S(1)}, u32[]{:S(2)}, u32[]{:S(2)}) collective-permute-start(bf16[32,768]{1,0:T(8,128)(2,1)S(1)} %hidden.1.refs_0_.refs_1_), channel_id=1, source_target_pairs={{0,1},{1,0},{2,3},{3,2},{4,5},{5,4},{6,7},{7,6},{8,9},{9,8},{10,11... | collective-permute-start | bytes 147464 | tf_op jit(solution)/shard_map/ppermute | solution.py:189
  44.1 6.6 %collective-permute-start.18 = (bf16[64,768]{1,0:T(8,128)(2,1)S(1)}, bf16[64,768]{1,0:T(8,128)(2,1)S(1)}, u32[]{:S(2)}, u32[]{:S(2)}) collective-permute-start(bf16[64,768]{1,0:T(8,128)(2,1)S(1)} %get-tuple-element.189), channel_id=1, source_target_pairs={{0,24},{4,28},{8,16},{12,20},{16,8},{20,12},{24,0},{28,4},{1,25},{... | collective-permute-start | bytes 294920 | tf_op jit(solution)/shard_map/ppermute | solution.py:189
  45.5 6.8 %collective-permute-start.19 = (bf16[64,768]{1,0:T(8,128)(2,1)S(1)}, bf16[64,768]{1,0:T(8,128)(2,1)S(1)}, u32[]{:S(2)}, u32[]{:S(2)}) collective-permute-start(bf16[64,768]{1,0:T(8,128)(2,1)S(1)} %get-tuple-element.190), channel_id=1, source_target_pairs={{0,16},{4,20},{8,24},{12,28},{16,0},{20,4},{24,8},{28,12},{1,17},{... | collective-permute-start | bytes 294920 | tf_op jit(solution)/shard_map/ppermute | solution.py:189
  46.6 5.7 %collective-permute-start.20 = (bf16[64,768]{1,0:T(8,128)(2,1)S(1)}, bf16[64,768]{1,0:T(8,128)(2,1)S(1)}, u32[]{:S(2)}, u32[]{:S(2)}) collective-permute-start(bf16[64,768]{1,0:T(8,128)(2,1)S(1)} %get-tuple-element.191), channel_id=1, source_target_pairs={{0,8},{4,12},{8,0},{12,4},{16,24},{20,28},{24,16},{28,20},{1,9},{5... | collective-permute-start | bytes 294920 | tf_op jit(solution)/shard_map/ppermute | solution.py:189
  65.5 6.5 %collective-permute-start.25 = (bf16[64,768]{1,0:T(8,128)(2,1)S(1)}, bf16[64,768]{1,0:T(8,128)(2,1)S(1)}, u32[]{:S(2)}, u32[]{:S(2)}) collective-permute-start(bf16[64,768]{1,0:T(8,128)(2,1)S(1)} %get-tuple-element.222), channel_id=1, source_target_pairs={{0,24},{4,28},{8,16},{12,20},{16,8},{20,12},{24,0},{28,4},{1,25},{... | collective-permute-start | bytes 294920 | tf_op jit(solution)/shard_map/ppermute | solution.py:189
  66.9 6.4 %collective-permute-start.26 = (bf16[64,768]{1,0:T(8,128)(2,1)S(1)}, bf16[64,768]{1,0:T(8,128)(2,1)S(1)}, u32[]{:S(2)}, u32[]{:S(2)}) collective-permute-start(bf16[64,768]{1,0:T(8,128)(2,1)S(1)} %get-tuple-element.223), channel_id=1, source_target_pairs={{0,16},{4,20},{8,24},{12,28},{16,0},{20,4},{24,8},{28,12},{1,17},{... | collective-permute-start | bytes 294920 | tf_op jit(solution)/shard_map/ppermute | solution.py:189
  68.0 5.3 %collective-permute-start.27 = (bf16[64,768]{1,0:T(8,128)(2,1)S(1)}, bf16[64,768]{1,0:T(8,128)(2,1)S(1)}, u32[]{:S(2)}, u32[]{:S(2)}) collective-permute-start(bf16[64,768]{1,0:T(8,128)(2,1)S(1)} %get-tuple-element.224), channel_id=1, source_target_pairs={{0,8},{4,12},{8,0},{12,4},{16,24},{20,28},{24,16},{28,20},{1,9},{5... | collective-permute-start | bytes 294920 | tf_op jit(solution)/shard_map/ppermute | solution.py:189
  73.7 6.2 %collective-permute-start.29 = (bf16[32,768]{1,0:T(8,128)(2,1)S(1)}, bf16[32,768]{1,0:T(8,128)(2,1)S(1)}, u32[]{:S(2)}, u32[]{:S(2)}) collective-permute-start(bf16[32,768]{1,0:T(8,128)(2,1)S(1)} %get-tuple-element.230), channel_id=1, source_target_pairs={{0,3},{1,2},{2,1},{3,0},{4,7},{5,6},{6,5},{7,4},{8,11},{9,10},{10,... | collective-permute-start | bytes 147464 | tf_op jit(solution)/shard_map/ppermute | solution.py:189
  75.8 5.5 %collective-permute-start.30 = (bf16[32,768]{1,0:T(8,128)(2,1)S(1)}, bf16[32,768]{1,0:T(8,128)(2,1)S(1)}, u32[]{:S(2)}, u32[]{:S(2)}) collective-permute-start(bf16[32,768]{1,0:T(8,128)(2,1)S(1)} %get-tuple-element.231), channel_id=1, source_target_pairs={{0,2},{1,3},{2,0},{3,1},{4,6},{5,7},{6,4},{7,5},{8,10},{9,11},{10,... | collective-permute-start | bytes 147464 | tf_op jit(solution)/shard_map/ppermute | solution.py:189
  76.1 5.3 %collective-permute-start.31 = (bf16[32,768]{1,0:T(8,128)(2,1)S(1)}, bf16[32,768]{1,0:T(8,128)(2,1)S(1)}, u32[]{:S(2)}, u32[]{:S(2)}) collective-permute-start(bf16[32,768]{1,0:T(8,128)(2,1)S(1)} %get-tuple-element.232), channel_id=1, source_target_pairs={{0,1},{1,0},{2,3},{3,2},{4,5},{5,4},{6,7},{7,6},{8,9},{9,8},{10,11... | collective-permute-start | bytes 147464 | tf_op jit(solution)/shard_map/ppermute | solution.py:189
  (11 other events, 71.5 us)

commit v7 on v6

--- a/solution.py
+++ b/solution.py
@@ -181,7 +181,7 @@
 HBM_SPEC = pl.BlockSpec(memory_space=pl.ANY)
 SMALL_MIB = 8
 STAGE_AT = ((0,), (1, 2, 4), (6,), (3,), (7,), (5,))
-EXPERTS_MIB = 12
+EXPERTS_MIB = 9
 
 
 def swap(array, axis_name, mask):
@@ -340,6 +340,9 @@
     half = len(part_refs)
     heads, head_dim = part_refs[0].shape[0] - 1, part_refs[0].shape[2]
     tok = part_refs[0].shape[1] // half
+    width = heads * head_dim
+    lane = lax.broadcasted_iota(jnp.int32, (tok, head_dim), 1)
+    collected = [[] for _ in range(half)]
     for block in range(half):
         spans = [slice((k ^ block) * tok, ((k ^ block) + 1) * tok) for k in range(half)]
         stats = [ref[heads, span, :].astype(F32) for ref, span in zip(part_refs, spans)]
@@ -350,11 +353,23 @@
             for stat in stats
         ]
         total = sum(lift * denom for lift, denom in zip(lifts, denoms))
-        shares = [lift / total for lift in lifts]
+        total = jnp.where(lane < heads, total, 1.0)
+        for k, lift in enumerate(lifts):
+            collected[k].append(jnp.where(lane < heads, lift / total, 0.0))
+    shares = jnp.concatenate([share for column in collected for share in column], axis=0)
+    high = shares.astype(BF16)
+    low = (shares - high.astype(F32)).astype(BF16)
+    row = lax.broadcasted_iota(jnp.int32, (head_dim, width), 0)
+    column = lax.broadcasted_iota(jnp.int32, (head_dim, width), 1)
+    spread_out = (lax.div(column, head_dim) == row).astype(F32).astype(BF16)
+    wide = jnp.dot(high, spread_out, preferred_element_type=F32) + jnp.dot(low, spread_out, preferred_element_type=F32)
+    rows = half * tok
+    for block in range(half):
         for head in range(heads):
             mixed = sum(
-                share[:, head : head + 1] * ref[head, span, :].astype(F32)
-                for share, ref, span in zip(shares, part_refs, spans)
+                wide[k * rows + block * tok : k * rows + (block + 1) * tok, head * head_dim : (head + 1) * head_dim]
+                * ref[head, (k ^ block) * tok : ((k ^ block) + 1) * tok, :].astype(F32)
+                for k, ref in enumerate(part_refs)
             )
             attn_ref[block * tok : (block + 1) * tok, head * head_dim : (head + 1) * head_dim] = mixed.astype(BF16)
 
@@ -457,9 +472,15 @@
     count, begun = len(numbers), 0 not in numbers
     row_refs, gain_ref, weight_refs, refs = refs[:count], refs[count], refs[count + 1 : 3 * count + 1], refs[3 * count + 1 :]
     sums_in, refs = (refs[:3], refs[3:]) if begun else (None, refs)
+    columns_in, columns_out, columns_sem = (None,) * 3
+    if not begun:
+        columns_in, columns_out, columns_sem, refs = refs[2], refs[-4], refs[-1], (*refs[:2], *refs[3:-4], *refs[-3:-1])
     gate_hbm, up_hbm, gate_acc, up_acc, squares_ref = refs[:5]
     scaled_ref = refs[-1]
     copies = stage_copies(steps, gate_hbm, up_hbm, refs[5:-2], refs[-2]) if steps else []
+    if columns_in is not None:
+        columns = block_rows(3, columns_out.shape[1])
+        copies.append(pltpu.make_async_copy(columns_in.at[0, :, columns], columns_out, columns_sem))
     for copy in copies:
         copy.start()
     squares = sums_in[2][:, 0:1] if begun else 0.0
@@ -486,17 +507,18 @@
 def experts_kernel(numbers, *refs):
     count = len(numbers)
     row_refs, gain_ref, weight_refs, refs = refs[:count], refs[count], refs[count + 1 : 3 * count + 1], refs[3 * count + 1 :]
-    gate_in, up_in, squares_ref, down_hbm, odd_ref, act_ref = refs[:6]
-    even_refs, (gate_acc, up_acc, scaled_ref, squares_acc, odd_buf, sem) = refs[6:-6], refs[-6:]
+    gate_in, up_in, squares_ref, first_odd, down_hbm, odd_ref, act_ref = refs[:7]
+    even_refs, (gate_acc, up_acc, scaled_ref, squares_acc, odd_buf, sem) = refs[7:-6], refs[-6:]
     chips = len(even_refs)
     deep = odd_ref.shape[2]
-    targets = [(2 * k + 3, odd_buf.at[k]) for k in range(chips)] + [(2 * k + 2, ref) for k, ref in enumerate(even_refs)]
+    targets = [(2 * k + 3, odd_buf.at[k - 1]) for k in range(1, chips)] + [(2 * k + 2, ref) for k, ref in enumerate(even_refs)]
     copies = [
         pltpu.make_async_copy(down_hbm.at[0, :, block_rows(number, deep)], target, sem.at[at])
         for at, (number, target) in enumerate(targets)
     ]
     for copy in copies[:chips]:
         copy.start()
+    odd_weights = [first_odd] + [odd_buf.at[k] for k in range(chips - 1)]
     squares = squares_ref[:, 0:1]
     for order, number in enumerate(numbers):
         more, scaled_ref[order] = scaled_rows(row_refs[order], gain_ref, number)
@@ -517,13 +539,14 @@
     gate = rms * gate_acc[...]
     act_ref[...] = (gate / (1.0 + jnp.exp(-gate)) * (rms * up_acc[...])).astype(BF16)
     for k in range(chips):
-        copies[k].wait()
+        if k:
+            copies[k - 1].wait()
 
         @own_block
         def _():
-            odd_ref[k] = jnp.dot(act_ref[...], odd_buf[k], preferred_element_type=F32).astype(BF16)
-
-    for copy in copies[chips:]:
+            odd_ref[k] = jnp.dot(act_ref[...], odd_weights[k][...], preferred_element_type=F32).astype(BF16)
+
+    for copy in copies[chips - 1 :]:
         copy.wait()
 
 
@@ -562,18 +585,20 @@
     even_ref[...] = total.astype(BF16)
 
 
-def run_early(numbers, rows, gain, staged, sums, steps, gate_proj, up_proj):
+def run_early(numbers, rows, gain, staged, sums, steps, gate_proj, up_proj, *down):
     tokens, deep = rows[0].shape
     units = gate_proj.shape[2]
     acc = pltpu.VMEM((tokens, units), F32)
     outs = (acc, acc, pltpu.VMEM((tokens, 128), F32)) + (staged_like(steps, deep, units) if steps else ())
+    outs += tuple(pltpu.VMEM((units, deep), BF16) for _ in down)
     return pl.pallas_call(
         functools.partial(early_kernel, numbers, steps),
         out_shape=outs,
-        in_specs=[VMEM_SPEC] * (len(rows) + 1 + len(staged) + len(sums)) + [HBM_SPEC] * 2,
+        in_specs=[VMEM_SPEC] * (len(rows) + 1 + len(staged) + len(sums)) + [HBM_SPEC] * (2 + len(down)),
         out_specs=(VMEM_SPEC,) * len(outs),
         scratch_shapes=([pltpu.SemaphoreType.DMA((2 * len(steps),))] if steps else [])
-        + [pltpu.VMEM((len(rows), tokens, deep), BF16)],
+        + [pltpu.VMEM((len(rows), tokens, deep), BF16)]
+        + [pltpu.SemaphoreType.DMA(()) for _ in down],
         compiler_params=pltpu.CompilerParams(vmem_limit_bytes=5 << 20),
         cost_estimate=pl.CostEstimate(
             flops=4 * tokens * deep * units * len(rows),
@@ -581,10 +606,10 @@
             transcendentals=0,
         ),
         name="early",
-    )(*rows, gain, *[in_vmem(array) for array in staged], *sums, gate_proj, up_proj)
-
-
-def run_experts(numbers, rows, gain, staged, sums, down_proj):
+    )(*rows, gain, *[in_vmem(array) for array in staged], *sums, gate_proj, up_proj, *down)
+
+
+def run_experts(numbers, rows, gain, staged, sums, first_odd, down_proj):
     tokens, deep = rows[0].shape
     units = down_proj.shape[1]
     count = len(rows)
@@ -592,15 +617,15 @@
         functools.partial(experts_kernel, numbers),
         out_shape=(like((count, tokens, deep)), pltpu.VMEM((tokens, units), BF16))
         + (pltpu.VMEM((units, deep), BF16),) * count,
-        in_specs=[VMEM_SPEC] * (3 * count + 1 + 3) + [HBM_SPEC],
+        in_specs=[VMEM_SPEC] * (3 * count + 1 + 4) + [HBM_SPEC],
         out_specs=(VMEM_SPEC,) * (count + 2),
         scratch_shapes=[
             pltpu.VMEM((tokens, units), F32),
             pltpu.VMEM((tokens, units), F32),
             pltpu.VMEM((count, tokens, deep), BF16),
             pltpu.VMEM((tokens, 128), F32),
-            pltpu.VMEM((count, units, deep), BF16),
-            pltpu.SemaphoreType.DMA((2 * count,)),
+            pltpu.VMEM((count - 1, units, deep), BF16),
+            pltpu.SemaphoreType.DMA((2 * count - 1,)),
         ],
         compiler_params=pltpu.CompilerParams(vmem_limit_bytes=EXPERTS_MIB << 20),
         cost_estimate=pl.CostEstimate(
@@ -609,7 +634,7 @@
             transcendentals=tokens * units,
         ),
         name="experts",
-    )(*rows, gain, *[in_vmem(array) for array in staged], *sums, down_proj)
+    )(*rows, gain, *[in_vmem(array) for array in staged], *sums, in_vmem(first_odd), down_proj)
 
 
 def pair_total_kernel(even_ref, other_ref, *out_refs):
@@ -735,10 +760,10 @@
     even = [even[0]] + spread(even[1:], "ctx", 2)
     numbered = [number for steps in STAGE_AT for number in steps]
     odd = swap(even[0], "ctx", 1)
-    sums = run_early((0, 1), [even[0], odd], gain, staged[:4], (), STAGE_AT[4], gate_hbm, up_hbm)
+    sums = run_early((0, 1), [even[0], odd], gain, staged[:4], (), STAGE_AT[4], gate_hbm, up_hbm, down_hbm)
     sums, even = lax.optimization_barrier((sums, even[:0:-1]))
     even = even[::-1]
-    staged, sums = [*staged, *sums[3:]], sums[:3]
+    staged, sums, first_odd = [*staged, *sums[3:-1]], sums[:3], sums[-1]
     odd = [swap(piece, "ctx", 1) for piece in even]
     held = {number: staged[2 * at : 2 * at + 2] for at, number in enumerate(numbered[: len(staged) // 2])}
     numbers = tuple(range(2, ctx_count, 2))
@@ -748,7 +773,7 @@
     odd_numbers = tuple(range(3, ctx_count, 2))
     held[5] = (gate_last, up_last)
     out_odd, act, *even_weights = run_experts(
-        odd_numbers, odd, gain, [array for number in odd_numbers for array in held[number]], sums, down_hbm
+        odd_numbers, odd, gain, [array for number in odd_numbers for array in held[number]], sums, first_odd, down_hbm
     )
     out_even, odd_weight = device_call(
         even_columns_kernel,

time: 82.1 us -> 81.4 us (level)
  waiting for transfers between devices: 11 us -> 10.1 us
    pallas_call x2, Pallas kernels: 6.08 us -> 7.04 us  [run_early(): pl.pallas_call(functools.partial(early_kernel, numbers, steps), out_shape...]
    ppermute x32, waiting for transfers between devices: 11 us -> 10.1 us  [swap(): return lax.ppermute(array, axis_name, [(i, i ^ mask) for i in range(count)])]
  transfers between devices with their start and end apart: 32 -> 32, of which waited for: 11 -> 10; matrix products, arithmetic and copies ran while one was open for 0% -> 0% of each run, Pallas kernels for 33% -> 34%
where the time goes in v7:
time: 81.4 us; the launch traced here: 81.2 us
  Pallas kernels  38.9 us (48%)
  starting transfers between devices  31.9 us (39%)
  waiting for transfers between devices  10.1 us (12%)
    ppermute x32, starting transfers between devices, swap(): return lax.ppermute(array, axis_name, [(i, i ^ mask) for i in range(count)])  31.9 us
    pallas_call x4, Pallas kernels, stage(): pl.pallas_call(functools.partial(stage_kernel, steps), out_shape=staged_l...  16.1 us
    ppermute x32, waiting for transfers between devices, swap(): return lax.ppermute(array, axis_name, [(i, i ^ mask) for i in range(count)])  10.1 us
    pallas_call x11, Pallas kernels, device_call(): pl.pallas_call(kernel, out_shape=outs, in_specs=specs or [VMEM_SPEC] * le...  9.24 us
    pallas_call x2, Pallas kernels, run_early(): pl.pallas_call(functools.partial(early_kernel, numbers, steps), out_shape...  7.04 us
    pallas_call x1, Pallas kernels, run_experts(): pl.pallas_call(functools.partial(experts_kernel, numbers), out_shape=(lik...  6.54 us
  transfers between devices with their start and end apart: 32, of which 10 were waited for; matrix products, arithmetic and copies ran while one was open for 0% of the time, Pallas kernels for 34%

profile of v7, /device:TPU:0, one launch (start us, length us, event | category | flops | bytes accessed | tf_op | source)
XLA Modules:
  0.0 81.2 jit_solution(12503193830396053084)
XLA Ops:
  1.1 2.9 %collective-permute-start = (bf16[16,1536]{1,0:T(8,128)(2,1)}, bf16[16,1536]{1,0:T(8,128)(2,1)S(1)}, u32[]{:S(2)}, u32[]{:S(2)}) collective-permute-start(bf16[16,1536]{1,0:T(8,128)(2,1)} %refs_6_.1), channel_id=1, source_target_pairs={{0,8},{4,12},{8,0},{12,4},{16,24},{20,28},{24,16},{28,20},{1,9},{5... | collective-permute-start | bytes 147464 | tf_op jit(solution)/shard_map/ppermute | solution.py:189
  4.0 2.1 %collective-permute-start.2 = (bf16[16,1536]{1,0:T(8,128)(2,1)}, bf16[16,1536]{1,0:T(8,128)(2,1)S(1)}, u32[]{:S(2)}, u32[]{:S(2)}) collective-permute-start(bf16[16,1536]{1,0:T(8,128)(2,1)} %refs_6_.1), channel_id=1, source_target_pairs={{0,24},{4,28},{8,16},{12,20},{16,8},{20,12},{24,0},{28,4},{1,25},{... | collective-permute-start | bytes 147464 | tf_op jit(solution)/shard_map/ppermute | solution.py:189
  6.6 3.1 %stage.4 = (bf16[768,2048]{1,0:T(8,128)(2,1)S(1)}, bf16[768,2048]{1,0:T(8,128)(2,1)S(1)}, bf16[2,512,128]{2,1,0:T(8,128)(2,1)S(1)}, bf16[2,512,128]{2,1,0:T(8,12...) custom-call(bf16[1,6144,2048]{2,1,0:T(8,128)(2,1)} %refs_13_.1, ...), custom_call_target="tpu_custom_call" | custom-call | bytes 6291456 | tf_op jit(solution)/shard_map/stage/pallas_call | solution.py:450
  10.4 2.1 %attention.1.refs_0_ = bf16[13,64,128]{2,1,0:T(8,128)(2,1)S(1)} custom-call(bf16[16,1536]{1,0:T(8,128)(2,1)S(1)} %get-tuple-element.128.refs_0_, bf16[16,1536]{1,0:T(8,128)(2,1)S(1)} %collective-permute-done.refs_1_, bf16[16,1536]{1,0:T(8,128)(2,1)S(1)} %collective-permute-done.1.refs_2_, bf16[16,1536]{1,0:T(8,128)(2,1)S(1)} %collective-permute-done.2.refs_3_, ...), custom_call_target="tpu_custom_call" | custom-call | flops 415236096 | bytes 1277952 | tf_op jit(solution)/shard_map/attention/pallas_call | solution.py:200
  12.5 1.5 %collective-permute-start.9 = (bf16[13,64,128]{2,1,0:T(8,128)(2,1)S(1)}, bf16[13,64,128]{2,1,0:T(8,128)(2,1)S(1)}, u32[]{:S(2)}, u32[]{:S(2)}) collective-permute-start(bf16[13,64,128]{2,1,0:T(8,128)(2,1)S(1)} %attention.1.refs_0_), channel_id=1, source_target_pairs={{0,24},{4,28},{8,16},{12,20},{16,8},{20,12},{24,0},{28,4},{1,25},{... | collective-permute-start | bytes 638984 | tf_op jit(solution)/shard_map/ppermute | solution.py:189
  16.4 7.2 %stage.5 = (bf16[768,2048]{1,0:T(8,128)(2,1)S(1)}, bf16[768,2048]{1,0:T(8,128)(2,1)S(1)}, bf16[768,2048]{1,0:T(8,128)(2,1)S(1)}, bf16[768,2048]{1,0:T(8,128)(2,1...) custom-call(bf16[1,6144,2048]{2,1,0:T(8,128)(2,1)} %refs_13_.1, ...), custom_call_target="tpu_custom_call" | custom-call | bytes 18874368 | tf_op jit(solution)/shard_map/stage/pallas_call | solution.py:450
  25.1 1.4 %collective-permute-done.10.pair_ref = bf16[64,1536]{1,0:T(8,128)(2,1)S(1)} collective-permute-done((bf16[64,1536]{1,0:T(8,128)(2,1)S(1)}, bf16[64,1536]{1,0:T(8,128)(2,1)S(1)}, u32[]{:S(2)}, u32[]{:S(2)}) %collective-permute-start.10) | collective-permute-done | bytes 196640 | tf_op jit(solution)/shard_map/ppermute | solution.py:189
  27.0 3.7 %collective-permute-start.11 = (bf16[32,768]{1,0:T(8,128)(2,1)S(1)}, bf16[32,768]{1,0:T(8,128)(2,1)S(1)}, u32[]{:S(2)}, u32[]{:S(2)}) collective-permute-start(bf16[32,768]{1,0:T(8,128)(2,1)S(1)} %get-tuple-element.168), channel_id=1, source_target_pairs={{0,3},{1,2},{2,1},{3,0},{4,7},{5,6},{6,5},{7,4},{8,11},{9,10},{10,... | collective-permute-start | bytes 147464 | tf_op jit(solution)/shard_map/ppermute | solution.py:189
  31.5 2.9 %stage.6 = (bf16[768,2048]{1,0:T(8,128)(2,1)S(1)}, bf16[768,2048]{1,0:T(8,128)(2,1)S(1)}) custom-call(bf16[1,6144,2048]{2,1,0:T(8,128)(2,1)} %refs_13_.1, bf16[1,6144,2048]{2,1,0:T(8,128)(2,1)} %refs_14_.2), custom_call_target="tpu_custom_call" | custom-call | bytes 6291456 | tf_op jit(solution)/shard_map/stage/pallas_call | solution.py:450
  35.7 2.4 %collective-permute-start.16 = (bf16[32,768]{1,0:T(8,128)(2,1)S(1)}, bf16[32,768]{1,0:T(8,128)(2,1)S(1)}, u32[]{:S(2)}, u32[]{:S(2)}) collective-permute-start(bf16[32,768]{1,0:T(8,128)(2,1)S(1)} %hidden.1.refs_0_.refs_1_), channel_id=1, source_target_pairs={{0,3},{1,2},{2,1},{3,0},{4,7},{5,6},{6,5},{7,4},{8,11},{9,10},{10,... | collective-permute-start | bytes 147464 | tf_op jit(solution)/shard_map/ppermute | solution.py:189
  38.1 2.0 %collective-permute-start.14 = (bf16[32,768]{1,0:T(8,128)(2,1)S(1)}, bf16[32,768]{1,0:T(8,128)(2,1)S(1)}, u32[]{:S(2)}, u32[]{:S(2)}) collective-permute-start(bf16[32,768]{1,0:T(8,128)(2,1)S(1)} %hidden.1.refs_0_.refs_1_), channel_id=1, source_target_pairs={{0,1},{1,0},{2,3},{3,2},{4,5},{5,4},{6,7},{7,6},{8,9},{9,8},{10,11... | collective-permute-start | bytes 147464 | tf_op jit(solution)/shard_map/ppermute | solution.py:189
  40.1 2.9 %stage.7 = (bf16[768,2048]{1,0:T(8,128)(2,1)S(1)}, bf16[768,2048]{1,0:T(8,128)(2,1)S(1)}) custom-call(bf16[1,6144,2048]{2,1,0:T(8,128)(2,1)} %refs_13_.1, bf16[1,6144,2048]{2,1,0:T(8,128)(2,1)} %refs_14_.2), custom_call_target="tpu_custom_call" | custom-call | bytes 6291456 | tf_op jit(solution)/shard_map/stage/pallas_call | solution.py:450
  43.7 1.4 %collective-permute-start.18 = (bf16[64,768]{1,0:T(8,128)(2,1)S(1)}, bf16[64,768]{1,0:T(8,128)(2,1)S(1)}, u32[]{:S(2)}, u32[]{:S(2)}) collective-permute-start(bf16[64,768]{1,0:T(8,128)(2,1)S(1)} %get-tuple-element.192), channel_id=1, source_target_pairs={{0,24},{4,28},{8,16},{12,20},{16,8},{20,12},{24,0},{28,4},{1,25},{... | collective-permute-start | bytes 294920 | tf_op jit(solution)/shard_map/ppermute | solution.py:189
  47.2 3.8 %early.2 = (f32[64,2048]{1,0:T(8,128)S(1)}, f32[64,2048]{1,0:T(8,128)S(1)}, f32[64,128]{1,0:T(8,128)S(1)}, bf16[768,2048]{1,0:T(8,128)(2,1)S(1)}, bf16[768,2048]...) custom-call(bf16[64,768]{1,0:T(8,128)(2,1)S(1)} %get-tuple-element.180.refs_0_, ...), custom_call_target="tpu_custom_call" | custom-call | flops 805306368 | bytes 6291456 | tf_op jit(solution)/shard_map/early/pallas_call | solution.py:594
  52.4 3.2 %early.3 = (f32[64,2048]{1,0:T(8,128)S(1)}, f32[64,2048]{1,0:T(8,128)S(1)}, f32[64,128]{1,0:T(8,128)S(1)}, bf16[768,2048]{1,0:T(8,128)(2,1)S(1)}, bf16[768,2048]{1,0:T(8,128)(2,1)S(1)}) custom-call(bf16[64,768]{1,0:T(8,128)(2,1)S(1)} %collective-permute-done.20.refs_0_, bf16[64,768]{1,0:T(8,128)(2,1)S(1)} %collective-permute-done.19.refs_1_, ...), custom_call_target="tpu_custom_call" | custom-call | flops 1207959552 | bytes 6291456 | tf_op jit(solution)/shard_map/early/pallas_call | solution.py:594
  55.7 6.5 %experts.1 = (bf16[3,64,768]{2,1,0:T(8,128)(2,1)S(1)}, bf16[64,2048]{1,0:T(8,128)(2,1)S(1)}, bf16[2048,768]{1,0:T(8,128)(2,1)S(1)}, bf16[2048,768]{1,0:T(8,128)(2,1)S(1)}, bf16[2048,768]{1,0:T(8,128)(2,1)S(1)}) custom-call(bf16[64,768]{1,0:T(8,128)(2,1)S(1)} %collective-permute-done.21.refs_0_, bf16[64,768]{1,0:T(8,128)(2,1)S(1)} %collective-permute-done.22.refs_1_, ...), custom_call_target="tpu_custom_call" | custom-call | flops 1811939328 | bytes 18874368 | tf_op jit(solution)/shard_map/experts/pallas_call | solution.py:616
  62.8 1.9 %even_columns.1 = (bf16[3,64,768]{2,1,0:T(8,128)(2,1)S(1)}, bf16[2048,768]{1,0:T(8,128)(2,1)S(1)}) custom-call(bf16[64,2048]{1,0:T(8,128)(2,1)S(1)} %get-tuple-element.229.act_ref, bf16[2048,768]{1,0:T(8,128)(2,1)S(1)} %get-tuple-element.218.refs_0_, bf16[2048,768]{1,0:T(8,128)(2,1)S(1)} %get-tuple-element.219.refs_1_, ...), custom_call_target="tpu_custom_call" | custom-call | bytes 3145728 | tf_op jit(solution)/shard_map/even_columns/pallas_call | solution.py:200
  64.8 1.4 %collective-permute-start.25 = (bf16[64,768]{1,0:T(8,128)(2,1)S(1)}, bf16[64,768]{1,0:T(8,128)(2,1)S(1)}, u32[]{:S(2)}, u32[]{:S(2)}) collective-permute-start(bf16[64,768]{1,0:T(8,128)(2,1)S(1)} %get-tuple-element.226), channel_id=1, source_target_pairs={{0,24},{4,28},{8,16},{12,20},{16,8},{20,12},{24,0},{28,4},{1,25},{... | collective-permute-start | bytes 294920 | tf_op jit(solution)/shard_map/ppermute | solution.py:189
  68.3 2.6 %own_columns.1 = (bf16[64,768]{1,0:T(8,128)(2,1)S(1)}, bf16[64,768]{1,0:T(8,128)(2,1)S(1)}) custom-call(bf16[64,2048]{1,0:T(8,128)(2,1)S(1)} %get-tuple-element.229.act_ref, bf16[2048,768]{1,0:T(8,128)(2,1)S(1)} %get-tuple-element.230.odd_weight_ref, bf16[1,2048,6144]{2,1,0:T(8,128)(2,1)} %down_hbm.1), custom_call_target="tpu_custom_call" | custom-call | bytes 1 | tf_op jit(solution)/shard_map/own_columns/pallas_call | solution.py:200
  71.2 1.3 %collective-permute-done.26.refs_1_ = bf16[64,768]{1,0:T(8,128)(2,1)S(1)} collective-permute-done((bf16[64,768]{1,0:T(8,128)(2,1)S(1)}, bf16[64,768]{1,0:T(8,128)(2,1)S(1)}, u32[]{:S(2)}, u32[]{:S(2)}) %collective-permute-start.26) | collective-permute-done | bytes 98336 | tf_op jit(solution)/shard_map/ppermute | solution.py:189
  72.9 2.2 %collective-permute-start.29 = (bf16[32,768]{1,0:T(8,128)(2,1)S(1)}, bf16[32,768]{1,0:T(8,128)(2,1)S(1)}, u32[]{:S(2)}, u32[]{:S(2)}) collective-permute-start(bf16[32,768]{1,0:T(8,128)(2,1)S(1)} %get-tuple-element.234), channel_id=1, source_target_pairs={{0,3},{1,2},{2,1},{3,0},{4,7},{5,6},{6,5},{7,4},{8,11},{9,10},{10,... | collective-permute-start | bytes 147464 | tf_op jit(solution)/shard_map/ppermute | solution.py:189
  75.3 2.0 %collective-permute-start.31 = (bf16[32,768]{1,0:T(8,128)(2,1)S(1)}, bf16[32,768]{1,0:T(8,128)(2,1)S(1)}, u32[]{:S(2)}, u32[]{:S(2)}) collective-permute-start(bf16[32,768]{1,0:T(8,128)(2,1)S(1)} %get-tuple-element.236), channel_id=1, source_target_pairs={{0,1},{1,0},{2,3},{3,2},{4,5},{5,4},{6,7},{7,6},{8,9},{9,8},{10,11... | collective-permute-start | bytes 147464 | tf_op jit(solution)/shard_map/ppermute | solution.py:189
  77.4 1.7 %collective-permute-done.29.refs_2_ = bf16[32,768]{1,0:T(8,128)(2,1)S(1)} collective-permute-done((bf16[32,768]{1,0:T(8,128)(2,1)S(1)}, bf16[32,768]{1,0:T(8,128)(2,1)S(1)}, u32[]{:S(2)}, u32[]{:S(2)}) %collective-permute-start.29) | collective-permute-done | bytes 49184 | tf_op jit(solution)/shard_map/ppermute | solution.py:189
  79.1 1.5 %collective-permute-done.30.refs_3_ = bf16[32,768]{1,0:T(8,128)(2,1)S(1)} collective-permute-done((bf16[32,768]{1,0:T(8,128)(2,1)S(1)}, bf16[32,768]{1,0:T(8,128)(2,1)S(1)}, u32[]{:S(2)}, u32[]{:S(2)}) %collective-permute-start.30) | collective-permute-done | bytes 49184 | tf_op jit(solution)/shard_map/ppermute | solution.py:189
  (65 shorter events, 17.3 us)
Async XLA Ops:
  0.0 10.4 %collective-permute-start.3 = (bf16[2,512,128]{2,1,0:T(8,128)(2,1)}, bf16[2,512,128]{2,1,0:T(8,128)(2,1)S(1)}, u32[]{:S(2)}, u32[]{:S(2)}) collective-permute-start(bf16[2,512,128]{2,1,0:T(8,128)(2,1)} %refs_2_.2), channel_id=1, source_target_pairs={{0,4},{4,0},{8,12},{12,8},{16,20},{20,16},{24,28},{28,24},{1,5},{5... | collective-permute-start | bytes 786440 | tf_op jit(solution)/shard_map/ppermute | solution.py:189
  0.5 9.9 %collective-permute-start.4 = (bf16[2,512,128]{2,1,0:T(8,128)(2,1)}, bf16[2,512,128]{2,1,0:T(8,128)(2,1)S(1)}, u32[]{:S(2)}, u32[]{:S(2)}) collective-permute-start(bf16[2,512,128]{2,1,0:T(8,128)(2,1)} %refs_3_.3), channel_id=1, source_target_pairs={{0,4},{4,0},{8,12},{12,8},{16,20},{20,16},{24,28},{28,24},{1,5},{5... | collective-permute-start | bytes 786440 | tf_op jit(solution)/shard_map/ppermute | solution.py:189
  1.0 5.1 %collective-permute-start.6 = (bf16[2,16,128]{2,1,0:T(8,128)(2,1)}, bf16[2,16,128]{2,1,0:T(8,128)(2,1)S(1)}, u32[]{:S(2)}, u32[]{:S(2)}) collective-permute-start(bf16[2,16,128]{2,1,0:T(8,128)(2,1)} %refs_5_.1), channel_id=1, source_target_pairs={{0,4},{4,0},{8,12},{12,8},{16,20},{20,16},{24,28},{28,24},{1,5},{5... | collective-permute-start | bytes 24584 | tf_op jit(solution)/shard_map/ppermute | solution.py:189
  1.1 8.6 %collective-permute-start = (bf16[16,1536]{1,0:T(8,128)(2,1)}, bf16[16,1536]{1,0:T(8,128)(2,1)S(1)}, u32[]{:S(2)}, u32[]{:S(2)}) collective-permute-start(bf16[16,1536]{1,0:T(8,128)(2,1)} %refs_6_.1), channel_id=1, source_target_pairs={{0,8},{4,12},{8,0},{12,4},{16,24},{20,28},{24,16},{28,20},{1,9},{5... | collective-permute-start | bytes 147464 | tf_op jit(solution)/shard_map/ppermute | solution.py:189
  4.0 5.7 %collective-permute-start.2 = (bf16[16,1536]{1,0:T(8,128)(2,1)}, bf16[16,1536]{1,0:T(8,128)(2,1)S(1)}, u32[]{:S(2)}, u32[]{:S(2)}) collective-permute-start(bf16[16,1536]{1,0:T(8,128)(2,1)} %refs_6_.1), channel_id=1, source_target_pairs={{0,24},{4,28},{8,16},{12,20},{16,8},{20,12},{24,0},{28,4},{1,25},{... | collective-permute-start | bytes 147464 | tf_op jit(solution)/shard_map/ppermute | solution.py:189
  6.1 4.3 %collective-permute-start.1 = (bf16[16,1536]{1,0:T(8,128)(2,1)}, bf16[16,1536]{1,0:T(8,128)(2,1)S(1)}, u32[]{:S(2)}, u32[]{:S(2)}) collective-permute-start(bf16[16,1536]{1,0:T(8,128)(2,1)} %refs_6_.1), channel_id=1, source_target_pairs={{0,16},{4,20},{8,24},{12,28},{16,0},{20,4},{24,8},{28,12},{1,17},{... | collective-permute-start | bytes 147464 | tf_op jit(solution)/shard_map/ppermute | solution.py:189
  12.5 11.1 %collective-permute-start.9 = (bf16[13,64,128]{2,1,0:T(8,128)(2,1)S(1)}, bf16[13,64,128]{2,1,0:T(8,128)(2,1)S(1)}, u32[]{:S(2)}, u32[]{:S(2)}) collective-permute-start(bf16[13,64,128]{2,1,0:T(8,128)(2,1)S(1)} %attention.1.refs_0_), channel_id=1, source_target_pairs={{0,24},{4,28},{8,16},{12,20},{16,8},{20,12},{24,0},{28,4},{1,25},{... | collective-permute-start | bytes 638984 | tf_op jit(solution)/shard_map/ppermute | solution.py:189
  13.9 10.4 %collective-permute-start.8 = (bf16[13,64,128]{2,1,0:T(8,128)(2,1)S(1)}, bf16[13,64,128]{2,1,0:T(8,128)(2,1)S(1)}, u32[]{:S(2)}, u32[]{:S(2)}) collective-permute-start(bf16[13,64,128]{2,1,0:T(8,128)(2,1)S(1)} %attention.1.refs_0_), channel_id=1, source_target_pairs={{0,16},{4,20},{8,24},{12,28},{16,0},{20,4},{24,8},{28,12},{1,17},{... | collective-permute-start | bytes 638984 | tf_op jit(solution)/shard_map/ppermute | solution.py:189
  14.9 9.4 %collective-permute-start.7 = (bf16[13,64,128]{2,1,0:T(8,128)(2,1)S(1)}, bf16[13,64,128]{2,1,0:T(8,128)(2,1)S(1)}, u32[]{:S(2)}, u32[]{:S(2)}) collective-permute-start(bf16[13,64,128]{2,1,0:T(8,128)(2,1)S(1)} %attention.1.refs_0_), channel_id=1, source_target_pairs={{0,8},{4,12},{8,0},{12,4},{16,24},{20,28},{24,16},{28,20},{1,9},{5... | collective-permute-start | bytes 638984 | tf_op jit(solution)/shard_map/ppermute | solution.py:189
  27.0 7.3 %collective-permute-start.11 = (bf16[32,768]{1,0:T(8,128)(2,1)S(1)}, bf16[32,768]{1,0:T(8,128)(2,1)S(1)}, u32[]{:S(2)}, u32[]{:S(2)}) collective-permute-start(bf16[32,768]{1,0:T(8,128)(2,1)S(1)} %get-tuple-element.168), channel_id=1, source_target_pairs={{0,3},{1,2},{2,1},{3,0},{4,7},{5,6},{6,5},{7,4},{8,11},{9,10},{10,... | collective-permute-start | bytes 147464 | tf_op jit(solution)/shard_map/ppermute | solution.py:189
  30.7 5.0 %collective-permute-start.12 = (bf16[32,768]{1,0:T(8,128)(2,1)S(1)}, bf16[32,768]{1,0:T(8,128)(2,1)S(1)}, u32[]{:S(2)}, u32[]{:S(2)}) collective-permute-start(bf16[32,768]{1,0:T(8,128)(2,1)S(1)} %get-tuple-element.169), channel_id=1, source_target_pairs={{0,2},{1,3},{2,0},{3,1},{4,6},{5,7},{6,4},{7,5},{8,10},{9,11},{10,... | collective-permute-start | bytes 147464 | tf_op jit(solution)/shard_map/ppermute | solution.py:189
  30.7 5.0 %collective-permute-start.13 = (bf16[32,768]{1,0:T(8,128)(2,1)S(1)}, bf16[32,768]{1,0:T(8,128)(2,1)S(1)}, u32[]{:S(2)}, u32[]{:S(2)}) collective-permute-start(bf16[32,768]{1,0:T(8,128)(2,1)S(1)} %get-tuple-element.170), channel_id=1, source_target_pairs={{0,1},{1,0},{2,3},{3,2},{4,5},{5,4},{6,7},{7,6},{8,9},{9,8},{10,11... | collective-permute-start | bytes 147464 | tf_op jit(solution)/shard_map/ppermute | solution.py:189
  35.7 7.3 %collective-permute-start.16 = (bf16[32,768]{1,0:T(8,128)(2,1)S(1)}, bf16[32,768]{1,0:T(8,128)(2,1)S(1)}, u32[]{:S(2)}, u32[]{:S(2)}) collective-permute-start(bf16[32,768]{1,0:T(8,128)(2,1)S(1)} %hidden.1.refs_0_.refs_1_), channel_id=1, source_target_pairs={{0,3},{1,2},{2,1},{3,0},{4,7},{5,6},{6,5},{7,4},{8,11},{9,10},{10,... | collective-permute-start | bytes 147464 | tf_op jit(solution)/shard_map/ppermute | solution.py:189
  38.1 5.3 %collective-permute-start.15 = (bf16[32,768]{1,0:T(8,128)(2,1)S(1)}, bf16[32,768]{1,0:T(8,128)(2,1)S(1)}, u32[]{:S(2)}, u32[]{:S(2)}) collective-permute-start(bf16[32,768]{1,0:T(8,128)(2,1)S(1)} %hidden.1.refs_0_.refs_1_), channel_id=1, source_target_pairs={{0,2},{1,3},{2,0},{3,1},{4,6},{5,7},{6,4},{7,5},{8,10},{9,11},{10,... | collective-permute-start | bytes 147464 | tf_op jit(solution)/shard_map/ppermute | solution.py:189
  38.1 5.2 %collective-permute-start.14 = (bf16[32,768]{1,0:T(8,128)(2,1)S(1)}, bf16[32,768]{1,0:T(8,128)(2,1)S(1)}, u32[]{:S(2)}, u32[]{:S(2)}) collective-permute-start(bf16[32,768]{1,0:T(8,128)(2,1)S(1)} %hidden.1.refs_0_.refs_1_), channel_id=1, source_target_pairs={{0,1},{1,0},{2,3},{3,2},{4,5},{5,4},{6,7},{7,6},{8,9},{9,8},{10,11... | collective-permute-start | bytes 147464 | tf_op jit(solution)/shard_map/ppermute | solution.py:189
  43.7 7.4 %collective-permute-start.18 = (bf16[64,768]{1,0:T(8,128)(2,1)S(1)}, bf16[64,768]{1,0:T(8,128)(2,1)S(1)}, u32[]{:S(2)}, u32[]{:S(2)}) collective-permute-start(bf16[64,768]{1,0:T(8,128)(2,1)S(1)} %get-tuple-element.192), channel_id=1, source_target_pairs={{0,24},{4,28},{8,16},{12,20},{16,8},{20,12},{24,0},{28,4},{1,25},{... | collective-permute-start | bytes 294920 | tf_op jit(solution)/shard_map/ppermute | solution.py:189
  45.1 6.8 %collective-permute-start.19 = (bf16[64,768]{1,0:T(8,128)(2,1)S(1)}, bf16[64,768]{1,0:T(8,128)(2,1)S(1)}, u32[]{:S(2)}, u32[]{:S(2)}) collective-permute-start(bf16[64,768]{1,0:T(8,128)(2,1)S(1)} %get-tuple-element.193), channel_id=1, source_target_pairs={{0,16},{4,20},{8,24},{12,28},{16,0},{20,4},{24,8},{28,12},{1,17},{... | collective-permute-start | bytes 294920 | tf_op jit(solution)/shard_map/ppermute | solution.py:189
  46.2 5.7 %collective-permute-start.20 = (bf16[64,768]{1,0:T(8,128)(2,1)S(1)}, bf16[64,768]{1,0:T(8,128)(2,1)S(1)}, u32[]{:S(2)}, u32[]{:S(2)}) collective-permute-start(bf16[64,768]{1,0:T(8,128)(2,1)S(1)} %get-tuple-element.194), channel_id=1, source_target_pairs={{0,8},{4,12},{8,0},{12,4},{16,24},{20,28},{24,16},{28,20},{1,9},{5... | collective-permute-start | bytes 294920 | tf_op jit(solution)/shard_map/ppermute | solution.py:189
  64.8 6.5 %collective-permute-start.25 = (bf16[64,768]{1,0:T(8,128)(2,1)S(1)}, bf16[64,768]{1,0:T(8,128)(2,1)S(1)}, u32[]{:S(2)}, u32[]{:S(2)}) collective-permute-start(bf16[64,768]{1,0:T(8,128)(2,1)S(1)} %get-tuple-element.226), channel_id=1, source_target_pairs={{0,24},{4,28},{8,16},{12,20},{16,8},{20,12},{24,0},{28,4},{1,25},{... | collective-permute-start | bytes 294920 | tf_op jit(solution)/shard_map/ppermute | solution.py:189
  66.2 6.4 %collective-permute-start.26 = (bf16[64,768]{1,0:T(8,128)(2,1)S(1)}, bf16[64,768]{1,0:T(8,128)(2,1)S(1)}, u32[]{:S(2)}, u32[]{:S(2)}) collective-permute-start(bf16[64,768]{1,0:T(8,128)(2,1)S(1)} %get-tuple-element.227), channel_id=1, source_target_pairs={{0,16},{4,20},{8,24},{12,28},{16,0},{20,4},{24,8},{28,12},{1,17},{... | collective-permute-start | bytes 294920 | tf_op jit(solution)/shard_map/ppermute | solution.py:189
  67.3 5.3 %collective-permute-start.27 = (bf16[64,768]{1,0:T(8,128)(2,1)S(1)}, bf16[64,768]{1,0:T(8,128)(2,1)S(1)}, u32[]{:S(2)}, u32[]{:S(2)}) collective-permute-start(bf16[64,768]{1,0:T(8,128)(2,1)S(1)} %get-tuple-element.228), channel_id=1, source_target_pairs={{0,8},{4,12},{8,0},{12,4},{16,24},{20,28},{24,16},{28,20},{1,9},{5... | collective-permute-start | bytes 294920 | tf_op jit(solution)/shard_map/ppermute | solution.py:189
  72.9 6.2 %collective-permute-start.29 = (bf16[32,768]{1,0:T(8,128)(2,1)S(1)}, bf16[32,768]{1,0:T(8,128)(2,1)S(1)}, u32[]{:S(2)}, u32[]{:S(2)}) collective-permute-start(bf16[32,768]{1,0:T(8,128)(2,1)S(1)} %get-tuple-element.234), channel_id=1, source_target_pairs={{0,3},{1,2},{2,1},{3,0},{4,7},{5,6},{6,5},{7,4},{8,11},{9,10},{10,... | collective-permute-start | bytes 147464 | tf_op jit(solution)/shard_map/ppermute | solution.py:189
  75.1 5.5 %collective-permute-start.30 = (bf16[32,768]{1,0:T(8,128)(2,1)S(1)}, bf16[32,768]{1,0:T(8,128)(2,1)S(1)}, u32[]{:S(2)}, u32[]{:S(2)}) collective-permute-start(bf16[32,768]{1,0:T(8,128)(2,1)S(1)} %get-tuple-element.235), channel_id=1, source_target_pairs={{0,2},{1,3},{2,0},{3,1},{4,6},{5,7},{6,4},{7,5},{8,10},{9,11},{10,... | collective-permute-start | bytes 147464 | tf_op jit(solution)/shard_map/ppermute | solution.py:189
  75.3 5.2 %collective-permute-start.31 = (bf16[32,768]{1,0:T(8,128)(2,1)S(1)}, bf16[32,768]{1,0:T(8,128)(2,1)S(1)}, u32[]{:S(2)}, u32[]{:S(2)}) collective-permute-start(bf16[32,768]{1,0:T(8,128)(2,1)S(1)} %get-tuple-element.236), channel_id=1, source_target_pairs={{0,1},{1,0},{2,3},{3,2},{4,5},{5,4},{6,7},{7,6},{8,9},{9,8},{10,11... | collective-permute-start | bytes 147464 | tf_op jit(solution)/shard_map/ppermute | solution.py:189
  (11 other events, 71.7 us)
